TPU v7x, 32 devices: a whole 2x2x4 slice. The times are simulated.
32 devices in a mesh: gz: 8 (over z, y), gy: 4 (over x, core).
Axes of the slice: x: 2, y: 2, z: 4, core: 2. Of those that a mesh axis runs over, the one named last changes fastest.
Arguments:
- velocity: float32 [2, 6, 1024, 2048], P(None, None, 'gy', 'gz'), may hold values from -6 to 6
Outputs:
- spectrum: float32 [2, 6, 1024, 2048], P(None, None, 'gy', 'gz')
All inputs are finite; a program needn't handle non-finite values.
Results may differ from a plain program's by a relative error of at most 0.000098.
Values sent between devices are 32-bit elements; how exact they have to be, the bound alone decides.
No kernel may reach another device: no remote copies, remote signals or barrier semaphores. Data moves between devices by JAX's collectives and lax.ppermute only.
A program may use at most 64 MiB of HBM per device.

v0:
```python
import functools
import math

import jax
import jax.numpy as jnp
import numpy as np
from jax import lax
from jax.experimental import pallas as pl
from jax.experimental.pallas import tpu as pltpu
from jax.sharding import PartitionSpec as P


GRANT = 16 * 2**20

F32 = jnp.float32
BF16 = jnp.bfloat16
SMEM = pl.BlockSpec(memory_space=pltpu.SMEM)
VMEM = pl.BlockSpec(memory_space=pltpu.VMEM)
ANY = pl.BlockSpec(memory_space=pl.ANY)


def exchanged(block, axis, mask):
    count = lax.axis_size(axis)
    return lax.ppermute(block, axis, [(i, i ^ mask) for i in range(count)])


def reversed_bits(index, bit_count):
    return sum(((index >> place) & 1) << (bit_count - 1 - place) for place in range(bit_count))


def unit(products, length):
    phase = -2.0 * math.pi * (products % length).astype(F32) / length
    return jnp.cos(phase), jnp.sin(phase)


def estimate(flops, count):
    return pl.CostEstimate(flops=flops, transcendentals=0, bytes_accessed=4 * count)


def dft_matrix(frequency, count, local, at):
    length = count * local
    to = jnp.arange(local, dtype=jnp.int32)
    cosine, sine = unit(at[:, None] * (frequency + count * to[None, :]), length)
    scale = 1.0 / math.sqrt(length)
    return cosine * scale, sine * scale


def split(values):
    high = lax.reduce_precision(values, 8, 7)
    return jnp.stack([high.astype(BF16), (values - high).astype(BF16)])


def right_matrix(frequency, count, local):
    cosine, sine = dft_matrix(frequency, count, local, jnp.arange(local, dtype=jnp.int32))
    return split(jnp.block([[cosine, sine], [-sine, cosine]]))


def left_matrix(frequency, count, local, part):
    at = jnp.arange(local, dtype=jnp.int32)
    quarter = local // 4
    at = (part ^ (at // quarter)) * quarter + at % quarter
    cosine, sine = dft_matrix(frequency, count, local, at)
    return split(jnp.block([[cosine.T, -sine.T], [sine.T, cosine.T]]))


def halves(values):
    high = values.astype(BF16)
    return high, (values - high.astype(F32)).astype(BF16)


def dot3(left, right):
    def single(a, b):
        return jnp.dot(a, b, preferred_element_type=F32)

    return single(left[0], right[0]) + (single(left[1], right[0]) + single(left[0], right[1]))


def along_last(real, imag, matrix_ref):
    local = real.shape[-1]
    mixed = dot3(halves(jnp.concatenate([real, imag], axis=1)), (matrix_ref[0], matrix_ref[1]))
    return mixed[:, :local], mixed[:, local:]


def along_first(real, imag, matrix_ref):
    local = real.shape[0]
    mixed = dot3((matrix_ref[0], matrix_ref[1]), halves(jnp.concatenate([real, imag], axis=0)))
    return mixed[:local], mixed[local:]


def after(value, done):
    return value if done is None else lax.optimization_barrier((value, done))[0]


def per_rows(planes, rows, step, body):
    def one(at, carry):
        body(at // (rows // step), pl.multiple_of(at % (rows // step) * step, step))
        return carry

    lax.fori_loop(0, planes * (rows // step), one, 0, unroll=4)


def mix_kernel(coef_ref, *refs):
    pieces, outs = refs[:4], refs[4:]
    planes, half = outs[0].shape[2:4]
    for h, out_ref in enumerate(outs):

        def body(plane, at, h=h, out_ref=out_ref):
            rows = pl.ds(h * half + at, 8)
            values = [(ref[0, plane, rows, :], ref[1, plane, rows, :]) for ref in pieces]
            for e in range(4):
                real, imag = None, None
                for d in range(4):
                    c, s = coef_ref[4 * e + d], coef_ref[16 + 4 * e + d]
                    a, b = values[d]
                    re, im = a * c - b * s, a * s + b * c
                    real = re if real is None else real + re
                    imag = im if imag is None else imag + im
                out_ref[e, 0, plane, pl.ds(at, 8), :] = real
                out_ref[e, 1, plane, pl.ds(at, 8), :] = imag

        per_rows(planes, half, 8, body)


def mix(pieces, coefs):
    _, planes, quarter, columns = pieces[0].shape
    half = jax.ShapeDtypeStruct((4, 2, planes, quarter // 2, columns), F32)
    return pl.pallas_call(
        mix_kernel,
        in_specs=[SMEM] + [VMEM] * 4,
        out_specs=[VMEM] * 2,
        out_shape=[half] * 2,
        compiler_params=pltpu.CompilerParams(vmem_limit_bytes=GRANT),
        cost_estimate=estimate(128 * planes * quarter * columns, 16 * planes * quarter * columns),
        name="mix",
    )(coefs, *pieces)


def butterfly_kernel(kinds, apart, *refs):
    sides, outs = refs[2:6], refs[6:]
    groups, _, planes, half, _ = sides[0].shape
    for h, (source, at_coef, twist) in enumerate(kinds):
        coef_ref, own_ref, other_ref = refs[source], sides[2 * h], sides[2 * h + 1]
        flip, c, s = [coef_ref[at_coef + i] for i in range(3)]

        def body(plane, at):
            rows = pl.ds(at, 8)
            for e in range(groups):
                real, imag = [own_ref[e, p, plane, rows, :] * flip + other_ref[e, p, plane, rows, :] for p in range(2)]
                if twist:
                    real, imag = real * c - imag * s, real * s + imag * c
                if apart:
                    into = pl.ds(h * half + at, 8)
                    outs[e][0, plane, into, :] = real
                    outs[e][1, plane, into, :] = imag
                else:
                    outs[h][e, 0, plane, rows, :] = real
                    outs[h][e, 1, plane, rows, :] = imag

        per_rows(planes, half, 8, body)


def butterfly(own, other, kinds, coefs, apart):
    groups, _, planes, half, columns = own[0].shape
    if apart:
        shapes = [jax.ShapeDtypeStruct((2, planes, 2 * half, columns), F32)] * groups
    else:
        shapes = [jax.ShapeDtypeStruct(own[0].shape, F32)] * 2
    return list(
        pl.pallas_call(
            functools.partial(butterfly_kernel, kinds, apart),
            in_specs=[SMEM] * 2 + [VMEM] * 4,
            out_specs=[VMEM] * len(shapes),
            out_shape=shapes,
            compiler_params=pltpu.CompilerParams(vmem_limit_bytes=GRANT),
            cost_estimate=estimate(10 * own[0].size, 6 * own[0].size),
            name="butterfly",
        )(*coefs, own[0], other[0], own[1], other[1])
    )


def finish_kernel(start, right_ref, left_ref, e0_ref, e1_ref, e2_ref, e3_ref, *rest):
    out_ref, done, sems = rest[-3:]
    planes = e0_ref.shape[1]
    copies = []
    for plane in range(planes):
        refs = (e0_ref, e1_ref, e2_ref, e3_ref)
        whole = [jnp.concatenate([ref[part, plane] for ref in refs], axis=0) for part in range(2)]
        real, imag = along_last(whole[0], whole[1], right_ref)
        real, imag = along_first(real, imag, left_ref)
        done[plane, 0] = real
        done[plane, 1] = imag
        copies.append(pltpu.make_async_copy(done.at[plane], out_ref.at[:, start + plane], sems.at[plane]))
        copies[-1].start()
    for copy in copies:
        copy.wait()


def finish(pieces, right, left, out, start, total):
    _, planes, quarter, columns = pieces[0].shape
    rows = 4 * quarter
    in_specs = [VMEM] * 6
    args = [right, left, *pieces]
    aliases = {}
    if out is not None:
        in_specs.append(ANY)
        aliases = {len(args): 0}
        args.append(out)
    return pl.pallas_call(
        functools.partial(finish_kernel, start),
        in_specs=in_specs,
        out_specs=ANY,
        out_shape=jax.ShapeDtypeStruct((2, total, rows, columns), F32),
        scratch_shapes=[
            pltpu.VMEM((planes, 2, rows, columns), F32),
            pltpu.SemaphoreType.DMA((planes,)),
        ],
        input_output_aliases=aliases,
        compiler_params=pltpu.CompilerParams(vmem_limit_bytes=GRANT),
        cost_estimate=estimate(24 * planes * rows * columns * (rows + columns), 4 * planes * rows * columns),
        name="finish",
    )(*args)


def host_unit(products, length):
    value = np.exp(-2j * np.pi * (np.asarray(products) % length) / length)
    return value.real, value.imag


def pair_table(count, bit):
    index = np.arange(count)
    upper = (index >> bit) & 1
    return np.stack([1 - 2 * upper, *host_unit((index % 2**bit) * upper, 2 ** (bit + 1))], axis=1)


def mix_table(count):
    index, step = np.arange(count), np.arange(4)
    part, rest = index // (count // 4), index % (count // 4)
    k = reversed_bits(part[:, None] ^ step, 2)[:, :, None]
    d = (part[:, None] ^ step)[:, None, :]
    cosine, sine = host_unit(rest[:, None, None] * k + (count // 4) * (d * k), count)
    return np.concatenate([cosine.reshape(count, 16), sine.reshape(count, 16)], axis=1)


def row_of(table, index):
    table = jnp.asarray(table, F32)
    row = lax.dynamic_slice(table, (index, jnp.uint32(0)), (1, table.shape[1]))
    return row.reshape(table.shape[1])


def chunks_of(planes):
    size = max(1, -(-planes // 3))
    return [(at, min(size, planes - at)) for at in range(0, planes, size)]


def plan_of(chunks, steps):
    events, ready, arrived = [], [], 0.1
    for i, (_, size) in enumerate(chunks):
        events.append((arrived - 0.35, "go", i, 0))
        arrived += size + 0.1
        ready.append((arrived, i, 0))
    free, last = 0.0, {}
    while ready:
        ready.sort()
        now, i, step = ready.pop(0)
        events.append((now, "node", i, step))
        if step < steps - 2:
            free = max(now + 0.25, free) + chunks[i][1] / 2
            ready.append((free, i, step + 1))
        elif step < steps - 1:
            ready.append((now + 0.3, i, step + 1))
        else:
            last[i] = now + 0.1
    for i, (_, size) in enumerate(chunks):
        arrived = max(arrived, last[i])
        events.append((arrived - 0.35, "back", i, 0))
        arrived += size + 0.1
        events.append((arrived, "end", i, 0))
    return [event[1:] for event in sorted(events)]


def shards(velocity):
    _, planes, rows, columns = velocity.shape
    z_count = lax.axis_size("gz")
    y_count = lax.axis_size("gy")
    z_bits = z_count.bit_length() - 1
    y_bits = y_count.bit_length() - 1
    stride = z_count // 4
    quarter = rows // 4
    z_index = lax.axis_index("gz").astype(jnp.uint32)
    y_index = lax.axis_index("gy").astype(jnp.uint32)
    part = z_index >> (z_bits - 2)
    peers = [part ^ d for d in range(4)]
    shifts = [reversed_bits(z_index, z_bits), reversed_bits(y_index, y_bits)]
    velocity, z_index, y_index, part, peers, shifts = lax.optimization_barrier(
        (velocity, z_index, y_index, part, peers, shifts)
    )

    chunks = chunks_of(planes)
    quarters = velocity.reshape(2, planes, 4, quarter, columns)
    received = []
    zero = jnp.uint32(0)
    for start, size in chunks:
        shape = (2, size, 1, quarter, columns)
        at = jnp.uint32(start)
        pieces = [lax.dynamic_slice(quarters, (zero, at, peer, zero, zero), shape)[:, :, 0] for peer in peers]
        quarters = after(quarters, pieces)
        received.append(pieces[:1] + [exchanged(pieces[d], "gz", d * stride) for d in range(1, 4)])

    z_steps, y_steps = list(reversed(range(z_bits - 2))), list(reversed(range(y_bits)))
    z_table = np.concatenate([mix_table(z_count)] + [pair_table(z_count, bit) for bit in z_steps], axis=1)
    y_table = np.concatenate([pair_table(y_count, bit) for bit in y_steps], axis=1)
    coefs = [row_of(z_table, z_index), row_of(y_table, y_index)]
    right = right_matrix(shifts[0].astype(jnp.int32), z_count, columns)
    left = left_matrix(shifts[1].astype(jnp.int32), y_count, rows, part.astype(jnp.int32))
    z_pairs = [("gz", bit, (0, 32 + 3 * i, bit > 0)) for i, bit in enumerate(z_steps)]
    y_pairs = [("gy", bit, (1, 3 * i, bit > 0)) for i, bit in enumerate(y_steps)]
    ways = list(zip(z_pairs + y_pairs[:-1], y_pairs[:-1] + z_pairs))
    ways.append((y_pairs[-1], y_pairs[-1]))

    state = [None] * len(chunks)
    done = None
    steps = len(ways) + 1
    back = [None] * len(chunks)
    result = None
    for kind, i, step in plan_of(chunks, steps):
        if kind == "node" and step == 0:
            pieces = after(received[i], done)
            state[i] = mix(pieces, coefs[0])
        elif kind == "node":
            way = ways[step - 1]
            other = [exchanged(block, axis, 2**bit) for block, (axis, bit, _) in zip(state[i], way)]
            own, other = after((state[i], other), done)
            state[i] = butterfly(own, other, tuple(pair for _, _, pair in way), coefs, step == steps - 1)
            if step == steps - 1:
                back[i] = state[i][:1] + [exchanged(state[i][d], "gz", d * stride) for d in range(1, 4)]
        elif kind == "end":
            pieces = after(back[i], done)
            result = finish(pieces, right, left, result, chunks[i][0], planes)
        done = result if kind == "end" else state[i] if kind == "node" else done
    return result


def solution(mesh):
    in_specs = (P(None, None, "gy", "gz"),)
    out_specs = P(None, None, "gy", "gz")
    return jax.shard_map(shards, mesh=mesh, in_specs=in_specs, out_specs=out_specs, check_vma=False)
```

profile of v0, /device:TPU:19, one launch (start us, length us, event | category | flops | bytes accessed | tf_op | source)
XLA Modules:
  0.0 206.5 jit_solution(13275092533044303861)
XLA Ops:
  0.0 1.3 dynamic-slice_bitcast_fusion.8
  1.5 3.2 %collective-permute-start.7 = (f32[2,2,64,256]{3,2,1,0:T(8,128)S(1)}, f32[2,2,64,256]{3,2,1,0:T(8,128)S(1)}, u32[]{:S(2)}, u32[]{:S(2)}) collective-permute-start(f32[2,2,64,256]{3,2,1,0:T(8,128)S(1)} %get-tuple-element.210), channel_id=1, source_target_pairs={{0,16},{4,20},{8,24},{12,28},{16,0},{20,4},{24,8},{28,12},{1,17},{... | collective-permute-start | bytes 786440 | tf_op jit(solution)/shard_map/ppermute | solution.py:24
  5.4 14.4 %collective-permute-done.8.refs_3_ = f32[2,2,64,256]{3,2,1,0:T(8,128)S(1)} collective-permute-done((f32[2,2,64,256]{3,2,1,0:T(8,128)S(1)}, f32[2,2,64,256]{3,2,1,0:T(8,128)S(1)}, u32[]{:S(2)}, u32[]{:S(2)}) %collective-permute-start.8) | collective-permute-done | bytes 262176 | tf_op jit(solution)/shard_map/ppermute | solution.py:24
  19.8 3.8 %collective-permute-done.7.refs_2_ = f32[2,2,64,256]{3,2,1,0:T(8,128)S(1)} collective-permute-done((f32[2,2,64,256]{3,2,1,0:T(8,128)S(1)}, f32[2,2,64,256]{3,2,1,0:T(8,128)S(1)}, u32[]{:S(2)}, u32[]{:S(2)}) %collective-permute-start.7) | collective-permute-done | bytes 262176 | tf_op jit(solution)/shard_map/ppermute | solution.py:24
  24.7 1.3 collective-permute-start.9
  27.0 10.0 %collective-permute-done.9.refs_3_ = f32[4,2,2,32,256]{4,3,2,1,0:T(8,128)S(1)} collective-permute-done((f32[4,2,2,32,256]{4,3,2,1,0:T(8,128)S(1)}, f32[4,2,2,32,256]{4,3,2,1,0:T(8,128)S(1)}, u32[]{:S(2)}, u32[]{:S(2)}) %collective-permute-start.9) | collective-permute-done | bytes 524320 | tf_op jit(solution)/shard_map/ppermute | solution.py:24
  39.3 1.3 dynamic-slice_bitcast_fusion.4
  41.5 4.0 %collective-permute-start.4 = (f32[2,2,64,256]{3,2,1,0:T(8,128)S(1)}, f32[2,2,64,256]{3,2,1,0:T(8,128)S(1)}, u32[]{:S(2)}, u32[]{:S(2)}) collective-permute-start(f32[2,2,64,256]{3,2,1,0:T(8,128)S(1)} %get-tuple-element.206), channel_id=1, source_target_pairs={{0,16},{4,20},{8,24},{12,28},{16,0},{20,4},{24,8},{28,12},{1,17},{... | collective-permute-start | bytes 786440 | tf_op jit(solution)/shard_map/ppermute | solution.py:24
  46.1 15.9 %collective-permute-done.4.refs_2_ = f32[2,2,64,256]{3,2,1,0:T(8,128)S(1)} collective-permute-done((f32[2,2,64,256]{3,2,1,0:T(8,128)S(1)}, f32[2,2,64,256]{3,2,1,0:T(8,128)S(1)}, u32[]{:S(2)}, u32[]{:S(2)}) %collective-permute-start.4) | collective-permute-done | bytes 262176 | tf_op jit(solution)/shard_map/ppermute | solution.py:24
  64.0 3.2 %collective-permute-start.15 = (f32[4,2,2,32,256]{4,3,2,1,0:T(8,128)S(1)}, f32[4,2,2,32,256]{4,3,2,1,0:T(8,128)S(1)}, u32[]{:S(2)}, u32[]{:S(2)}) collective-permute-start(f32[4,2,2,32,256]{4,3,2,1,0:T(8,128)S(1)} %get-tuple-element.135.refs_2_), channel_id=1, source_target_pairs={{0,1},{1,0},{2,3},{3,2},{4,5},{5,4},{6,7},{7,6},{8,9},{9,8},{10,11... | collective-permute-start | bytes 1572872 | tf_op jit(solution)/shard_map/ppermute | solution.py:24
  70.5 9.9 %collective-permute-done.11.refs_3_ = f32[4,2,2,32,256]{4,3,2,1,0:T(8,128)S(1)} collective-permute-done((f32[4,2,2,32,256]{4,3,2,1,0:T(8,128)S(1)}, f32[4,2,2,32,256]{4,3,2,1,0:T(8,128)S(1)}, u32[]{:S(2)}, u32[]{:S(2)}) %collective-permute-start.11) | collective-permute-done | bytes 524320 | tf_op jit(solution)/shard_map/ppermute | solution.py:24
  82.0 1.3 collective-permute-start.19
  83.6 2.1 %dynamic-slice_bitcast_fusion = (f32[2,2,64,256]{3,2,1,0:T(8,128)}, f32[2,2,64,256]{3,2,1,0:T(8,128)}, f32[2,2,64,256]{3,2,1,0:T(8,128)}, f32[2,2,64,256]{3,2,1,0:T(8,128)S(1)}) fusion(u32[]{:T(128)S(6)} %xor.21, u32[]{:T(128)S(6)} %xor.20, u32[]{:T(128)S(6)} %xor.19, u32[]{:T(128)S(6)} %shift_right_logical.16, f32[2,6,4,64,256]{4,3,2,1,0:T(8,128)} %bitcast.47), kind=kLoop, calls=%fused_computation.28 | loop fusion | bytes 2097168 | tf_op jit(solution)/shard_map/squeeze | solution.py:305
  86.7 4.0 %collective-permute-start.1 = (f32[2,2,64,256]{3,2,1,0:T(8,128)}, f32[2,2,64,256]{3,2,1,0:T(8,128)S(1)}, u32[]{:S(2)}, u32[]{:S(2)}) collective-permute-start(f32[2,2,64,256]{3,2,1,0:T(8,128)} %get-tuple-element.202), channel_id=1, source_target_pairs={{0,16},{4,20},{8,24},{12,28},{16,0},{20,4},{24,8},{28,12},{1,17},{... | collective-permute-start | bytes 786440 | tf_op jit(solution)/shard_map/ppermute | solution.py:24
  92.0 15.5 %collective-permute-done.1.refs_2_ = f32[2,2,64,256]{3,2,1,0:T(8,128)S(1)} collective-permute-done((f32[2,2,64,256]{3,2,1,0:T(8,128)}, f32[2,2,64,256]{3,2,1,0:T(8,128)S(1)}, u32[]{:S(2)}, u32[]{:S(2)}) %collective-permute-start.1) | collective-permute-done | bytes 262176 | tf_op jit(solution)/shard_map/ppermute | solution.py:24
  111.0 3.5 %collective-permute-start.21 = (f32[4,2,2,32,256]{4,3,2,1,0:T(8,128)S(1)}, f32[4,2,2,32,256]{4,3,2,1,0:T(8,128)S(1)}, u32[]{:S(2)}, u32[]{:S(2)}) collective-permute-start(f32[4,2,2,32,256]{4,3,2,1,0:T(8,128)S(1)} %get-tuple-element.161.refs_2_), channel_id=1, source_target_pairs={{0,1},{1,0},{2,3},{3,2},{4,5},{5,4},{6,7},{7,6},{8,9},{9,8},{10,11... | collective-permute-start | bytes 1572872 | tf_op jit(solution)/shard_map/ppermute | solution.py:24
  117.5 1.9 collective-permute-done.17.refs_3_
  121.8 3.2 %collective-permute-start.25 = (f32[2,2,64,256]{3,2,1,0:T(8,128)S(1)}, f32[2,2,64,256]{3,2,1,0:T(8,128)S(1)}, u32[]{:S(2)}, u32[]{:S(2)}) collective-permute-start(f32[2,2,64,256]{3,2,1,0:T(8,128)S(1)} %copy-done.5), channel_id=1, source_target_pairs={{0,8},{4,12},{8,0},{12,4},{16,24},{20,28},{24,16},{28,20},{1,9},{5... | collective-permute-start | bytes 786440 | tf_op jit(solution)/shard_map/ppermute | solution.py:24
  125.1 1.3 collective-permute-start.27
  126.6 3.2 %collective-permute-done.25.e1_ref = f32[2,2,64,256]{3,2,1,0:T(8,128)S(1)} collective-permute-done((f32[2,2,64,256]{3,2,1,0:T(8,128)S(1)}, f32[2,2,64,256]{3,2,1,0:T(8,128)S(1)}, u32[]{:S(2)}, u32[]{:S(2)}) %collective-permute-start.25) | collective-permute-done | bytes 262176 | tf_op jit(solution)/shard_map/ppermute | solution.py:24
  129.8 2.6 %collective-permute-done.26.e2_ref = f32[2,2,64,256]{3,2,1,0:T(8,128)S(1)} collective-permute-done((f32[2,2,64,256]{3,2,1,0:T(8,128)S(1)}, f32[2,2,64,256]{3,2,1,0:T(8,128)S(1)}, u32[]{:S(2)}, u32[]{:S(2)}) %collective-permute-start.26) | collective-permute-done | bytes 262176 | tf_op jit(solution)/shard_map/ppermute | solution.py:24
  132.4 15.7 %collective-permute-done.27.e3_ref = f32[2,2,64,256]{3,2,1,0:T(8,128)S(1)} collective-permute-done((f32[2,2,64,256]{3,2,1,0:T(8,128)S(1)}, f32[2,2,64,256]{3,2,1,0:T(8,128)S(1)}, u32[]{:S(2)}, u32[]{:S(2)}) %collective-permute-start.27) | collective-permute-done | bytes 262176 | tf_op jit(solution)/shard_map/ppermute | solution.py:24
  148.1 3.5 %finish.3.rest_0_ = f32[2,6,256,256]{3,2,1,0:T(8,128)} custom-call(bf16[2,512,512]{2,1,0:T(8,128)(2,1)S(1)} %pad_maximum_fusion.1.right_ref, bf16[2,512,512]{2,1,0:T(8,128)(2,1)S(1)} %pad_maximum_fusion.3.left_ref, f32[2,2,64,256]{3,2,1,0:T(8,128)S(1)} %get-tuple-element.175.e0_ref, f32[2,2,64,256]{3,2,1,0:T(8,128)S(1)} %collective-permute-done.25.e1_ref, ...), custom_call_target="tpu_custom_call" | custom-call | flops 1610612736 | bytes 2097152 | tf_op jit(solution)/shard_map/finish/pallas_call | solution.py:208
  152.5 2.5 %collective-permute-start.28 = (f32[4,2,2,32,256]{4,3,2,1,0:T(8,128)S(1)}, f32[4,2,2,32,256]{4,3,2,1,0:T(8,128)S(1)}, u32[]{:S(2)}, u32[]{:S(2)}) collective-permute-start(f32[4,2,2,32,256]{4,3,2,1,0:T(8,128)S(1)} %get-tuple-element.185.refs_2_), channel_id=1, source_target_pairs={{0,1},{1,0},{2,3},{3,2},{4,5},{5,4},{6,7},{7,6},{8,9},{9,8},{10,11... | collective-permute-start | bytes 1572872 | tf_op jit(solution)/shard_map/ppermute | solution.py:24
  155.0 1.3 collective-permute-start.34
  156.4 1.3 collective-permute-start.35
  160.0 4.9 %collective-permute-done.33.e1_ref = f32[2,2,64,256]{3,2,1,0:T(8,128)S(1)} collective-permute-done((f32[2,2,64,256]{3,2,1,0:T(8,128)S(1)}, f32[2,2,64,256]{3,2,1,0:T(8,128)S(1)}, u32[]{:S(2)}, u32[]{:S(2)}) %collective-permute-start.33) | collective-permute-done | bytes 262176 | tf_op jit(solution)/shard_map/ppermute | solution.py:24
  165.7 2.3 %collective-permute-done.34.e2_ref = f32[2,2,64,256]{3,2,1,0:T(8,128)S(1)} collective-permute-done((f32[2,2,64,256]{3,2,1,0:T(8,128)S(1)}, f32[2,2,64,256]{3,2,1,0:T(8,128)S(1)}, u32[]{:S(2)}, u32[]{:S(2)}) %collective-permute-start.34) | collective-permute-done | bytes 262176 | tf_op jit(solution)/shard_map/ppermute | solution.py:24
  168.0 23.6 %collective-permute-done.35.e3_ref = f32[2,2,64,256]{3,2,1,0:T(8,128)S(1)} collective-permute-done((f32[2,2,64,256]{3,2,1,0:T(8,128)S(1)}, f32[2,2,64,256]{3,2,1,0:T(8,128)S(1)}, u32[]{:S(2)}, u32[]{:S(2)}) %collective-permute-start.35) | collective-permute-done | bytes 262176 | tf_op jit(solution)/shard_map/ppermute | solution.py:24
  191.6 3.5 %finish.4.rest_0_ = f32[2,6,256,256]{3,2,1,0:T(8,128)} custom-call(bf16[2,512,512]{2,1,0:T(8,128)(2,1)S(1)} %pad_maximum_fusion.1.right_ref, bf16[2,512,512]{2,1,0:T(8,128)(2,1)S(1)} %pad_maximum_fusion.3.left_ref, f32[2,2,64,256]{3,2,1,0:T(8,128)S(1)} %get-tuple-element.193.e0_ref, ...), custom_call_target="tpu_custom_call", output_to_operand_aliasing={{}: (6, {})} | custom-call | flops 1610612736 | bytes 2097152 | tf_op jit(solution)/shard_map/finish/pallas_call | solution.py:208
  195.2 7.7 %collective-permute-done.32.e3_ref = f32[2,2,64,256]{3,2,1,0:T(8,128)S(1)} collective-permute-done((f32[2,2,64,256]{3,2,1,0:T(8,128)S(1)}, f32[2,2,64,256]{3,2,1,0:T(8,128)S(1)}, u32[]{:S(2)}, u32[]{:S(2)}) %collective-permute-start.32) | collective-permute-done | bytes 262176 | tf_op jit(solution)/shard_map/ppermute | solution.py:24
  202.8 3.5 %finish.5 = f32[2,6,256,256]{3,2,1,0:T(8,128)} custom-call(bf16[2,512,512]{2,1,0:T(8,128)(2,1)S(1)} %pad_maximum_fusion.1.right_ref, bf16[2,512,512]{2,1,0:T(8,128)(2,1)S(1)} %pad_maximum_fusion.3.left_ref, f32[2,2,64,256]{3,2,1,0:T(8,128)S(1)} %get-tuple-element.197.e0_ref, ...), custom_call_target="tpu_custom_call", output_to_operand_aliasing={{}: (6, {})} | custom-call | flops 1610612736 | bytes 2097152 | tf_op jit(solution)/shard_map/finish/pallas_call | solution.py:208
  (82 shorter events, 29.6 us)
Async XLA Ops:
  1.3 18.5 %collective-permute-start.8 = (f32[2,2,64,256]{3,2,1,0:T(8,128)S(1)}, f32[2,2,64,256]{3,2,1,0:T(8,128)S(1)}, u32[]{:S(2)}, u32[]{:S(2)}) collective-permute-start(f32[2,2,64,256]{3,2,1,0:T(8,128)S(1)} %get-tuple-element.209), channel_id=1, source_target_pairs={{0,24},{4,28},{8,16},{12,20},{16,8},{20,12},{24,0},{28,4},{1,25},{... | collective-permute-start | bytes 786440 | tf_op jit(solution)/shard_map/ppermute | solution.py:24
  1.5 22.0 %collective-permute-start.7 = (f32[2,2,64,256]{3,2,1,0:T(8,128)S(1)}, f32[2,2,64,256]{3,2,1,0:T(8,128)S(1)}, u32[]{:S(2)}, u32[]{:S(2)}) collective-permute-start(f32[2,2,64,256]{3,2,1,0:T(8,128)S(1)} %get-tuple-element.210), channel_id=1, source_target_pairs={{0,16},{4,20},{8,24},{12,28},{16,0},{20,4},{24,8},{28,12},{1,17},{... | collective-permute-start | bytes 786440 | tf_op jit(solution)/shard_map/ppermute | solution.py:24
  4.7 18.8 %collective-permute-start.6 = (f32[2,2,64,256]{3,2,1,0:T(8,128)S(1)}, f32[2,2,64,256]{3,2,1,0:T(8,128)S(1)}, u32[]{:S(2)}, u32[]{:S(2)}) collective-permute-start(f32[2,2,64,256]{3,2,1,0:T(8,128)S(1)} %get-tuple-element.211), channel_id=1, source_target_pairs={{0,8},{4,12},{8,0},{12,4},{16,24},{20,28},{24,16},{28,20},{1,9},{5... | collective-permute-start | bytes 786440 | tf_op jit(solution)/shard_map/ppermute | solution.py:24
  24.7 12.2 %collective-permute-start.9 = (f32[4,2,2,32,256]{4,3,2,1,0:T(8,128)S(1)}, f32[4,2,2,32,256]{4,3,2,1,0:T(8,128)S(1)}, u32[]{:S(2)}, u32[]{:S(2)}) collective-permute-start(f32[4,2,2,32,256]{4,3,2,1,0:T(8,128)S(1)} %get-tuple-element.117.refs_2_), channel_id=1, source_target_pairs={{0,4},{4,0},{8,12},{12,8},{16,20},{20,16},{24,28},{28,24},{1,5},{5... | collective-permute-start | bytes 1572872 | tf_op jit(solution)/shard_map/ppermute | solution.py:24
  26.0 11.9 %collective-permute-start.10 = (f32[4,2,2,32,256]{4,3,2,1,0:T(8,128)S(1)}, f32[4,2,2,32,256]{4,3,2,1,0:T(8,128)S(1)}, u32[]{:S(2)}, u32[]{:S(2)}) collective-permute-start(f32[4,2,2,32,256]{4,3,2,1,0:T(8,128)S(1)} %get-tuple-element.119.refs_4_), channel_id=1, source_target_pairs={{0,2},{1,3},{2,0},{3,1},{4,6},{5,7},{6,4},{7,5},{8,10},{9,11},{10,... | collective-permute-start | bytes 1572872 | tf_op jit(solution)/shard_map/ppermute | solution.py:24
  38.7 24.5 %collective-permute-start.13 = (f32[4,2,2,32,256]{4,3,2,1,0:T(8,128)S(1)}, f32[4,2,2,32,256]{4,3,2,1,0:T(8,128)S(1)}, u32[]{:S(2)}, u32[]{:S(2)}) collective-permute-start(f32[4,2,2,32,256]{4,3,2,1,0:T(8,128)S(1)} %get-tuple-element.129.refs_2_), channel_id=1, source_target_pairs={{0,2},{1,3},{2,0},{3,1},{4,6},{5,7},{6,4},{7,5},{8,10},{9,11},{10,... | collective-permute-start | bytes 1572872 | tf_op jit(solution)/shard_map/ppermute | solution.py:24
  39.0 24.2 %collective-permute-start.14 = (f32[4,2,2,32,256]{4,3,2,1,0:T(8,128)S(1)}, f32[4,2,2,32,256]{4,3,2,1,0:T(8,128)S(1)}, u32[]{:S(2)}, u32[]{:S(2)}) collective-permute-start(f32[4,2,2,32,256]{4,3,2,1,0:T(8,128)S(1)} %get-tuple-element.131.refs_4_), channel_id=1, source_target_pairs={{0,4},{4,0},{8,12},{12,8},{16,20},{20,16},{24,28},{28,24},{1,5},{5... | collective-permute-start | bytes 1572872 | tf_op jit(solution)/shard_map/ppermute | solution.py:24
  40.5 5.6 %collective-permute-start.5 = (f32[2,2,64,256]{3,2,1,0:T(8,128)S(1)}, f32[2,2,64,256]{3,2,1,0:T(8,128)S(1)}, u32[]{:S(2)}, u32[]{:S(2)}) collective-permute-start(f32[2,2,64,256]{3,2,1,0:T(8,128)S(1)} %get-tuple-element.205), channel_id=1, source_target_pairs={{0,24},{4,28},{8,16},{12,20},{16,8},{20,12},{24,0},{28,4},{1,25},{... | collective-permute-start | bytes 786440 | tf_op jit(solution)/shard_map/ppermute | solution.py:24
  41.5 20.5 %collective-permute-start.4 = (f32[2,2,64,256]{3,2,1,0:T(8,128)S(1)}, f32[2,2,64,256]{3,2,1,0:T(8,128)S(1)}, u32[]{:S(2)}, u32[]{:S(2)}) collective-permute-start(f32[2,2,64,256]{3,2,1,0:T(8,128)S(1)} %get-tuple-element.206), channel_id=1, source_target_pairs={{0,16},{4,20},{8,24},{12,28},{16,0},{20,4},{24,8},{28,12},{1,17},{... | collective-permute-start | bytes 786440 | tf_op jit(solution)/shard_map/ppermute | solution.py:24
  45.5 16.5 %collective-permute-start.3 = (f32[2,2,64,256]{3,2,1,0:T(8,128)S(1)}, f32[2,2,64,256]{3,2,1,0:T(8,128)S(1)}, u32[]{:S(2)}, u32[]{:S(2)}) collective-permute-start(f32[2,2,64,256]{3,2,1,0:T(8,128)S(1)} %get-tuple-element.207), channel_id=1, source_target_pairs={{0,8},{4,12},{8,0},{12,4},{16,24},{20,28},{24,16},{28,20},{1,9},{5... | collective-permute-start | bytes 786440 | tf_op jit(solution)/shard_map/ppermute | solution.py:24
  64.0 5.7 %collective-permute-start.15 = (f32[4,2,2,32,256]{4,3,2,1,0:T(8,128)S(1)}, f32[4,2,2,32,256]{4,3,2,1,0:T(8,128)S(1)}, u32[]{:S(2)}, u32[]{:S(2)}) collective-permute-start(f32[4,2,2,32,256]{4,3,2,1,0:T(8,128)S(1)} %get-tuple-element.135.refs_2_), channel_id=1, source_target_pairs={{0,1},{1,0},{2,3},{3,2},{4,5},{5,4},{6,7},{7,6},{8,9},{9,8},{10,11... | collective-permute-start | bytes 1572872 | tf_op jit(solution)/shard_map/ppermute | solution.py:24
  67.3 13.1 %collective-permute-start.11 = (f32[4,2,2,32,256]{4,3,2,1,0:T(8,128)S(1)}, f32[4,2,2,32,256]{4,3,2,1,0:T(8,128)S(1)}, u32[]{:S(2)}, u32[]{:S(2)}) collective-permute-start(f32[4,2,2,32,256]{4,3,2,1,0:T(8,128)S(1)} %get-tuple-element.143.refs_2_), channel_id=1, source_target_pairs={{0,4},{4,0},{8,12},{12,8},{16,20},{20,16},{24,28},{28,24},{1,5},{5... | collective-permute-start | bytes 1572872 | tf_op jit(solution)/shard_map/ppermute | solution.py:24
  68.5 12.8 %collective-permute-start.12 = (f32[4,2,2,32,256]{4,3,2,1,0:T(8,128)S(1)}, f32[4,2,2,32,256]{4,3,2,1,0:T(8,128)S(1)}, u32[]{:S(2)}, u32[]{:S(2)}) collective-permute-start(f32[4,2,2,32,256]{4,3,2,1,0:T(8,128)S(1)} %get-tuple-element.145.refs_4_), channel_id=1, source_target_pairs={{0,2},{1,3},{2,0},{3,1},{4,6},{5,7},{6,4},{7,5},{8,10},{9,11},{10,... | collective-permute-start | bytes 1572872 | tf_op jit(solution)/shard_map/ppermute | solution.py:24
  82.0 28.2 %collective-permute-start.19 = (f32[4,2,2,32,256]{4,3,2,1,0:T(8,128)S(1)}, f32[4,2,2,32,256]{4,3,2,1,0:T(8,128)S(1)}, u32[]{:S(2)}, u32[]{:S(2)}) collective-permute-start(f32[4,2,2,32,256]{4,3,2,1,0:T(8,128)S(1)} %get-tuple-element.155.refs_2_), channel_id=1, source_target_pairs={{0,2},{1,3},{2,0},{3,1},{4,6},{5,7},{6,4},{7,5},{8,10},{9,11},{10,... | collective-permute-start | bytes 1572872 | tf_op jit(solution)/shard_map/ppermute | solution.py:24
  83.3 26.9 %collective-permute-start.20 = (f32[4,2,2,32,256]{4,3,2,1,0:T(8,128)S(1)}, f32[4,2,2,32,256]{4,3,2,1,0:T(8,128)S(1)}, u32[]{:S(2)}, u32[]{:S(2)}) collective-permute-start(f32[4,2,2,32,256]{4,3,2,1,0:T(8,128)S(1)} %get-tuple-element.157.refs_4_), channel_id=1, source_target_pairs={{0,4},{4,0},{8,12},{12,8},{16,20},{20,16},{24,28},{28,24},{1,5},{5... | collective-permute-start | bytes 1572872 | tf_op jit(solution)/shard_map/ppermute | solution.py:24
  85.7 6.3 %collective-permute-start.2 = (f32[2,2,64,256]{3,2,1,0:T(8,128)}, f32[2,2,64,256]{3,2,1,0:T(8,128)S(1)}, u32[]{:S(2)}, u32[]{:S(2)}) collective-permute-start(f32[2,2,64,256]{3,2,1,0:T(8,128)} %get-tuple-element.201), channel_id=1, source_target_pairs={{0,24},{4,28},{8,16},{12,20},{16,8},{20,12},{24,0},{28,4},{1,25},{... | collective-permute-start | bytes 786440 | tf_op jit(solution)/shard_map/ppermute | solution.py:24
  86.7 20.9 %collective-permute-start.1 = (f32[2,2,64,256]{3,2,1,0:T(8,128)}, f32[2,2,64,256]{3,2,1,0:T(8,128)S(1)}, u32[]{:S(2)}, u32[]{:S(2)}) collective-permute-start(f32[2,2,64,256]{3,2,1,0:T(8,128)} %get-tuple-element.202), channel_id=1, source_target_pairs={{0,16},{4,20},{8,24},{12,28},{16,0},{20,4},{24,8},{28,12},{1,17},{... | collective-permute-start | bytes 786440 | tf_op jit(solution)/shard_map/ppermute | solution.py:24
  90.7 16.9 %collective-permute-start = (f32[2,2,64,256]{3,2,1,0:T(8,128)}, f32[2,2,64,256]{3,2,1,0:T(8,128)S(1)}, u32[]{:S(2)}, u32[]{:S(2)}) collective-permute-start(f32[2,2,64,256]{3,2,1,0:T(8,128)} %get-tuple-element.203), channel_id=1, source_target_pairs={{0,8},{4,12},{8,0},{12,4},{16,24},{20,28},{24,16},{28,20},{1,9},{5... | collective-permute-start | bytes 786440 | tf_op jit(solution)/shard_map/ppermute | solution.py:24
  108.7 10.7 %collective-permute-start.17 = (f32[4,2,2,32,256]{4,3,2,1,0:T(8,128)S(1)}, f32[4,2,2,32,256]{4,3,2,1,0:T(8,128)S(1)}, u32[]{:S(2)}, u32[]{:S(2)}) collective-permute-start(f32[4,2,2,32,256]{4,3,2,1,0:T(8,128)S(1)} %get-tuple-element.169.refs_2_), channel_id=1, source_target_pairs={{0,4},{4,0},{8,12},{12,8},{16,20},{20,16},{24,28},{28,24},{1,5},{5... | collective-permute-start | bytes 1572872 | tf_op jit(solution)/shard_map/ppermute | solution.py:24
  110.0 10.4 %collective-permute-start.18 = (f32[4,2,2,32,256]{4,3,2,1,0:T(8,128)S(1)}, f32[4,2,2,32,256]{4,3,2,1,0:T(8,128)S(1)}, u32[]{:S(2)}, u32[]{:S(2)}) collective-permute-start(f32[4,2,2,32,256]{4,3,2,1,0:T(8,128)S(1)} %get-tuple-element.171.refs_4_), channel_id=1, source_target_pairs={{0,2},{1,3},{2,0},{3,1},{4,6},{5,7},{6,4},{7,5},{8,10},{9,11},{10,... | collective-permute-start | bytes 1572872 | tf_op jit(solution)/shard_map/ppermute | solution.py:24
  121.1 30.6 %collective-permute-start.23 = (f32[4,2,2,32,256]{4,3,2,1,0:T(8,128)S(1)}, f32[4,2,2,32,256]{4,3,2,1,0:T(8,128)S(1)}, u32[]{:S(2)}, u32[]{:S(2)}) collective-permute-start(f32[4,2,2,32,256]{4,3,2,1,0:T(8,128)S(1)} %get-tuple-element.179.refs_2_), channel_id=1, source_target_pairs={{0,2},{1,3},{2,0},{3,1},{4,6},{5,7},{6,4},{7,5},{8,10},{9,11},{10,... | collective-permute-start | bytes 1572872 | tf_op jit(solution)/shard_map/ppermute | solution.py:24
  121.4 30.3 %collective-permute-start.24 = (f32[4,2,2,32,256]{4,3,2,1,0:T(8,128)S(1)}, f32[4,2,2,32,256]{4,3,2,1,0:T(8,128)S(1)}, u32[]{:S(2)}, u32[]{:S(2)}) collective-permute-start(f32[4,2,2,32,256]{4,3,2,1,0:T(8,128)S(1)} %get-tuple-element.181.refs_4_), channel_id=1, source_target_pairs={{0,4},{4,0},{8,12},{12,8},{16,20},{20,16},{24,28},{28,24},{1,5},{5... | collective-permute-start | bytes 1572872 | tf_op jit(solution)/shard_map/ppermute | solution.py:24
  121.8 8.0 %collective-permute-start.25 = (f32[2,2,64,256]{3,2,1,0:T(8,128)S(1)}, f32[2,2,64,256]{3,2,1,0:T(8,128)S(1)}, u32[]{:S(2)}, u32[]{:S(2)}) collective-permute-start(f32[2,2,64,256]{3,2,1,0:T(8,128)S(1)} %copy-done.5), channel_id=1, source_target_pairs={{0,8},{4,12},{8,0},{12,4},{16,24},{20,28},{24,16},{28,20},{1,9},{5... | collective-permute-start | bytes 786440 | tf_op jit(solution)/shard_map/ppermute | solution.py:24
  125.1 7.4 %collective-permute-start.26 = (f32[2,2,64,256]{3,2,1,0:T(8,128)S(1)}, f32[2,2,64,256]{3,2,1,0:T(8,128)S(1)}, u32[]{:S(2)}, u32[]{:S(2)}) collective-permute-start(f32[2,2,64,256]{3,2,1,0:T(8,128)S(1)} %copy-done.3), channel_id=1, source_target_pairs={{0,16},{4,20},{8,24},{12,28},{16,0},{20,4},{24,8},{28,12},{1,17},{... | collective-permute-start | bytes 786440 | tf_op jit(solution)/shard_map/ppermute | solution.py:24
  125.1 23.1 %collective-permute-start.27 = (f32[2,2,64,256]{3,2,1,0:T(8,128)S(1)}, f32[2,2,64,256]{3,2,1,0:T(8,128)S(1)}, u32[]{:S(2)}, u32[]{:S(2)}) collective-permute-start(f32[2,2,64,256]{3,2,1,0:T(8,128)S(1)} %copy-done.1), channel_id=1, source_target_pairs={{0,24},{4,28},{8,16},{12,20},{16,8},{20,12},{24,0},{28,4},{1,25},{... | collective-permute-start | bytes 786440 | tf_op jit(solution)/shard_map/ppermute | solution.py:24
  152.5 5.2 %collective-permute-start.28 = (f32[4,2,2,32,256]{4,3,2,1,0:T(8,128)S(1)}, f32[4,2,2,32,256]{4,3,2,1,0:T(8,128)S(1)}, u32[]{:S(2)}, u32[]{:S(2)}) collective-permute-start(f32[4,2,2,32,256]{4,3,2,1,0:T(8,128)S(1)} %get-tuple-element.185.refs_2_), channel_id=1, source_target_pairs={{0,1},{1,0},{2,3},{3,2},{4,5},{5,4},{6,7},{7,6},{8,9},{9,8},{10,11... | collective-permute-start | bytes 1572872 | tf_op jit(solution)/shard_map/ppermute | solution.py:24
  155.0 9.9 %collective-permute-start.33 = (f32[2,2,64,256]{3,2,1,0:T(8,128)S(1)}, f32[2,2,64,256]{3,2,1,0:T(8,128)S(1)}, u32[]{:S(2)}, u32[]{:S(2)}) collective-permute-start(f32[2,2,64,256]{3,2,1,0:T(8,128)S(1)} %get-tuple-element.166), channel_id=1, source_target_pairs={{0,8},{4,12},{8,0},{12,4},{16,24},{20,28},{24,16},{28,20},{1,9},{5... | collective-permute-start | bytes 786440 | tf_op jit(solution)/shard_map/ppermute | solution.py:24
  155.0 13.0 %collective-permute-start.34 = (f32[2,2,64,256]{3,2,1,0:T(8,128)S(1)}, f32[2,2,64,256]{3,2,1,0:T(8,128)S(1)}, u32[]{:S(2)}, u32[]{:S(2)}) collective-permute-start(f32[2,2,64,256]{3,2,1,0:T(8,128)S(1)} %get-tuple-element.167), channel_id=1, source_target_pairs={{0,16},{4,20},{8,24},{12,28},{16,0},{20,4},{24,8},{28,12},{1,17},{... | collective-permute-start | bytes 786440 | tf_op jit(solution)/shard_map/ppermute | solution.py:24
  156.4 35.2 %collective-permute-start.35 = (f32[2,2,64,256]{3,2,1,0:T(8,128)S(1)}, f32[2,2,64,256]{3,2,1,0:T(8,128)S(1)}, u32[]{:S(2)}, u32[]{:S(2)}) collective-permute-start(f32[2,2,64,256]{3,2,1,0:T(8,128)S(1)} %get-tuple-element.168), channel_id=1, source_target_pairs={{0,24},{4,28},{8,16},{12,20},{16,8},{20,12},{24,0},{28,4},{1,25},{... | collective-permute-start | bytes 786440 | tf_op jit(solution)/shard_map/ppermute | solution.py:24
  158.6 36.5 %collective-permute-start.30 = (f32[2,2,64,256]{3,2,1,0:T(8,128)S(1)}, f32[2,2,64,256]{3,2,1,0:T(8,128)S(1)}, u32[]{:S(2)}, u32[]{:S(2)}) collective-permute-start(f32[2,2,64,256]{3,2,1,0:T(8,128)S(1)} %get-tuple-element.190), channel_id=1, source_target_pairs={{0,8},{4,12},{8,0},{12,4},{16,24},{20,28},{24,16},{28,20},{1,9},{5... | collective-permute-start | bytes 786440 | tf_op jit(solution)/shard_map/ppermute | solution.py:24
  159.6 35.6 %collective-permute-start.31 = (f32[2,2,64,256]{3,2,1,0:T(8,128)S(1)}, f32[2,2,64,256]{3,2,1,0:T(8,128)S(1)}, u32[]{:S(2)}, u32[]{:S(2)}) collective-permute-start(f32[2,2,64,256]{3,2,1,0:T(8,128)S(1)} %get-tuple-element.191), channel_id=1, source_target_pairs={{0,16},{4,20},{8,24},{12,28},{16,0},{20,4},{24,8},{28,12},{1,17},{... | collective-permute-start | bytes 786440 | tf_op jit(solution)/shard_map/ppermute | solution.py:24
  164.9 37.9 %collective-permute-start.32 = (f32[2,2,64,256]{3,2,1,0:T(8,128)S(1)}, f32[2,2,64,256]{3,2,1,0:T(8,128)S(1)}, u32[]{:S(2)}, u32[]{:S(2)}) collective-permute-start(f32[2,2,64,256]{3,2,1,0:T(8,128)S(1)} %get-tuple-element.192), channel_id=1, source_target_pairs={{0,24},{4,28},{8,16},{12,20},{16,8},{20,12},{24,0},{28,4},{1,25},{... | collective-permute-start | bytes 786440 | tf_op jit(solution)/shard_map/ppermute | solution.py:24
  (10 other events, 97.3 us)
where the time goes:
time: 209 us; the launch traced here: 207 us
  waiting for transfers between devices  135 us (65%)
  starting transfers between devices  40.4 us (19%)
  Pallas kernels  21.2 us (10%)
  local copies, waits for them, and re-layouts  6.03 us (3%)
  other arithmetic  2.93 us (1%)
    ppermute x36, waiting for transfers between devices, exchanged(): return lax.ppermute(block, axis, [(i, i ^ mask) for i in range(count)])  135 us
    ppermute x36, starting transfers between devices, exchanged(): return lax.ppermute(block, axis, [(i, i ^ mask) for i in range(count)])  40.4 us
    pallas_call x3, Pallas kernels, finish(): pl.pallas_call(functools.partial(finish_kernel, start), in_specs=in_specs...  10.6 us
    pallas_call x9, Pallas kernels, butterfly(): pl.pallas_call(functools.partial(butterfly_kernel, kinds, apart), in_spec...  7.11 us
    squeeze x3, local copies, waits for them, and re-layouts, shards(): lax.dynamic_slice(quarters, (zero, at, peer, zero, zero), shape)[:, :, 0]  4.63 us
  transfers between devices with their start and end apart: 36, of which 20 were waited for; matrix products, arithmetic and copies ran while one was open for 4% of the time, Pallas kernels for 6%

commit v1 on v0

--- a/solution.py
+++ b/solution.py
@@ -11,6 +11,7 @@
 
 
 GRANT = 16 * 2**20
+LANES = (3, 2, 1)
 
 F32 = jnp.float32
 BF16 = jnp.bfloat16
@@ -37,30 +38,26 @@
     return pl.CostEstimate(flops=flops, transcendentals=0, bytes_accessed=4 * count)
 
 
-def dft_matrix(frequency, count, local, at):
+def dft_table(inputs, outputs, count, local, frequency):
     length = count * local
-    to = jnp.arange(local, dtype=jnp.int32)
-    cosine, sine = unit(at[:, None] * (frequency + count * to[None, :]), length)
-    scale = 1.0 / math.sqrt(length)
-    return cosine * scale, sine * scale
-
-
-def split(values):
+    turn = (inputs[1] - outputs[1]) * (length // 4)
+    values = unit(inputs[0] * (frequency + count * outputs[0]) - turn, length)[0] * (1.0 / math.sqrt(length))
     high = lax.reduce_precision(values, 8, 7)
-    return jnp.stack([high.astype(BF16), (values - high).astype(BF16)])
-
-
-def right_matrix(frequency, count, local):
-    cosine, sine = dft_matrix(frequency, count, local, jnp.arange(local, dtype=jnp.int32))
-    return split(jnp.block([[cosine, sine], [-sine, cosine]]))
-
-
-def left_matrix(frequency, count, local, part):
-    at = jnp.arange(local, dtype=jnp.int32)
+    return high.astype(BF16), (values - high).astype(BF16)
+
+
+def right_tables(frequency, count, local):
+    at = jnp.arange(2 * local, dtype=jnp.int32)
+    at = at % local, at // local
+    return dft_table([x[:, None] for x in at], [x[None, :] for x in at], count, local, frequency)
+
+
+def left_tables(frequency, count, local, part):
+    at = jnp.arange(2 * local, dtype=jnp.int32)
     quarter = local // 4
-    at = (part ^ (at // quarter)) * quarter + at % quarter
-    cosine, sine = dft_matrix(frequency, count, local, at)
-    return split(jnp.block([[cosine.T, -sine.T], [sine.T, cosine.T]]))
+    row = (part ^ (at // (2 * quarter))) * quarter + at % quarter
+    inputs = row[None, :], (at // quarter % 2)[None, :]
+    return dft_table(inputs, [x[:, None] for x in (at % local, at // local)], count, local, frequency)
 
 
 def halves(values):
@@ -73,18 +70,6 @@
         return jnp.dot(a, b, preferred_element_type=F32)
 
     return single(left[0], right[0]) + (single(left[1], right[0]) + single(left[0], right[1]))
-
-
-def along_last(real, imag, matrix_ref):
-    local = real.shape[-1]
-    mixed = dot3(halves(jnp.concatenate([real, imag], axis=1)), (matrix_ref[0], matrix_ref[1]))
-    return mixed[:, :local], mixed[:, local:]
-
-
-def along_first(real, imag, matrix_ref):
-    local = real.shape[0]
-    mixed = dot3((matrix_ref[0], matrix_ref[1]), halves(jnp.concatenate([real, imag], axis=0)))
-    return mixed[:local], mixed[local:]
 
 
 def after(value, done):
@@ -178,35 +163,71 @@
     )
 
 
-def finish_kernel(start, right_ref, left_ref, e0_ref, e1_ref, e2_ref, e3_ref, *rest):
-    out_ref, done, sems = rest[-3:]
-    planes = e0_ref.shape[1]
+def transformed(plane, lanes, tables, piece_refs):
+    right, left = tables[:2], tables[2:]
+    quarter, columns = piece_refs[0].shape[2:]
+    data = [jnp.concatenate([ref[0, plane], ref[1, plane]], axis=1) for ref in piece_refs]
+    mixed = dot3(halves(jnp.concatenate(data, axis=0)), [ref[...] for ref in right])
+    rows = []
+    for i in range(len(lanes)):
+        part = mixed[i * quarter : (i + 1) * quarter]
+        rows += [part[:, :columns], part[:, columns:]]
+    width = 2 * quarter
+    sides = [jnp.concatenate([ref[:, d * width : (d + 1) * width] for d in lanes], axis=1) for ref in left]
+    return dot3(sides, halves(jnp.concatenate(rows, axis=0)))
+
+
+def begin_kernel(lanes, *refs):
+    base_ref = refs[-1]
+    local = base_ref.shape[2]
+    for plane in range(base_ref.shape[0]):
+        values = transformed(plane, lanes, refs[:4], refs[4:-1])
+        base_ref[plane, 0] = values[:local]
+        base_ref[plane, 1] = values[local:]
+
+
+def begin(pieces, lanes, tables):
+    _, planes, quarter, columns = pieces[0].shape
+    rows = 4 * quarter
+    return pl.pallas_call(
+        functools.partial(begin_kernel, lanes),
+        in_specs=[VMEM] * (4 + len(lanes)),
+        out_specs=VMEM,
+        out_shape=jax.ShapeDtypeStruct((planes, 2, rows, columns), F32),
+        compiler_params=pltpu.CompilerParams(vmem_limit_bytes=GRANT),
+        cost_estimate=estimate(6 * len(lanes) * planes * rows * columns * (rows + columns), 4 * planes * rows * columns),
+        name="begin",
+    )(*tables, *pieces)
+
+
+def finish_kernel(start, lanes, has_base, *refs):
+    out_ref, done, sems = refs[-3:]
+    count = len(lanes)
+    planes, _, local, _ = done.shape
     copies = []
     for plane in range(planes):
-        refs = (e0_ref, e1_ref, e2_ref, e3_ref)
-        whole = [jnp.concatenate([ref[part, plane] for ref in refs], axis=0) for part in range(2)]
-        real, imag = along_last(whole[0], whole[1], right_ref)
-        real, imag = along_first(real, imag, left_ref)
-        done[plane, 0] = real
-        done[plane, 1] = imag
+        values = transformed(plane, lanes, refs[:4], refs[4 : 4 + count])
+        for part in range(2):
+            half = values[part * local : (part + 1) * local]
+            done[plane, part] = half + refs[4 + count][plane, part] if has_base else half
         copies.append(pltpu.make_async_copy(done.at[plane], out_ref.at[:, start + plane], sems.at[plane]))
         copies[-1].start()
     for copy in copies:
         copy.wait()
 
 
-def finish(pieces, right, left, out, start, total):
+def finish(pieces, lanes, base, tables, out, start, total):
     _, planes, quarter, columns = pieces[0].shape
     rows = 4 * quarter
-    in_specs = [VMEM] * 6
-    args = [right, left, *pieces]
+    args = [*tables, *pieces] + ([] if base is None else [base])
+    in_specs = [VMEM] * len(args)
     aliases = {}
     if out is not None:
         in_specs.append(ANY)
         aliases = {len(args): 0}
         args.append(out)
     return pl.pallas_call(
-        functools.partial(finish_kernel, start),
+        functools.partial(finish_kernel, start, lanes, base is not None),
         in_specs=in_specs,
         out_specs=ANY,
         out_shape=jax.ShapeDtypeStruct((2, total, rows, columns), F32),
@@ -216,7 +237,7 @@
         ],
         input_output_aliases=aliases,
         compiler_params=pltpu.CompilerParams(vmem_limit_bytes=GRANT),
-        cost_estimate=estimate(24 * planes * rows * columns * (rows + columns), 4 * planes * rows * columns),
+        cost_estimate=estimate(6 * len(lanes) * planes * rows * columns * (rows + columns), 4 * planes * rows * columns),
         name="finish",
     )(*args)
 
@@ -299,19 +320,24 @@
     quarters = velocity.reshape(2, planes, 4, quarter, columns)
     received = []
     zero = jnp.uint32(0)
-    for start, size in chunks:
+    for i, (start, size) in enumerate(chunks):
         shape = (2, size, 1, quarter, columns)
         at = jnp.uint32(start)
-        pieces = [lax.dynamic_slice(quarters, (zero, at, peer, zero, zero), shape)[:, :, 0] for peer in peers]
-        quarters = after(quarters, pieces)
+        pieces = [None] * 4
+        for lanes in ((LANES[0],), (*LANES[1:], 0)) if i == 0 else ((*LANES, 0),):
+            for d in lanes:
+                pieces[d] = lax.dynamic_slice(quarters, (zero, at, peers[d], zero, zero), shape)[:, :, 0]
+            quarters = after(quarters, [pieces[d] for d in lanes])
         received.append(pieces[:1] + [exchanged(pieces[d], "gz", d * stride) for d in range(1, 4)])
 
     z_steps, y_steps = list(reversed(range(z_bits - 2))), list(reversed(range(y_bits)))
     z_table = np.concatenate([mix_table(z_count)] + [pair_table(z_count, bit) for bit in z_steps], axis=1)
     y_table = np.concatenate([pair_table(y_count, bit) for bit in y_steps], axis=1)
     coefs = [row_of(z_table, z_index), row_of(y_table, y_index)]
-    right = right_matrix(shifts[0].astype(jnp.int32), z_count, columns)
-    left = left_matrix(shifts[1].astype(jnp.int32), y_count, rows, part.astype(jnp.int32))
+    tables = [
+        *right_tables(shifts[0].astype(jnp.int32), z_count, columns),
+        *left_tables(shifts[1].astype(jnp.int32), y_count, rows, part.astype(jnp.int32)),
+    ]
     z_pairs = [("gz", bit, (0, 32 + 3 * i, bit > 0)) for i, bit in enumerate(z_steps)]
     y_pairs = [("gy", bit, (1, 3 * i, bit > 0)) for i, bit in enumerate(y_steps)]
     ways = list(zip(z_pairs + y_pairs[:-1], y_pairs[:-1] + z_pairs))
@@ -334,8 +360,14 @@
             if step == steps - 1:
                 back[i] = state[i][:1] + [exchanged(state[i][d], "gz", d * stride) for d in range(1, 4)]
         elif kind == "end":
-            pieces = after(back[i], done)
-            result = finish(pieces, right, left, result, chunks[i][0], planes)
+            lanes, base = (0, 1, 2, 3), None
+            if i == len(chunks) - 1:
+                early, lanes = (0, 1, 3), (2,)
+                pieces = after([back[i][d] for d in early], done)
+                base = begin(pieces, early, tables)
+                done = base
+            pieces = after([back[i][d] for d in lanes], done)
+            result = finish(pieces, lanes, base, tables, result, chunks[i][0], planes)
         done = result if kind == "end" else state[i] if kind == "node" else done
     return result
 

time: 209 us -> 203 us (0.971)
  the two profiles are of different devices: /device:TPU:19 before, /device:TPU:0 now
where the time goes in v1:
time: 203 us
  waiting for transfers between devices  121 us (60%)
  starting transfers between devices  43.3 us (21%)
  Pallas kernels  22.7 us (11%)
  other arithmetic  8.73 us (4%)
  local copies, waits for them, and re-layouts  6.08 us (3%)
    ppermute x36, waiting for transfers between devices, exchanged(): return lax.ppermute(block, axis, [(i, i ^ mask) for i in range(count)])  121 us
    ppermute x36, starting transfers between devices, exchanged(): return lax.ppermute(block, axis, [(i, i ^ mask) for i in range(count)])  43.3 us
    pallas_call x3, Pallas kernels, finish(): pl.pallas_call(functools.partial(finish_kernel, start, lanes, base is not...  9.71 us
    convert_element_type x1, other arithmetic, dft_table(): return (high.astype(BF16), (values - high).astype(BF16))  8.71 us
    pallas_call x9, Pallas kernels, butterfly(): pl.pallas_call(functools.partial(butterfly_kernel, kinds, apart), in_spec...  7.77 us
    squeeze x4, local copies, waits for them, and re-layouts, shards(): lax.dynamic_slice(quarters, (zero, at, peers[d], zero, zero), shape)  4.69 us
  transfers between devices with their start and end apart: 36, of which 18 were waited for; matrix products, arithmetic and copies ran while one was open for 7% of the time, Pallas kernels for 7%

profile of v1, /device:TPU:0, one launch (start us, length us, event | category | flops | bytes accessed | tf_op | source)
XLA Modules:
  0.0 202.8 jit_solution(4217930668710112718)
XLA Ops:
  1.0 5.1 %collective-permute-start.8 = (f32[2,2,64,256]{3,2,1,0:T(8,128)S(1)}, f32[2,2,64,256]{3,2,1,0:T(8,128)S(1)}, u32[]{:S(2)}, u32[]{:S(2)}) collective-permute-start(f32[2,2,64,256]{3,2,1,0:T(8,128)S(1)} %dynamic-slice_bitcast_fusion.11), channel_id=1, source_target_pairs={{0,24},{4,28},{8,16},{12,20},{16,8},{20,12},{24,0},{28,4},{1,25},{... | collective-permute-start | bytes 786440 | tf_op jit(solution)/shard_map/ppermute | solution.py:25
  8.6 4.7 %collective-permute-done.8.refs_3_ = f32[2,2,64,256]{3,2,1,0:T(8,128)S(1)} collective-permute-done((f32[2,2,64,256]{3,2,1,0:T(8,128)S(1)}, f32[2,2,64,256]{3,2,1,0:T(8,128)S(1)}, u32[]{:S(2)}, u32[]{:S(2)}) %collective-permute-start.8) | collective-permute-done | bytes 262176 | tf_op jit(solution)/shard_map/ppermute | solution.py:25
  13.3 5.8 %collective-permute-done.6.refs_1_ = f32[2,2,64,256]{3,2,1,0:T(8,128)S(1)} collective-permute-done((f32[2,2,64,256]{3,2,1,0:T(8,128)S(1)}, f32[2,2,64,256]{3,2,1,0:T(8,128)S(1)}, u32[]{:S(2)}, u32[]{:S(2)}) %collective-permute-start.6) | collective-permute-done | bytes 262176 | tf_op jit(solution)/shard_map/ppermute | solution.py:25
  19.1 9.3 %collective-permute-done.7.refs_2_ = f32[2,2,64,256]{3,2,1,0:T(8,128)S(1)} collective-permute-done((f32[2,2,64,256]{3,2,1,0:T(8,128)S(1)}, f32[2,2,64,256]{3,2,1,0:T(8,128)S(1)}, u32[]{:S(2)}, u32[]{:S(2)}) %collective-permute-start.7) | collective-permute-done | bytes 262176 | tf_op jit(solution)/shard_map/ppermute | solution.py:25
  29.6 1.6 collective-permute-start.9
  33.4 9.3 %collective-permute-done.9.refs_3_ = f32[4,2,2,32,256]{4,3,2,1,0:T(8,128)S(1)} collective-permute-done((f32[4,2,2,32,256]{4,3,2,1,0:T(8,128)S(1)}, f32[4,2,2,32,256]{4,3,2,1,0:T(8,128)S(1)}, u32[]{:S(2)}, u32[]{:S(2)}) %collective-permute-start.9) | collective-permute-done | bytes 524320 | tf_op jit(solution)/shard_map/ppermute | solution.py:25
  44.7 1.6 collective-permute-start.13
  48.1 2.8 %collective-permute-start.4 = (f32[2,2,64,256]{3,2,1,0:T(8,128)S(1)}, f32[2,2,64,256]{3,2,1,0:T(8,128)S(1)}, u32[]{:S(2)}, u32[]{:S(2)}) collective-permute-start(f32[2,2,64,256]{3,2,1,0:T(8,128)S(1)} %get-tuple-element.209), channel_id=1, source_target_pairs={{0,16},{4,20},{8,24},{12,28},{16,0},{20,4},{24,8},{28,12},{1,17},{... | collective-permute-start | bytes 786440 | tf_op jit(solution)/shard_map/ppermute | solution.py:25
  51.0 1.5 collective-permute-start.5
  52.5 6.8 %collective-permute-done.3.refs_1_ = f32[2,2,64,256]{3,2,1,0:T(8,128)S(1)} collective-permute-done((f32[2,2,64,256]{3,2,1,0:T(8,128)S(1)}, f32[2,2,64,256]{3,2,1,0:T(8,128)S(1)}, u32[]{:S(2)}, u32[]{:S(2)}) %collective-permute-start.3) | collective-permute-done | bytes 262176 | tf_op jit(solution)/shard_map/ppermute | solution.py:25
  59.3 9.3 %collective-permute-done.4.refs_2_ = f32[2,2,64,256]{3,2,1,0:T(8,128)S(1)} collective-permute-done((f32[2,2,64,256]{3,2,1,0:T(8,128)S(1)}, f32[2,2,64,256]{3,2,1,0:T(8,128)S(1)}, u32[]{:S(2)}, u32[]{:S(2)}) %collective-permute-start.4) | collective-permute-done | bytes 262176 | tf_op jit(solution)/shard_map/ppermute | solution.py:25
  74.1 11.0 %collective-permute-done.11.refs_3_ = f32[4,2,2,32,256]{4,3,2,1,0:T(8,128)S(1)} collective-permute-done((f32[4,2,2,32,256]{4,3,2,1,0:T(8,128)S(1)}, f32[4,2,2,32,256]{4,3,2,1,0:T(8,128)S(1)}, u32[]{:S(2)}, u32[]{:S(2)}) %collective-permute-start.11) | collective-permute-done | bytes 524320 | tf_op jit(solution)/shard_map/ppermute | solution.py:25
  89.5 2.2 %collective-permute-start.2 = (f32[2,2,64,256]{3,2,1,0:T(8,128)S(1)}, f32[2,2,64,256]{3,2,1,0:T(8,128)S(1)}, u32[]{:S(2)}, u32[]{:S(2)}) collective-permute-start(f32[2,2,64,256]{3,2,1,0:T(8,128)S(1)} %get-tuple-element.203), channel_id=1, source_target_pairs={{0,24},{4,28},{8,16},{12,20},{16,8},{20,12},{24,0},{28,4},{1,25},{... | collective-permute-start | bytes 786440 | tf_op jit(solution)/shard_map/ppermute | solution.py:25
  91.7 3.0 %collective-permute-start.1 = (f32[2,2,64,256]{3,2,1,0:T(8,128)S(1)}, f32[2,2,64,256]{3,2,1,0:T(8,128)S(1)}, u32[]{:S(2)}, u32[]{:S(2)}) collective-permute-start(f32[2,2,64,256]{3,2,1,0:T(8,128)S(1)} %get-tuple-element.204), channel_id=1, source_target_pairs={{0,16},{4,20},{8,24},{12,28},{16,0},{20,4},{24,8},{28,12},{1,17},{... | collective-permute-start | bytes 786440 | tf_op jit(solution)/shard_map/ppermute | solution.py:25
  94.7 5.9 %collective-permute-done.2.refs_3_ = f32[2,2,64,256]{3,2,1,0:T(8,128)S(1)} collective-permute-done((f32[2,2,64,256]{3,2,1,0:T(8,128)S(1)}, f32[2,2,64,256]{3,2,1,0:T(8,128)S(1)}, u32[]{:S(2)}, u32[]{:S(2)}) %collective-permute-start.2) | collective-permute-done | bytes 262176 | tf_op jit(solution)/shard_map/ppermute | solution.py:25
  100.6 14.2 %collective-permute-done.1.refs_2_ = f32[2,2,64,256]{3,2,1,0:T(8,128)S(1)} collective-permute-done((f32[2,2,64,256]{3,2,1,0:T(8,128)S(1)}, f32[2,2,64,256]{3,2,1,0:T(8,128)S(1)}, u32[]{:S(2)}, u32[]{:S(2)}) %collective-permute-start.1) | collective-permute-done | bytes 262176 | tf_op jit(solution)/shard_map/ppermute | solution.py:25
  120.5 2.6 %collective-permute-start.26 = (f32[2,2,64,256]{3,2,1,0:T(8,128)}, f32[2,2,64,256]{3,2,1,0:T(8,128)S(1)}, u32[]{:S(2)}, u32[]{:S(2)}) collective-permute-start(f32[2,2,64,256]{3,2,1,0:T(8,128)} %copy-done.1), channel_id=1, source_target_pairs={{0,16},{4,20},{8,24},{12,28},{16,0},{20,4},{24,8},{28,12},{1,17},{... | collective-permute-start | bytes 786440 | tf_op jit(solution)/shard_map/ppermute | solution.py:25
  123.1 1.7 collective-permute-start.27
  126.3 5.0 %collective-permute-done.17.refs_3_ = f32[4,2,2,32,256]{4,3,2,1,0:T(8,128)S(1)} collective-permute-done((f32[4,2,2,32,256]{4,3,2,1,0:T(8,128)S(1)}, f32[4,2,2,32,256]{4,3,2,1,0:T(8,128)S(1)}, u32[]{:S(2)}, u32[]{:S(2)}) %collective-permute-start.17) | collective-permute-done | bytes 524320 | tf_op jit(solution)/shard_map/ppermute | solution.py:25
  133.3 1.6 collective-permute-start.23
  135.4 8.7 %fusion.1 = (bf16[512,512]{1,0:T(8,128)(2,1)S(1)}, bf16[512,512]{1,0:T(8,128)(2,1)S(1)}, bf16[512,512]{1,0:T(8,128)(2,1)S(1)}, bf16[512,512]{1,0:T(8,128)(2,1)S(1)}) fusion(s32[512]{0:T(512)S(1)} %get-tuple-element.221, s32[512]{0:T(512)S(1)} %get-tuple-element.220, s32[512]{0:T(512)S(1)} %get-tuple-element.224, s32[512]{0:T(512)S(1)} %get-tuple-element.223, ...), kind=kLoop, calls=%fused_computation.11 | loop fusion | flops 11534336 | bytes 2109440 | tf_op jit(solution)/shard_map/convert_element_type | solution.py:46
  144.2 3.6 %finish.3.refs_8_ = f32[2,6,256,256]{3,2,1,0:T(8,128)} custom-call(bf16[512,512]{1,0:T(8,128)(2,1)S(1)} %get-tuple-element.218.refs_0_, bf16[512,512]{1,0:T(8,128)(2,1)S(1)} %get-tuple-element.219.refs_1_, bf16[512,512]{1,0:T(8,128)(2,1)S(1)} %get-tuple-element.215.refs_2_, bf16[512,512]{1,0:T(8,128)(2,1)S(1)} %get-tuple-element.214.refs_3_, ...), custom_call_target="tpu_custom_call" | custom-call | flops 1610612736 | bytes 2097152 | tf_op jit(solution)/shard_map/finish/pallas_call | solution.py:229
  149.2 2.7 %collective-permute-start.33 = (f32[2,2,64,256]{3,2,1,0:T(8,128)S(1)}, f32[2,2,64,256]{3,2,1,0:T(8,128)S(1)}, u32[]{:S(2)}, u32[]{:S(2)}) collective-permute-start(f32[2,2,64,256]{3,2,1,0:T(8,128)S(1)} %get-tuple-element.168), channel_id=1, source_target_pairs={{0,8},{4,12},{8,0},{12,4},{16,24},{20,28},{24,16},{28,20},{1,9},{5... | collective-permute-start | bytes 786440 | tf_op jit(solution)/shard_map/ppermute | solution.py:25
  152.5 1.7 collective-permute-start.35
  156.3 2.1 %collective-permute-start.32 = (f32[2,2,64,256]{3,2,1,0:T(8,128)S(1)}, f32[2,2,64,256]{3,2,1,0:T(8,128)S(1)}, u32[]{:S(2)}, u32[]{:S(2)}) collective-permute-start(f32[2,2,64,256]{3,2,1,0:T(8,128)S(1)} %get-tuple-element.194), channel_id=1, source_target_pairs={{0,24},{4,28},{8,16},{12,20},{16,8},{20,12},{24,0},{28,4},{1,25},{... | collective-permute-start | bytes 786440 | tf_op jit(solution)/shard_map/ppermute | solution.py:25
  158.4 5.4 %collective-permute-done.33.refs_5_ = f32[2,2,64,256]{3,2,1,0:T(8,128)S(1)} collective-permute-done((f32[2,2,64,256]{3,2,1,0:T(8,128)S(1)}, f32[2,2,64,256]{3,2,1,0:T(8,128)S(1)}, u32[]{:S(2)}, u32[]{:S(2)}) %collective-permute-start.33) | collective-permute-done | bytes 262176 | tf_op jit(solution)/shard_map/ppermute | solution.py:25
  163.8 9.4 %collective-permute-done.34.refs_6_ = f32[2,2,64,256]{3,2,1,0:T(8,128)S(1)} collective-permute-done((f32[2,2,64,256]{3,2,1,0:T(8,128)S(1)}, f32[2,2,64,256]{3,2,1,0:T(8,128)S(1)}, u32[]{:S(2)}, u32[]{:S(2)}) %collective-permute-start.34) | collective-permute-done | bytes 262176 | tf_op jit(solution)/shard_map/ppermute | solution.py:25
  173.2 3.6 %finish.4.refs_6_ = f32[2,6,256,256]{3,2,1,0:T(8,128)} custom-call(bf16[512,512]{1,0:T(8,128)(2,1)S(1)} %get-tuple-element.218.refs_0_, bf16[512,512]{1,0:T(8,128)(2,1)S(1)} %get-tuple-element.219.refs_1_, bf16[512,512]{1,0:T(8,128)(2,1)S(1)} %get-tuple-element.215.refs_2_, ...), custom_call_target="tpu_custom_call", output_to_operand_aliasing={{}: (8, {})} | custom-call | flops 1610612736 | bytes 2097152 | tf_op jit(solution)/shard_map/finish/pallas_call | solution.py:229
  176.8 6.9 %collective-permute-done.32.refs_6_ = f32[2,2,64,256]{3,2,1,0:T(8,128)S(1)} collective-permute-done((f32[2,2,64,256]{3,2,1,0:T(8,128)S(1)}, f32[2,2,64,256]{3,2,1,0:T(8,128)S(1)}, u32[]{:S(2)}, u32[]{:S(2)}) %collective-permute-start.32) | collective-permute-done | bytes 262176 | tf_op jit(solution)/shard_map/ppermute | solution.py:25
  183.7 1.7 begin.1.refs_5_
  185.5 14.7 %collective-permute-done.30.refs_4_ = f32[2,2,64,256]{3,2,1,0:T(8,128)S(1)} collective-permute-done((f32[2,2,64,256]{3,2,1,0:T(8,128)S(1)}, f32[2,2,64,256]{3,2,1,0:T(8,128)S(1)}, u32[]{:S(2)}, u32[]{:S(2)}) %collective-permute-start.30) | collective-permute-done | bytes 262176 | tf_op jit(solution)/shard_map/ppermute | solution.py:25
  200.2 2.5 %finish.5 = f32[2,6,256,256]{3,2,1,0:T(8,128)} custom-call(bf16[512,512]{1,0:T(8,128)(2,1)S(1)} %get-tuple-element.218.refs_0_, bf16[512,512]{1,0:T(8,128)(2,1)S(1)} %get-tuple-element.219.refs_1_, bf16[512,512]{1,0:T(8,128)(2,1)S(1)} %get-tuple-element.215.refs_2_, bf16[512,512]{1,0:T(8,128)(2,1)S(1)} %get-tuple-element.214.refs_3_, ...), custom_call_target="tpu_custom_call", output_to_operand_aliasing={{}: (6, {})} | custom-call | flops 402653184 | bytes 2097152 | tf_op jit(solution)/shard_map/finish/pallas_call | solution.py:229
  (72 shorter events, 34.2 us)
Async XLA Ops:
  1.0 12.3 %collective-permute-start.8 = (f32[2,2,64,256]{3,2,1,0:T(8,128)S(1)}, f32[2,2,64,256]{3,2,1,0:T(8,128)S(1)}, u32[]{:S(2)}, u32[]{:S(2)}) collective-permute-start(f32[2,2,64,256]{3,2,1,0:T(8,128)S(1)} %dynamic-slice_bitcast_fusion.11), channel_id=1, source_target_pairs={{0,24},{4,28},{8,16},{12,20},{16,8},{20,12},{24,0},{28,4},{1,25},{... | collective-permute-start | bytes 786440 | tf_op jit(solution)/shard_map/ppermute | solution.py:25
  7.3 11.8 %collective-permute-start.6 = (f32[2,2,64,256]{3,2,1,0:T(8,128)S(1)}, f32[2,2,64,256]{3,2,1,0:T(8,128)S(1)}, u32[]{:S(2)}, u32[]{:S(2)}) collective-permute-start(f32[2,2,64,256]{3,2,1,0:T(8,128)S(1)} %get-tuple-element.212), channel_id=1, source_target_pairs={{0,8},{4,12},{8,0},{12,4},{16,24},{20,28},{24,16},{28,20},{1,9},{5... | collective-permute-start | bytes 786440 | tf_op jit(solution)/shard_map/ppermute | solution.py:25
  7.4 21.1 %collective-permute-start.7 = (f32[2,2,64,256]{3,2,1,0:T(8,128)S(1)}, f32[2,2,64,256]{3,2,1,0:T(8,128)S(1)}, u32[]{:S(2)}, u32[]{:S(2)}) collective-permute-start(f32[2,2,64,256]{3,2,1,0:T(8,128)S(1)} %get-tuple-element.213), channel_id=1, source_target_pairs={{0,16},{4,20},{8,24},{12,28},{16,0},{20,4},{24,8},{28,12},{1,17},{... | collective-permute-start | bytes 786440 | tf_op jit(solution)/shard_map/ppermute | solution.py:25
  29.6 13.1 %collective-permute-start.9 = (f32[4,2,2,32,256]{4,3,2,1,0:T(8,128)S(1)}, f32[4,2,2,32,256]{4,3,2,1,0:T(8,128)S(1)}, u32[]{:S(2)}, u32[]{:S(2)}) collective-permute-start(f32[4,2,2,32,256]{4,3,2,1,0:T(8,128)S(1)} %get-tuple-element.119.refs_2_), channel_id=1, source_target_pairs={{0,4},{4,0},{8,12},{12,8},{16,20},{20,16},{24,28},{28,24},{1,5},{5... | collective-permute-start | bytes 1572872 | tf_op jit(solution)/shard_map/ppermute | solution.py:25
  31.2 12.7 %collective-permute-start.10 = (f32[4,2,2,32,256]{4,3,2,1,0:T(8,128)S(1)}, f32[4,2,2,32,256]{4,3,2,1,0:T(8,128)S(1)}, u32[]{:S(2)}, u32[]{:S(2)}) collective-permute-start(f32[4,2,2,32,256]{4,3,2,1,0:T(8,128)S(1)} %get-tuple-element.121.refs_4_), channel_id=1, source_target_pairs={{0,2},{1,3},{2,0},{3,1},{4,6},{5,7},{6,4},{7,5},{8,10},{9,11},{10,... | collective-permute-start | bytes 1572872 | tf_op jit(solution)/shard_map/ppermute | solution.py:25
  44.7 25.1 %collective-permute-start.13 = (f32[4,2,2,32,256]{4,3,2,1,0:T(8,128)S(1)}, f32[4,2,2,32,256]{4,3,2,1,0:T(8,128)S(1)}, u32[]{:S(2)}, u32[]{:S(2)}) collective-permute-start(f32[4,2,2,32,256]{4,3,2,1,0:T(8,128)S(1)} %get-tuple-element.131.refs_2_), channel_id=1, source_target_pairs={{0,2},{1,3},{2,0},{3,1},{4,6},{5,7},{6,4},{7,5},{8,10},{9,11},{10,... | collective-permute-start | bytes 1572872 | tf_op jit(solution)/shard_map/ppermute | solution.py:25
  46.2 23.6 %collective-permute-start.14 = (f32[4,2,2,32,256]{4,3,2,1,0:T(8,128)S(1)}, f32[4,2,2,32,256]{4,3,2,1,0:T(8,128)S(1)}, u32[]{:S(2)}, u32[]{:S(2)}) collective-permute-start(f32[4,2,2,32,256]{4,3,2,1,0:T(8,128)S(1)} %get-tuple-element.133.refs_4_), channel_id=1, source_target_pairs={{0,4},{4,0},{8,12},{12,8},{16,20},{20,16},{24,28},{28,24},{1,5},{5... | collective-permute-start | bytes 1572872 | tf_op jit(solution)/shard_map/ppermute | solution.py:25
  48.0 11.2 %collective-permute-start.3 = (f32[2,2,64,256]{3,2,1,0:T(8,128)S(1)}, f32[2,2,64,256]{3,2,1,0:T(8,128)S(1)}, u32[]{:S(2)}, u32[]{:S(2)}) collective-permute-start(f32[2,2,64,256]{3,2,1,0:T(8,128)S(1)} %get-tuple-element.208), channel_id=1, source_target_pairs={{0,8},{4,12},{8,0},{12,4},{16,24},{20,28},{24,16},{28,20},{1,9},{5... | collective-permute-start | bytes 786440 | tf_op jit(solution)/shard_map/ppermute | solution.py:25
  48.1 20.5 %collective-permute-start.4 = (f32[2,2,64,256]{3,2,1,0:T(8,128)S(1)}, f32[2,2,64,256]{3,2,1,0:T(8,128)S(1)}, u32[]{:S(2)}, u32[]{:S(2)}) collective-permute-start(f32[2,2,64,256]{3,2,1,0:T(8,128)S(1)} %get-tuple-element.209), channel_id=1, source_target_pairs={{0,16},{4,20},{8,24},{12,28},{16,0},{20,4},{24,8},{28,12},{1,17},{... | collective-permute-start | bytes 786440 | tf_op jit(solution)/shard_map/ppermute | solution.py:25
  51.0 17.6 %collective-permute-start.5 = (f32[2,2,64,256]{3,2,1,0:T(8,128)S(1)}, f32[2,2,64,256]{3,2,1,0:T(8,128)S(1)}, u32[]{:S(2)}, u32[]{:S(2)}) collective-permute-start(f32[2,2,64,256]{3,2,1,0:T(8,128)S(1)} %get-tuple-element.210), channel_id=1, source_target_pairs={{0,24},{4,28},{8,16},{12,20},{16,8},{20,12},{24,0},{28,4},{1,25},{... | collective-permute-start | bytes 786440 | tf_op jit(solution)/shard_map/ppermute | solution.py:25
  71.2 13.9 %collective-permute-start.11 = (f32[4,2,2,32,256]{4,3,2,1,0:T(8,128)S(1)}, f32[4,2,2,32,256]{4,3,2,1,0:T(8,128)S(1)}, u32[]{:S(2)}, u32[]{:S(2)}) collective-permute-start(f32[4,2,2,32,256]{4,3,2,1,0:T(8,128)S(1)} %get-tuple-element.145.refs_2_), channel_id=1, source_target_pairs={{0,4},{4,0},{8,12},{12,8},{16,20},{20,16},{24,28},{28,24},{1,5},{5... | collective-permute-start | bytes 1572872 | tf_op jit(solution)/shard_map/ppermute | solution.py:25
  72.6 13.6 %collective-permute-start.12 = (f32[4,2,2,32,256]{4,3,2,1,0:T(8,128)S(1)}, f32[4,2,2,32,256]{4,3,2,1,0:T(8,128)S(1)}, u32[]{:S(2)}, u32[]{:S(2)}) collective-permute-start(f32[4,2,2,32,256]{4,3,2,1,0:T(8,128)S(1)} %get-tuple-element.147.refs_4_), channel_id=1, source_target_pairs={{0,2},{1,3},{2,0},{3,1},{4,6},{5,7},{6,4},{7,5},{8,10},{9,11},{10,... | collective-permute-start | bytes 1572872 | tf_op jit(solution)/shard_map/ppermute | solution.py:25
  87.1 28.9 %collective-permute-start.19 = (f32[4,2,2,32,256]{4,3,2,1,0:T(8,128)S(1)}, f32[4,2,2,32,256]{4,3,2,1,0:T(8,128)S(1)}, u32[]{:S(2)}, u32[]{:S(2)}) collective-permute-start(f32[4,2,2,32,256]{4,3,2,1,0:T(8,128)S(1)} %get-tuple-element.157.refs_2_), channel_id=1, source_target_pairs={{0,2},{1,3},{2,0},{3,1},{4,6},{5,7},{6,4},{7,5},{8,10},{9,11},{10,... | collective-permute-start | bytes 1572872 | tf_op jit(solution)/shard_map/ppermute | solution.py:25
  87.7 28.4 %collective-permute-start.20 = (f32[4,2,2,32,256]{4,3,2,1,0:T(8,128)S(1)}, f32[4,2,2,32,256]{4,3,2,1,0:T(8,128)S(1)}, u32[]{:S(2)}, u32[]{:S(2)}) collective-permute-start(f32[4,2,2,32,256]{4,3,2,1,0:T(8,128)S(1)} %get-tuple-element.159.refs_4_), channel_id=1, source_target_pairs={{0,4},{4,0},{8,12},{12,8},{16,20},{20,16},{24,28},{28,24},{1,5},{5... | collective-permute-start | bytes 1572872 | tf_op jit(solution)/shard_map/ppermute | solution.py:25
  89.5 11.1 %collective-permute-start.2 = (f32[2,2,64,256]{3,2,1,0:T(8,128)S(1)}, f32[2,2,64,256]{3,2,1,0:T(8,128)S(1)}, u32[]{:S(2)}, u32[]{:S(2)}) collective-permute-start(f32[2,2,64,256]{3,2,1,0:T(8,128)S(1)} %get-tuple-element.203), channel_id=1, source_target_pairs={{0,24},{4,28},{8,16},{12,20},{16,8},{20,12},{24,0},{28,4},{1,25},{... | collective-permute-start | bytes 786440 | tf_op jit(solution)/shard_map/ppermute | solution.py:25
  91.7 23.2 %collective-permute-start.1 = (f32[2,2,64,256]{3,2,1,0:T(8,128)S(1)}, f32[2,2,64,256]{3,2,1,0:T(8,128)S(1)}, u32[]{:S(2)}, u32[]{:S(2)}) collective-permute-start(f32[2,2,64,256]{3,2,1,0:T(8,128)S(1)} %get-tuple-element.204), channel_id=1, source_target_pairs={{0,16},{4,20},{8,24},{12,28},{16,0},{20,4},{24,8},{28,12},{1,17},{... | collective-permute-start | bytes 786440 | tf_op jit(solution)/shard_map/ppermute | solution.py:25
  94.7 20.1 %collective-permute-start = (f32[2,2,64,256]{3,2,1,0:T(8,128)S(1)}, f32[2,2,64,256]{3,2,1,0:T(8,128)S(1)}, u32[]{:S(2)}, u32[]{:S(2)}) collective-permute-start(f32[2,2,64,256]{3,2,1,0:T(8,128)S(1)} %get-tuple-element.205), channel_id=1, source_target_pairs={{0,8},{4,12},{8,0},{12,4},{16,24},{20,28},{24,16},{28,20},{1,9},{5... | collective-permute-start | bytes 786440 | tf_op jit(solution)/shard_map/ppermute | solution.py:25
  116.9 6.2 %collective-permute-start.22 = (f32[4,2,2,32,256]{4,3,2,1,0:T(8,128)S(1)}, f32[4,2,2,32,256]{4,3,2,1,0:T(8,128)}, u32[]{:S(2)}, u32[]{:S(2)}) collective-permute-start(f32[4,2,2,32,256]{4,3,2,1,0:T(8,128)S(1)} %get-tuple-element.165.refs_4_), channel_id=1, source_target_pairs={{0,1},{1,0},{2,3},{3,2},{4,5},{5,4},{6,7},{7,6},{8,9},{9,8},{10,11... | collective-permute-start | bytes 1572872 | tf_op jit(solution)/shard_map/ppermute | solution.py:25
  117.4 13.9 %collective-permute-start.17 = (f32[4,2,2,32,256]{4,3,2,1,0:T(8,128)S(1)}, f32[4,2,2,32,256]{4,3,2,1,0:T(8,128)S(1)}, u32[]{:S(2)}, u32[]{:S(2)}) collective-permute-start(f32[4,2,2,32,256]{4,3,2,1,0:T(8,128)S(1)} %get-tuple-element.171.refs_2_), channel_id=1, source_target_pairs={{0,4},{4,0},{8,12},{12,8},{16,20},{20,16},{24,28},{28,24},{1,5},{5... | collective-permute-start | bytes 1572872 | tf_op jit(solution)/shard_map/ppermute | solution.py:25
  118.9 13.6 %collective-permute-start.18 = (f32[4,2,2,32,256]{4,3,2,1,0:T(8,128)S(1)}, f32[4,2,2,32,256]{4,3,2,1,0:T(8,128)S(1)}, u32[]{:S(2)}, u32[]{:S(2)}) collective-permute-start(f32[4,2,2,32,256]{4,3,2,1,0:T(8,128)S(1)} %get-tuple-element.173.refs_4_), channel_id=1, source_target_pairs={{0,2},{1,3},{2,0},{3,1},{4,6},{5,7},{6,4},{7,5},{8,10},{9,11},{10,... | collective-permute-start | bytes 1572872 | tf_op jit(solution)/shard_map/ppermute | solution.py:25
  120.4 23.7 %collective-permute-start.25 = (f32[2,2,64,256]{3,2,1,0:T(8,128)}, f32[2,2,64,256]{3,2,1,0:T(8,128)S(1)}, u32[]{:S(2)}, u32[]{:S(2)}) collective-permute-start(f32[2,2,64,256]{3,2,1,0:T(8,128)} %copy-done.2), channel_id=1, source_target_pairs={{0,8},{4,12},{8,0},{12,4},{16,24},{20,28},{24,16},{28,20},{1,9},{5... | collective-permute-start | bytes 786440 | tf_op jit(solution)/shard_map/ppermute | solution.py:25
  120.5 23.7 %collective-permute-start.26 = (f32[2,2,64,256]{3,2,1,0:T(8,128)}, f32[2,2,64,256]{3,2,1,0:T(8,128)S(1)}, u32[]{:S(2)}, u32[]{:S(2)}) collective-permute-start(f32[2,2,64,256]{3,2,1,0:T(8,128)} %copy-done.1), channel_id=1, source_target_pairs={{0,16},{4,20},{8,24},{12,28},{16,0},{20,4},{24,8},{28,12},{1,17},{... | collective-permute-start | bytes 786440 | tf_op jit(solution)/shard_map/ppermute | solution.py:25
  123.1 21.0 %collective-permute-start.27 = (f32[2,2,64,256]{3,2,1,0:T(8,128)}, f32[2,2,64,256]{3,2,1,0:T(8,128)S(1)}, u32[]{:S(2)}, u32[]{:S(2)}) collective-permute-start(f32[2,2,64,256]{3,2,1,0:T(8,128)} %copy-done), channel_id=1, source_target_pairs={{0,24},{4,28},{8,16},{12,20},{16,8},{20,12},{24,0},{28,4},{1,25},{... | collective-permute-start | bytes 786440 | tf_op jit(solution)/shard_map/ppermute | solution.py:25
  133.3 14.5 %collective-permute-start.23 = (f32[4,2,2,32,256]{4,3,2,1,0:T(8,128)S(1)}, f32[4,2,2,32,256]{4,3,2,1,0:T(8,128)S(1)}, u32[]{:S(2)}, u32[]{:S(2)}) collective-permute-start(f32[4,2,2,32,256]{4,3,2,1,0:T(8,128)S(1)} %get-tuple-element.181.refs_2_), channel_id=1, source_target_pairs={{0,2},{1,3},{2,0},{3,1},{4,6},{5,7},{6,4},{7,5},{8,10},{9,11},{10,... | collective-permute-start | bytes 1572872 | tf_op jit(solution)/shard_map/ppermute | solution.py:25
  134.8 12.9 %collective-permute-start.24 = (f32[4,2,2,32,256]{4,3,2,1,0:T(8,128)S(1)}, f32[4,2,2,32,256]{4,3,2,1,0:T(8,128)S(1)}, u32[]{:S(2)}, u32[]{:S(2)}) collective-permute-start(f32[4,2,2,32,256]{4,3,2,1,0:T(8,128)S(1)} %get-tuple-element.183.refs_4_), channel_id=1, source_target_pairs={{0,4},{4,0},{8,12},{12,8},{16,20},{20,16},{24,28},{28,24},{1,5},{5... | collective-permute-start | bytes 1572872 | tf_op jit(solution)/shard_map/ppermute | solution.py:25
  148.6 5.6 %collective-permute-start.28 = (f32[4,2,2,32,256]{4,3,2,1,0:T(8,128)S(1)}, f32[4,2,2,32,256]{4,3,2,1,0:T(8,128)S(1)}, u32[]{:S(2)}, u32[]{:S(2)}) collective-permute-start(f32[4,2,2,32,256]{4,3,2,1,0:T(8,128)S(1)} %get-tuple-element.187.refs_2_), channel_id=1, source_target_pairs={{0,1},{1,0},{2,3},{3,2},{4,5},{5,4},{6,7},{7,6},{8,9},{9,8},{10,11... | collective-permute-start | bytes 1572872 | tf_op jit(solution)/shard_map/ppermute | solution.py:25
  149.2 14.6 %collective-permute-start.33 = (f32[2,2,64,256]{3,2,1,0:T(8,128)S(1)}, f32[2,2,64,256]{3,2,1,0:T(8,128)S(1)}, u32[]{:S(2)}, u32[]{:S(2)}) collective-permute-start(f32[2,2,64,256]{3,2,1,0:T(8,128)S(1)} %get-tuple-element.168), channel_id=1, source_target_pairs={{0,8},{4,12},{8,0},{12,4},{16,24},{20,28},{24,16},{28,20},{1,9},{5... | collective-permute-start | bytes 786440 | tf_op jit(solution)/shard_map/ppermute | solution.py:25
  151.8 21.4 %collective-permute-start.34 = (f32[2,2,64,256]{3,2,1,0:T(8,128)S(1)}, f32[2,2,64,256]{3,2,1,0:T(8,128)S(1)}, u32[]{:S(2)}, u32[]{:S(2)}) collective-permute-start(f32[2,2,64,256]{3,2,1,0:T(8,128)S(1)} %get-tuple-element.169), channel_id=1, source_target_pairs={{0,16},{4,20},{8,24},{12,28},{16,0},{20,4},{24,8},{28,12},{1,17},{... | collective-permute-start | bytes 786440 | tf_op jit(solution)/shard_map/ppermute | solution.py:25
  152.5 20.7 %collective-permute-start.35 = (f32[2,2,64,256]{3,2,1,0:T(8,128)S(1)}, f32[2,2,64,256]{3,2,1,0:T(8,128)S(1)}, u32[]{:S(2)}, u32[]{:S(2)}) collective-permute-start(f32[2,2,64,256]{3,2,1,0:T(8,128)S(1)} %get-tuple-element.170), channel_id=1, source_target_pairs={{0,24},{4,28},{8,16},{12,20},{16,8},{20,12},{24,0},{28,4},{1,25},{... | collective-permute-start | bytes 786440 | tf_op jit(solution)/shard_map/ppermute | solution.py:25
  155.1 21.7 %collective-permute-start.31 = (f32[2,2,64,256]{3,2,1,0:T(8,128)S(1)}, f32[2,2,64,256]{3,2,1,0:T(8,128)S(1)}, u32[]{:S(2)}, u32[]{:S(2)}) collective-permute-start(f32[2,2,64,256]{3,2,1,0:T(8,128)S(1)} %get-tuple-element.193), channel_id=1, source_target_pairs={{0,8},{4,12},{8,0},{12,4},{16,24},{20,28},{24,16},{28,20},{1,9},{5... | collective-permute-start | bytes 786440 | tf_op jit(solution)/shard_map/ppermute | solution.py:25
  156.3 27.4 %collective-permute-start.32 = (f32[2,2,64,256]{3,2,1,0:T(8,128)S(1)}, f32[2,2,64,256]{3,2,1,0:T(8,128)S(1)}, u32[]{:S(2)}, u32[]{:S(2)}) collective-permute-start(f32[2,2,64,256]{3,2,1,0:T(8,128)S(1)} %get-tuple-element.194), channel_id=1, source_target_pairs={{0,24},{4,28},{8,16},{12,20},{16,8},{20,12},{24,0},{28,4},{1,25},{... | collective-permute-start | bytes 786440 | tf_op jit(solution)/shard_map/ppermute | solution.py:25
  163.8 36.4 %collective-permute-start.30 = (f32[2,2,64,256]{3,2,1,0:T(8,128)S(1)}, f32[2,2,64,256]{3,2,1,0:T(8,128)S(1)}, u32[]{:S(2)}, u32[]{:S(2)}) collective-permute-start(f32[2,2,64,256]{3,2,1,0:T(8,128)S(1)} %get-tuple-element.191), channel_id=1, source_target_pairs={{0,16},{4,20},{8,24},{12,28},{16,0},{20,4},{24,8},{28,12},{1,17},{... | collective-permute-start | bytes 786440 | tf_op jit(solution)/shard_map/ppermute | solution.py:25
  (7 other events, 142.6 us)

commit v2 on v1

--- a/solution.py
+++ b/solution.py
@@ -163,25 +163,28 @@
     )
 
 
-def transformed(plane, lanes, tables, piece_refs):
+def transformed(lanes, tables, piece_refs):
     right, left = tables[:2], tables[2:]
-    quarter, columns = piece_refs[0].shape[2:]
-    data = [jnp.concatenate([ref[0, plane], ref[1, plane]], axis=1) for ref in piece_refs]
-    mixed = dot3(halves(jnp.concatenate(data, axis=0)), [ref[...] for ref in right])
-    rows = []
-    for i in range(len(lanes)):
-        part = mixed[i * quarter : (i + 1) * quarter]
-        rows += [part[:, :columns], part[:, columns:]]
+    _, planes, quarter, columns = piece_refs[0].shape
+    data = [jnp.concatenate([ref[0, plane], ref[1, plane]], axis=1) for plane in range(planes) for ref in piece_refs]
+    high, low = halves(jnp.concatenate(data, axis=0))
+    count = high.shape[0]
+    both = jnp.dot(jnp.concatenate([high, low], axis=0), right[0][...], preferred_element_type=F32)
+    mixed = both[:count] + (both[count:] + jnp.dot(high, right[1][...], preferred_element_type=F32))
     width = 2 * quarter
     sides = [jnp.concatenate([ref[:, d * width : (d + 1) * width] for d in lanes], axis=1) for ref in left]
-    return dot3(sides, halves(jnp.concatenate(rows, axis=0)))
+    for plane in range(planes):
+        rows = []
+        for i in range(len(lanes)):
+            at = (plane * len(lanes) + i) * quarter
+            rows += [mixed[at : at + quarter, :columns], mixed[at : at + quarter, columns:]]
+        yield dot3(sides, halves(jnp.concatenate(rows, axis=0)))
 
 
 def begin_kernel(lanes, *refs):
     base_ref = refs[-1]
     local = base_ref.shape[2]
-    for plane in range(base_ref.shape[0]):
-        values = transformed(plane, lanes, refs[:4], refs[4:-1])
+    for plane, values in enumerate(transformed(lanes, refs[:4], refs[4:-1])):
         base_ref[plane, 0] = values[:local]
         base_ref[plane, 1] = values[local:]
 
@@ -203,10 +206,9 @@
 def finish_kernel(start, lanes, has_base, *refs):
     out_ref, done, sems = refs[-3:]
     count = len(lanes)
-    planes, _, local, _ = done.shape
+    local = done.shape[2]
     copies = []
-    for plane in range(planes):
-        values = transformed(plane, lanes, refs[:4], refs[4 : 4 + count])
+    for plane, values in enumerate(transformed(lanes, refs[:4], refs[4 : 4 + count])):
         for part in range(2):
             half = values[part * local : (part + 1) * local]
             done[plane, part] = half + refs[4 + count][plane, part] if has_base else half
@@ -324,7 +326,7 @@
         shape = (2, size, 1, quarter, columns)
         at = jnp.uint32(start)
         pieces = [None] * 4
-        for lanes in ((LANES[0],), (*LANES[1:], 0)) if i == 0 else ((*LANES, 0),):
+        for lanes in (LANES, (0,)) if i == 0 else ((*LANES, 0),):
             for d in lanes:
                 pieces[d] = lax.dynamic_slice(quarters, (zero, at, peers[d], zero, zero), shape)[:, :, 0]
             quarters = after(quarters, [pieces[d] for d in lanes])

time: 203 us -> 203 us (level)
  starting transfers between devices: 43.3 us -> 46.5 us
  Pallas kernels: 22.7 us -> 20.3 us
    ppermute x36, starting transfers between devices: 43.3 us -> 46.5 us  [exchanged(): return lax.ppermute(block, axis, [(i, i ^ mask) for i in range(count)])]
    pallas_call x3, Pallas kernels: 9.71 us -> 7.51 us  [finish(): pl.pallas_call(functools.partial(finish_kernel, start, lanes, base is not...]
where the time goes in v2:
time: 203 us; the launch traced here: 202 us
  waiting for transfers between devices  120 us (59%)
  starting transfers between devices  46.5 us (23%)
  Pallas kernels  20.3 us (10%)
  other arithmetic  8.73 us (4%)
  local copies, waits for them, and re-layouts  6.08 us (3%)
    ppermute x36, waiting for transfers between devices, exchanged(): return lax.ppermute(block, axis, [(i, i ^ mask) for i in range(count)])  120 us
    ppermute x36, starting transfers between devices, exchanged(): return lax.ppermute(block, axis, [(i, i ^ mask) for i in range(count)])  46.5 us
    convert_element_type x1, other arithmetic, dft_table(): return (high.astype(BF16), (values - high).astype(BF16))  8.71 us
    pallas_call x9, Pallas kernels, butterfly(): pl.pallas_call(functools.partial(butterfly_kernel, kinds, apart), in_spec...  7.59 us
    pallas_call x3, Pallas kernels, finish(): pl.pallas_call(functools.partial(finish_kernel, start, lanes, base is not...  7.51 us
    squeeze x4, local copies, waits for them, and re-layouts, shards(): lax.dynamic_slice(quarters, (zero, at, peers[d], zero, zero), shape)  4.69 us
  transfers between devices with their start and end apart: 36, of which 18 were waited for; matrix products, arithmetic and copies ran while one was open for 7% of the time, Pallas kernels for 7%

profile of v2, /device:TPU:0, one launch (start us, length us, event | category | flops | bytes accessed | tf_op | source)
XLA Modules:
  0.0 202.4 jit_solution(18031640514231184299)
XLA Ops:
  1.2 3.1 %collective-permute-start.6 = (f32[2,2,64,256]{3,2,1,0:T(8,128)S(1)}, f32[2,2,64,256]{3,2,1,0:T(8,128)S(1)}, u32[]{:S(2)}, u32[]{:S(2)}) collective-permute-start(f32[2,2,64,256]{3,2,1,0:T(8,128)S(1)} %get-tuple-element.211), channel_id=1, source_target_pairs={{0,8},{4,12},{8,0},{12,4},{16,24},{20,28},{24,16},{28,20},{1,9},{5... | collective-permute-start | bytes 786440 | tf_op jit(solution)/shard_map/ppermute | solution.py:25
  4.3 2.6 %collective-permute-start.7 = (f32[2,2,64,256]{3,2,1,0:T(8,128)S(1)}, f32[2,2,64,256]{3,2,1,0:T(8,128)S(1)}, u32[]{:S(2)}, u32[]{:S(2)}) collective-permute-start(f32[2,2,64,256]{3,2,1,0:T(8,128)S(1)} %get-tuple-element.212), channel_id=1, source_target_pairs={{0,16},{4,20},{8,24},{12,28},{16,0},{20,4},{24,8},{28,12},{1,17},{... | collective-permute-start | bytes 786440 | tf_op jit(solution)/shard_map/ppermute | solution.py:25
  8.5 6.9 %collective-permute-done.6.refs_1_ = f32[2,2,64,256]{3,2,1,0:T(8,128)S(1)} collective-permute-done((f32[2,2,64,256]{3,2,1,0:T(8,128)S(1)}, f32[2,2,64,256]{3,2,1,0:T(8,128)S(1)}, u32[]{:S(2)}, u32[]{:S(2)}) %collective-permute-start.6) | collective-permute-done | bytes 262176 | tf_op jit(solution)/shard_map/ppermute | solution.py:25
  15.5 10.1 %collective-permute-done.7.refs_2_ = f32[2,2,64,256]{3,2,1,0:T(8,128)S(1)} collective-permute-done((f32[2,2,64,256]{3,2,1,0:T(8,128)S(1)}, f32[2,2,64,256]{3,2,1,0:T(8,128)S(1)}, u32[]{:S(2)}, u32[]{:S(2)}) %collective-permute-start.7) | collective-permute-done | bytes 262176 | tf_op jit(solution)/shard_map/ppermute | solution.py:25
  26.8 1.6 collective-permute-start.9
  28.4 1.5 collective-permute-start.10
  30.5 7.6 %collective-permute-done.9.refs_3_ = f32[4,2,2,32,256]{4,3,2,1,0:T(8,128)S(1)} collective-permute-done((f32[4,2,2,32,256]{4,3,2,1,0:T(8,128)S(1)}, f32[4,2,2,32,256]{4,3,2,1,0:T(8,128)S(1)}, u32[]{:S(2)}, u32[]{:S(2)}) %collective-permute-start.9) | collective-permute-done | bytes 524320 | tf_op jit(solution)/shard_map/ppermute | solution.py:25
  40.4 1.6 collective-permute-start.13
  43.7 6.0 %collective-permute-start.3 = (f32[2,2,64,256]{3,2,1,0:T(8,128)S(1)}, f32[2,2,64,256]{3,2,1,0:T(8,128)S(1)}, u32[]{:S(2)}, u32[]{:S(2)}) collective-permute-start(f32[2,2,64,256]{3,2,1,0:T(8,128)S(1)} %get-tuple-element.208), channel_id=1, source_target_pairs={{0,8},{4,12},{8,0},{12,4},{16,24},{20,28},{24,16},{28,20},{1,9},{5... | collective-permute-start | bytes 786440 | tf_op jit(solution)/shard_map/ppermute | solution.py:25
  52.1 4.6 %collective-permute-done.3.refs_1_ = f32[2,2,64,256]{3,2,1,0:T(8,128)S(1)} collective-permute-done((f32[2,2,64,256]{3,2,1,0:T(8,128)S(1)}, f32[2,2,64,256]{3,2,1,0:T(8,128)S(1)}, u32[]{:S(2)}, u32[]{:S(2)}) %collective-permute-start.3) | collective-permute-done | bytes 262176 | tf_op jit(solution)/shard_map/ppermute | solution.py:25
  56.7 13.0 %collective-permute-done.4.refs_2_ = f32[2,2,64,256]{3,2,1,0:T(8,128)S(1)} collective-permute-done((f32[2,2,64,256]{3,2,1,0:T(8,128)S(1)}, f32[2,2,64,256]{3,2,1,0:T(8,128)S(1)}, u32[]{:S(2)}, u32[]{:S(2)}) %collective-permute-start.4) | collective-permute-done | bytes 262176 | tf_op jit(solution)/shard_map/ppermute | solution.py:25
  75.2 11.0 %collective-permute-done.11.refs_3_ = f32[4,2,2,32,256]{4,3,2,1,0:T(8,128)S(1)} collective-permute-done((f32[4,2,2,32,256]{4,3,2,1,0:T(8,128)S(1)}, f32[4,2,2,32,256]{4,3,2,1,0:T(8,128)S(1)}, u32[]{:S(2)}, u32[]{:S(2)}) %collective-permute-start.11) | collective-permute-done | bytes 524320 | tf_op jit(solution)/shard_map/ppermute | solution.py:25
  90.6 2.0 collective-permute-start.2
  92.6 2.9 %collective-permute-start.1 = (f32[2,2,64,256]{3,2,1,0:T(8,128)S(1)}, f32[2,2,64,256]{3,2,1,0:T(8,128)S(1)}, u32[]{:S(2)}, u32[]{:S(2)}) collective-permute-start(f32[2,2,64,256]{3,2,1,0:T(8,128)S(1)} %get-tuple-element.204), channel_id=1, source_target_pairs={{0,16},{4,20},{8,24},{12,28},{16,0},{20,4},{24,8},{28,12},{1,17},{... | collective-permute-start | bytes 786440 | tf_op jit(solution)/shard_map/ppermute | solution.py:25
  95.6 6.0 %collective-permute-done.2.refs_3_ = f32[2,2,64,256]{3,2,1,0:T(8,128)S(1)} collective-permute-done((f32[2,2,64,256]{3,2,1,0:T(8,128)S(1)}, f32[2,2,64,256]{3,2,1,0:T(8,128)S(1)}, u32[]{:S(2)}, u32[]{:S(2)}) %collective-permute-start.2) | collective-permute-done | bytes 262176 | tf_op jit(solution)/shard_map/ppermute | solution.py:25
  101.6 14.3 %collective-permute-done.1.refs_2_ = f32[2,2,64,256]{3,2,1,0:T(8,128)S(1)} collective-permute-done((f32[2,2,64,256]{3,2,1,0:T(8,128)S(1)}, f32[2,2,64,256]{3,2,1,0:T(8,128)S(1)}, u32[]{:S(2)}, u32[]{:S(2)}) %collective-permute-start.1) | collective-permute-done | bytes 262176 | tf_op jit(solution)/shard_map/ppermute | solution.py:25
  121.6 2.5 %collective-permute-start.26 = (f32[2,2,64,256]{3,2,1,0:T(8,128)}, f32[2,2,64,256]{3,2,1,0:T(8,128)S(1)}, u32[]{:S(2)}, u32[]{:S(2)}) collective-permute-start(f32[2,2,64,256]{3,2,1,0:T(8,128)} %copy-done.1), channel_id=1, source_target_pairs={{0,16},{4,20},{8,24},{12,28},{16,0},{20,4},{24,8},{28,12},{1,17},{... | collective-permute-start | bytes 786440 | tf_op jit(solution)/shard_map/ppermute | solution.py:25
  124.1 1.9 collective-permute-start.27
  127.4 5.0 %collective-permute-done.17.refs_3_ = f32[4,2,2,32,256]{4,3,2,1,0:T(8,128)S(1)} collective-permute-done((f32[4,2,2,32,256]{4,3,2,1,0:T(8,128)S(1)}, f32[4,2,2,32,256]{4,3,2,1,0:T(8,128)S(1)}, u32[]{:S(2)}, u32[]{:S(2)}) %collective-permute-start.17) | collective-permute-done | bytes 524320 | tf_op jit(solution)/shard_map/ppermute | solution.py:25
  134.4 1.6 collective-permute-start.23
  136.5 8.7 %fusion.1 = (bf16[512,512]{1,0:T(8,128)(2,1)S(1)}, bf16[512,512]{1,0:T(8,128)(2,1)S(1)}, bf16[512,512]{1,0:T(8,128)(2,1)S(1)}, bf16[512,512]{1,0:T(8,128)(2,1)S(1)}) fusion(s32[512]{0:T(512)S(1)} %get-tuple-element.221, s32[512]{0:T(512)S(1)} %get-tuple-element.220, s32[512]{0:T(512)S(1)} %get-tuple-element.224, s32[512]{0:T(512)S(1)} %get-tuple-element.223, ...), kind=kLoop, calls=%fused_computation.11 | loop fusion | flops 11534336 | bytes 2109440 | tf_op jit(solution)/shard_map/convert_element_type | solution.py:46
  145.2 2.8 %finish.3.refs_8_ = f32[2,6,256,256]{3,2,1,0:T(8,128)} custom-call(bf16[512,512]{1,0:T(8,128)(2,1)S(1)} %get-tuple-element.218.refs_0_, bf16[512,512]{1,0:T(8,128)(2,1)S(1)} %get-tuple-element.219.refs_1_, bf16[512,512]{1,0:T(8,128)(2,1)S(1)} %get-tuple-element.215.refs_2_, bf16[512,512]{1,0:T(8,128)(2,1)S(1)} %get-tuple-element.214.refs_3_, ...), custom_call_target="tpu_custom_call" | custom-call | flops 1610612736 | bytes 2097152 | tf_op jit(solution)/shard_map/finish/pallas_call | solution.py:231
  149.8 2.3 %collective-permute-start.33 = (f32[2,2,64,256]{3,2,1,0:T(8,128)S(1)}, f32[2,2,64,256]{3,2,1,0:T(8,128)S(1)}, u32[]{:S(2)}, u32[]{:S(2)}) collective-permute-start(f32[2,2,64,256]{3,2,1,0:T(8,128)S(1)} %get-tuple-element.168), channel_id=1, source_target_pairs={{0,8},{4,12},{8,0},{12,4},{16,24},{20,28},{24,16},{28,20},{1,9},{5... | collective-permute-start | bytes 786440 | tf_op jit(solution)/shard_map/ppermute | solution.py:25
  152.6 1.9 collective-permute-start.35
  156.5 1.9 collective-permute-start.32
  158.4 5.6 %collective-permute-done.33.refs_5_ = f32[2,2,64,256]{3,2,1,0:T(8,128)S(1)} collective-permute-done((f32[2,2,64,256]{3,2,1,0:T(8,128)S(1)}, f32[2,2,64,256]{3,2,1,0:T(8,128)S(1)}, u32[]{:S(2)}, u32[]{:S(2)}) %collective-permute-start.33) | collective-permute-done | bytes 262176 | tf_op jit(solution)/shard_map/ppermute | solution.py:25
  164.0 9.5 %collective-permute-done.34.refs_6_ = f32[2,2,64,256]{3,2,1,0:T(8,128)S(1)} collective-permute-done((f32[2,2,64,256]{3,2,1,0:T(8,128)S(1)}, f32[2,2,64,256]{3,2,1,0:T(8,128)S(1)}, u32[]{:S(2)}, u32[]{:S(2)}) %collective-permute-start.34) | collective-permute-done | bytes 262176 | tf_op jit(solution)/shard_map/ppermute | solution.py:25
  173.5 2.8 %finish.4.refs_6_ = f32[2,6,256,256]{3,2,1,0:T(8,128)} custom-call(bf16[512,512]{1,0:T(8,128)(2,1)S(1)} %get-tuple-element.218.refs_0_, bf16[512,512]{1,0:T(8,128)(2,1)S(1)} %get-tuple-element.219.refs_1_, bf16[512,512]{1,0:T(8,128)(2,1)S(1)} %get-tuple-element.215.refs_2_, ...), custom_call_target="tpu_custom_call", output_to_operand_aliasing={{}: (8, {})} | custom-call | flops 1610612736 | bytes 2097152 | tf_op jit(solution)/shard_map/finish/pallas_call | solution.py:231
  176.3 7.6 %collective-permute-done.32.refs_6_ = f32[2,2,64,256]{3,2,1,0:T(8,128)S(1)} collective-permute-done((f32[2,2,64,256]{3,2,1,0:T(8,128)S(1)}, f32[2,2,64,256]{3,2,1,0:T(8,128)S(1)}, u32[]{:S(2)}, u32[]{:S(2)}) %collective-permute-start.32) | collective-permute-done | bytes 262176 | tf_op jit(solution)/shard_map/ppermute | solution.py:25
  183.9 1.7 begin.1.refs_5_
  185.6 14.9 %collective-permute-done.30.refs_4_ = f32[2,2,64,256]{3,2,1,0:T(8,128)S(1)} collective-permute-done((f32[2,2,64,256]{3,2,1,0:T(8,128)S(1)}, f32[2,2,64,256]{3,2,1,0:T(8,128)S(1)}, u32[]{:S(2)}, u32[]{:S(2)}) %collective-permute-start.30) | collective-permute-done | bytes 262176 | tf_op jit(solution)/shard_map/ppermute | solution.py:25
  200.5 1.9 finish.5
  (72 shorter events, 34.8 us)
Async XLA Ops:
  1.2 14.3 %collective-permute-start.6 = (f32[2,2,64,256]{3,2,1,0:T(8,128)S(1)}, f32[2,2,64,256]{3,2,1,0:T(8,128)S(1)}, u32[]{:S(2)}, u32[]{:S(2)}) collective-permute-start(f32[2,2,64,256]{3,2,1,0:T(8,128)S(1)} %get-tuple-element.211), channel_id=1, source_target_pairs={{0,8},{4,12},{8,0},{12,4},{16,24},{20,28},{24,16},{28,20},{1,9},{5... | collective-permute-start | bytes 786440 | tf_op jit(solution)/shard_map/ppermute | solution.py:25
  4.3 21.3 %collective-permute-start.7 = (f32[2,2,64,256]{3,2,1,0:T(8,128)S(1)}, f32[2,2,64,256]{3,2,1,0:T(8,128)S(1)}, u32[]{:S(2)}, u32[]{:S(2)}) collective-permute-start(f32[2,2,64,256]{3,2,1,0:T(8,128)S(1)} %get-tuple-element.212), channel_id=1, source_target_pairs={{0,16},{4,20},{8,24},{12,28},{16,0},{20,4},{24,8},{28,12},{1,17},{... | collective-permute-start | bytes 786440 | tf_op jit(solution)/shard_map/ppermute | solution.py:25
  6.9 18.7 %collective-permute-start.8 = (f32[2,2,64,256]{3,2,1,0:T(8,128)S(1)}, f32[2,2,64,256]{3,2,1,0:T(8,128)S(1)}, u32[]{:S(2)}, u32[]{:S(2)}) collective-permute-start(f32[2,2,64,256]{3,2,1,0:T(8,128)S(1)} %get-tuple-element.213), channel_id=1, source_target_pairs={{0,24},{4,28},{8,16},{12,20},{16,8},{20,12},{24,0},{28,4},{1,25},{... | collective-permute-start | bytes 786440 | tf_op jit(solution)/shard_map/ppermute | solution.py:25
  26.8 11.3 %collective-permute-start.9 = (f32[4,2,2,32,256]{4,3,2,1,0:T(8,128)S(1)}, f32[4,2,2,32,256]{4,3,2,1,0:T(8,128)S(1)}, u32[]{:S(2)}, u32[]{:S(2)}) collective-permute-start(f32[4,2,2,32,256]{4,3,2,1,0:T(8,128)S(1)} %get-tuple-element.119.refs_2_), channel_id=1, source_target_pairs={{0,4},{4,0},{8,12},{12,8},{16,20},{20,16},{24,28},{28,24},{1,5},{5... | collective-permute-start | bytes 1572872 | tf_op jit(solution)/shard_map/ppermute | solution.py:25
  28.4 11.2 %collective-permute-start.10 = (f32[4,2,2,32,256]{4,3,2,1,0:T(8,128)S(1)}, f32[4,2,2,32,256]{4,3,2,1,0:T(8,128)S(1)}, u32[]{:S(2)}, u32[]{:S(2)}) collective-permute-start(f32[4,2,2,32,256]{4,3,2,1,0:T(8,128)S(1)} %get-tuple-element.121.refs_4_), channel_id=1, source_target_pairs={{0,2},{1,3},{2,0},{3,1},{4,6},{5,7},{6,4},{7,5},{8,10},{9,11},{10,... | collective-permute-start | bytes 1572872 | tf_op jit(solution)/shard_map/ppermute | solution.py:25
  40.4 30.5 %collective-permute-start.13 = (f32[4,2,2,32,256]{4,3,2,1,0:T(8,128)S(1)}, f32[4,2,2,32,256]{4,3,2,1,0:T(8,128)S(1)}, u32[]{:S(2)}, u32[]{:S(2)}) collective-permute-start(f32[4,2,2,32,256]{4,3,2,1,0:T(8,128)S(1)} %get-tuple-element.131.refs_2_), channel_id=1, source_target_pairs={{0,2},{1,3},{2,0},{3,1},{4,6},{5,7},{6,4},{7,5},{8,10},{9,11},{10,... | collective-permute-start | bytes 1572872 | tf_op jit(solution)/shard_map/ppermute | solution.py:25
  41.9 29.0 %collective-permute-start.14 = (f32[4,2,2,32,256]{4,3,2,1,0:T(8,128)S(1)}, f32[4,2,2,32,256]{4,3,2,1,0:T(8,128)S(1)}, u32[]{:S(2)}, u32[]{:S(2)}) collective-permute-start(f32[4,2,2,32,256]{4,3,2,1,0:T(8,128)S(1)} %get-tuple-element.133.refs_4_), channel_id=1, source_target_pairs={{0,4},{4,0},{8,12},{12,8},{16,20},{20,16},{24,28},{28,24},{1,5},{5... | collective-permute-start | bytes 1572872 | tf_op jit(solution)/shard_map/ppermute | solution.py:25
  43.7 13.0 %collective-permute-start.3 = (f32[2,2,64,256]{3,2,1,0:T(8,128)S(1)}, f32[2,2,64,256]{3,2,1,0:T(8,128)S(1)}, u32[]{:S(2)}, u32[]{:S(2)}) collective-permute-start(f32[2,2,64,256]{3,2,1,0:T(8,128)S(1)} %get-tuple-element.208), channel_id=1, source_target_pairs={{0,8},{4,12},{8,0},{12,4},{16,24},{20,28},{24,16},{28,20},{1,9},{5... | collective-permute-start | bytes 786440 | tf_op jit(solution)/shard_map/ppermute | solution.py:25
  49.7 20.0 %collective-permute-start.4 = (f32[2,2,64,256]{3,2,1,0:T(8,128)S(1)}, f32[2,2,64,256]{3,2,1,0:T(8,128)S(1)}, u32[]{:S(2)}, u32[]{:S(2)}) collective-permute-start(f32[2,2,64,256]{3,2,1,0:T(8,128)S(1)} %get-tuple-element.209), channel_id=1, source_target_pairs={{0,16},{4,20},{8,24},{12,28},{16,0},{20,4},{24,8},{28,12},{1,17},{... | collective-permute-start | bytes 786440 | tf_op jit(solution)/shard_map/ppermute | solution.py:25
  50.8 18.9 %collective-permute-start.5 = (f32[2,2,64,256]{3,2,1,0:T(8,128)S(1)}, f32[2,2,64,256]{3,2,1,0:T(8,128)S(1)}, u32[]{:S(2)}, u32[]{:S(2)}) collective-permute-start(f32[2,2,64,256]{3,2,1,0:T(8,128)S(1)} %get-tuple-element.210), channel_id=1, source_target_pairs={{0,24},{4,28},{8,16},{12,20},{16,8},{20,12},{24,0},{28,4},{1,25},{... | collective-permute-start | bytes 786440 | tf_op jit(solution)/shard_map/ppermute | solution.py:25
  72.3 13.9 %collective-permute-start.11 = (f32[4,2,2,32,256]{4,3,2,1,0:T(8,128)S(1)}, f32[4,2,2,32,256]{4,3,2,1,0:T(8,128)S(1)}, u32[]{:S(2)}, u32[]{:S(2)}) collective-permute-start(f32[4,2,2,32,256]{4,3,2,1,0:T(8,128)S(1)} %get-tuple-element.145.refs_2_), channel_id=1, source_target_pairs={{0,4},{4,0},{8,12},{12,8},{16,20},{20,16},{24,28},{28,24},{1,5},{5... | collective-permute-start | bytes 1572872 | tf_op jit(solution)/shard_map/ppermute | solution.py:25
  73.7 13.6 %collective-permute-start.12 = (f32[4,2,2,32,256]{4,3,2,1,0:T(8,128)S(1)}, f32[4,2,2,32,256]{4,3,2,1,0:T(8,128)S(1)}, u32[]{:S(2)}, u32[]{:S(2)}) collective-permute-start(f32[4,2,2,32,256]{4,3,2,1,0:T(8,128)S(1)} %get-tuple-element.147.refs_4_), channel_id=1, source_target_pairs={{0,2},{1,3},{2,0},{3,1},{4,6},{5,7},{6,4},{7,5},{8,10},{9,11},{10,... | collective-permute-start | bytes 1572872 | tf_op jit(solution)/shard_map/ppermute | solution.py:25
  88.1 28.9 %collective-permute-start.19 = (f32[4,2,2,32,256]{4,3,2,1,0:T(8,128)S(1)}, f32[4,2,2,32,256]{4,3,2,1,0:T(8,128)S(1)}, u32[]{:S(2)}, u32[]{:S(2)}) collective-permute-start(f32[4,2,2,32,256]{4,3,2,1,0:T(8,128)S(1)} %get-tuple-element.157.refs_2_), channel_id=1, source_target_pairs={{0,2},{1,3},{2,0},{3,1},{4,6},{5,7},{6,4},{7,5},{8,10},{9,11},{10,... | collective-permute-start | bytes 1572872 | tf_op jit(solution)/shard_map/ppermute | solution.py:25
  88.7 28.4 %collective-permute-start.20 = (f32[4,2,2,32,256]{4,3,2,1,0:T(8,128)S(1)}, f32[4,2,2,32,256]{4,3,2,1,0:T(8,128)S(1)}, u32[]{:S(2)}, u32[]{:S(2)}) collective-permute-start(f32[4,2,2,32,256]{4,3,2,1,0:T(8,128)S(1)} %get-tuple-element.159.refs_4_), channel_id=1, source_target_pairs={{0,4},{4,0},{8,12},{12,8},{16,20},{20,16},{24,28},{28,24},{1,5},{5... | collective-permute-start | bytes 1572872 | tf_op jit(solution)/shard_map/ppermute | solution.py:25
  90.6 11.0 %collective-permute-start.2 = (f32[2,2,64,256]{3,2,1,0:T(8,128)S(1)}, f32[2,2,64,256]{3,2,1,0:T(8,128)S(1)}, u32[]{:S(2)}, u32[]{:S(2)}) collective-permute-start(f32[2,2,64,256]{3,2,1,0:T(8,128)S(1)} %get-tuple-element.203), channel_id=1, source_target_pairs={{0,24},{4,28},{8,16},{12,20},{16,8},{20,12},{24,0},{28,4},{1,25},{... | collective-permute-start | bytes 786440 | tf_op jit(solution)/shard_map/ppermute | solution.py:25
  92.6 23.3 %collective-permute-start.1 = (f32[2,2,64,256]{3,2,1,0:T(8,128)S(1)}, f32[2,2,64,256]{3,2,1,0:T(8,128)S(1)}, u32[]{:S(2)}, u32[]{:S(2)}) collective-permute-start(f32[2,2,64,256]{3,2,1,0:T(8,128)S(1)} %get-tuple-element.204), channel_id=1, source_target_pairs={{0,16},{4,20},{8,24},{12,28},{16,0},{20,4},{24,8},{28,12},{1,17},{... | collective-permute-start | bytes 786440 | tf_op jit(solution)/shard_map/ppermute | solution.py:25
  95.5 20.4 %collective-permute-start = (f32[2,2,64,256]{3,2,1,0:T(8,128)S(1)}, f32[2,2,64,256]{3,2,1,0:T(8,128)S(1)}, u32[]{:S(2)}, u32[]{:S(2)}) collective-permute-start(f32[2,2,64,256]{3,2,1,0:T(8,128)S(1)} %get-tuple-element.205), channel_id=1, source_target_pairs={{0,8},{4,12},{8,0},{12,4},{16,24},{20,28},{24,16},{28,20},{1,9},{5... | collective-permute-start | bytes 786440 | tf_op jit(solution)/shard_map/ppermute | solution.py:25
  118.0 6.1 %collective-permute-start.22 = (f32[4,2,2,32,256]{4,3,2,1,0:T(8,128)S(1)}, f32[4,2,2,32,256]{4,3,2,1,0:T(8,128)}, u32[]{:S(2)}, u32[]{:S(2)}) collective-permute-start(f32[4,2,2,32,256]{4,3,2,1,0:T(8,128)S(1)} %get-tuple-element.165.refs_4_), channel_id=1, source_target_pairs={{0,1},{1,0},{2,3},{3,2},{4,5},{5,4},{6,7},{7,6},{8,9},{9,8},{10,11... | collective-permute-start | bytes 1572872 | tf_op jit(solution)/shard_map/ppermute | solution.py:25
  118.5 13.9 %collective-permute-start.17 = (f32[4,2,2,32,256]{4,3,2,1,0:T(8,128)S(1)}, f32[4,2,2,32,256]{4,3,2,1,0:T(8,128)S(1)}, u32[]{:S(2)}, u32[]{:S(2)}) collective-permute-start(f32[4,2,2,32,256]{4,3,2,1,0:T(8,128)S(1)} %get-tuple-element.171.refs_2_), channel_id=1, source_target_pairs={{0,4},{4,0},{8,12},{12,8},{16,20},{20,16},{24,28},{28,24},{1,5},{5... | collective-permute-start | bytes 1572872 | tf_op jit(solution)/shard_map/ppermute | solution.py:25
  120.0 13.6 %collective-permute-start.18 = (f32[4,2,2,32,256]{4,3,2,1,0:T(8,128)S(1)}, f32[4,2,2,32,256]{4,3,2,1,0:T(8,128)S(1)}, u32[]{:S(2)}, u32[]{:S(2)}) collective-permute-start(f32[4,2,2,32,256]{4,3,2,1,0:T(8,128)S(1)} %get-tuple-element.173.refs_4_), channel_id=1, source_target_pairs={{0,2},{1,3},{2,0},{3,1},{4,6},{5,7},{6,4},{7,5},{8,10},{9,11},{10,... | collective-permute-start | bytes 1572872 | tf_op jit(solution)/shard_map/ppermute | solution.py:25
  121.5 23.7 %collective-permute-start.25 = (f32[2,2,64,256]{3,2,1,0:T(8,128)}, f32[2,2,64,256]{3,2,1,0:T(8,128)S(1)}, u32[]{:S(2)}, u32[]{:S(2)}) collective-permute-start(f32[2,2,64,256]{3,2,1,0:T(8,128)} %copy-done.2), channel_id=1, source_target_pairs={{0,8},{4,12},{8,0},{12,4},{16,24},{20,28},{24,16},{28,20},{1,9},{5... | collective-permute-start | bytes 786440 | tf_op jit(solution)/shard_map/ppermute | solution.py:25
  121.6 23.7 %collective-permute-start.26 = (f32[2,2,64,256]{3,2,1,0:T(8,128)}, f32[2,2,64,256]{3,2,1,0:T(8,128)S(1)}, u32[]{:S(2)}, u32[]{:S(2)}) collective-permute-start(f32[2,2,64,256]{3,2,1,0:T(8,128)} %copy-done.1), channel_id=1, source_target_pairs={{0,16},{4,20},{8,24},{12,28},{16,0},{20,4},{24,8},{28,12},{1,17},{... | collective-permute-start | bytes 786440 | tf_op jit(solution)/shard_map/ppermute | solution.py:25
  124.1 21.2 %collective-permute-start.27 = (f32[2,2,64,256]{3,2,1,0:T(8,128)}, f32[2,2,64,256]{3,2,1,0:T(8,128)S(1)}, u32[]{:S(2)}, u32[]{:S(2)}) collective-permute-start(f32[2,2,64,256]{3,2,1,0:T(8,128)} %copy-done), channel_id=1, source_target_pairs={{0,24},{4,28},{8,16},{12,20},{16,8},{20,12},{24,0},{28,4},{1,25},{... | collective-permute-start | bytes 786440 | tf_op jit(solution)/shard_map/ppermute | solution.py:25
  134.4 13.7 %collective-permute-start.23 = (f32[4,2,2,32,256]{4,3,2,1,0:T(8,128)S(1)}, f32[4,2,2,32,256]{4,3,2,1,0:T(8,128)S(1)}, u32[]{:S(2)}, u32[]{:S(2)}) collective-permute-start(f32[4,2,2,32,256]{4,3,2,1,0:T(8,128)S(1)} %get-tuple-element.181.refs_2_), channel_id=1, source_target_pairs={{0,2},{1,3},{2,0},{3,1},{4,6},{5,7},{6,4},{7,5},{8,10},{9,11},{10,... | collective-permute-start | bytes 1572872 | tf_op jit(solution)/shard_map/ppermute | solution.py:25
  135.9 12.5 %collective-permute-start.24 = (f32[4,2,2,32,256]{4,3,2,1,0:T(8,128)S(1)}, f32[4,2,2,32,256]{4,3,2,1,0:T(8,128)S(1)}, u32[]{:S(2)}, u32[]{:S(2)}) collective-permute-start(f32[4,2,2,32,256]{4,3,2,1,0:T(8,128)S(1)} %get-tuple-element.183.refs_4_), channel_id=1, source_target_pairs={{0,4},{4,0},{8,12},{12,8},{16,20},{20,16},{24,28},{28,24},{1,5},{5... | collective-permute-start | bytes 1572872 | tf_op jit(solution)/shard_map/ppermute | solution.py:25
  149.2 5.3 %collective-permute-start.28 = (f32[4,2,2,32,256]{4,3,2,1,0:T(8,128)S(1)}, f32[4,2,2,32,256]{4,3,2,1,0:T(8,128)S(1)}, u32[]{:S(2)}, u32[]{:S(2)}) collective-permute-start(f32[4,2,2,32,256]{4,3,2,1,0:T(8,128)S(1)} %get-tuple-element.187.refs_2_), channel_id=1, source_target_pairs={{0,1},{1,0},{2,3},{3,2},{4,5},{5,4},{6,7},{7,6},{8,9},{9,8},{10,11... | collective-permute-start | bytes 1572872 | tf_op jit(solution)/shard_map/ppermute | solution.py:25
  149.8 14.2 %collective-permute-start.33 = (f32[2,2,64,256]{3,2,1,0:T(8,128)S(1)}, f32[2,2,64,256]{3,2,1,0:T(8,128)S(1)}, u32[]{:S(2)}, u32[]{:S(2)}) collective-permute-start(f32[2,2,64,256]{3,2,1,0:T(8,128)S(1)} %get-tuple-element.168), channel_id=1, source_target_pairs={{0,8},{4,12},{8,0},{12,4},{16,24},{20,28},{24,16},{28,20},{1,9},{5... | collective-permute-start | bytes 786440 | tf_op jit(solution)/shard_map/ppermute | solution.py:25
  152.1 21.4 %collective-permute-start.34 = (f32[2,2,64,256]{3,2,1,0:T(8,128)S(1)}, f32[2,2,64,256]{3,2,1,0:T(8,128)S(1)}, u32[]{:S(2)}, u32[]{:S(2)}) collective-permute-start(f32[2,2,64,256]{3,2,1,0:T(8,128)S(1)} %get-tuple-element.169), channel_id=1, source_target_pairs={{0,16},{4,20},{8,24},{12,28},{16,0},{20,4},{24,8},{28,12},{1,17},{... | collective-permute-start | bytes 786440 | tf_op jit(solution)/shard_map/ppermute | solution.py:25
  152.6 20.9 %collective-permute-start.35 = (f32[2,2,64,256]{3,2,1,0:T(8,128)S(1)}, f32[2,2,64,256]{3,2,1,0:T(8,128)S(1)}, u32[]{:S(2)}, u32[]{:S(2)}) collective-permute-start(f32[2,2,64,256]{3,2,1,0:T(8,128)S(1)} %get-tuple-element.170), channel_id=1, source_target_pairs={{0,24},{4,28},{8,16},{12,20},{16,8},{20,12},{24,0},{28,4},{1,25},{... | collective-permute-start | bytes 786440 | tf_op jit(solution)/shard_map/ppermute | solution.py:25
  155.3 21.0 %collective-permute-start.31 = (f32[2,2,64,256]{3,2,1,0:T(8,128)S(1)}, f32[2,2,64,256]{3,2,1,0:T(8,128)S(1)}, u32[]{:S(2)}, u32[]{:S(2)}) collective-permute-start(f32[2,2,64,256]{3,2,1,0:T(8,128)S(1)} %get-tuple-element.193), channel_id=1, source_target_pairs={{0,8},{4,12},{8,0},{12,4},{16,24},{20,28},{24,16},{28,20},{1,9},{5... | collective-permute-start | bytes 786440 | tf_op jit(solution)/shard_map/ppermute | solution.py:25
  156.5 27.4 %collective-permute-start.32 = (f32[2,2,64,256]{3,2,1,0:T(8,128)S(1)}, f32[2,2,64,256]{3,2,1,0:T(8,128)S(1)}, u32[]{:S(2)}, u32[]{:S(2)}) collective-permute-start(f32[2,2,64,256]{3,2,1,0:T(8,128)S(1)} %get-tuple-element.194), channel_id=1, source_target_pairs={{0,24},{4,28},{8,16},{12,20},{16,8},{20,12},{24,0},{28,4},{1,25},{... | collective-permute-start | bytes 786440 | tf_op jit(solution)/shard_map/ppermute | solution.py:25
  164.0 36.4 %collective-permute-start.30 = (f32[2,2,64,256]{3,2,1,0:T(8,128)S(1)}, f32[2,2,64,256]{3,2,1,0:T(8,128)S(1)}, u32[]{:S(2)}, u32[]{:S(2)}) collective-permute-start(f32[2,2,64,256]{3,2,1,0:T(8,128)S(1)} %get-tuple-element.191), channel_id=1, source_target_pairs={{0,16},{4,20},{8,24},{12,28},{16,0},{20,4},{24,8},{28,12},{1,17},{... | collective-permute-start | bytes 786440 | tf_op jit(solution)/shard_map/ppermute | solution.py:25
  (7 other events, 142.2 us)

commit v3 on v2

--- a/solution.py
+++ b/solution.py
@@ -82,6 +82,36 @@
         return carry
 
     lax.fori_loop(0, planes * (rows // step), one, 0, unroll=4)
+
+
+def pack_kernel(stride, x_ref, *refs):
+    outs, sems = refs[:-1], refs[-1]
+    _, planes, quarter, _ = outs[0].shape
+    part = lax.axis_index("gz") // stride
+    copies = []
+    for d in (*LANES, 0):
+        rows = pl.ds(pl.multiple_of((part ^ d) * quarter, quarter), quarter)
+        copies.append(pltpu.make_async_copy(x_ref.at[:, pl.ds(0, planes), rows, :], outs[d], sems.at[d]))
+        copies[-1].start()
+    for copy in copies:
+        copy.wait()
+
+
+def pack(x, stride, planes):
+    _, _, rows, columns = x.shape
+    piece = jax.ShapeDtypeStruct((2, planes, rows // 4, columns), F32)
+    return list(
+        pl.pallas_call(
+            functools.partial(pack_kernel, stride),
+            in_specs=[ANY],
+            out_specs=[VMEM] * 4,
+            out_shape=[pltpu.VMEM(piece.shape, F32)] * 4,
+            scratch_shapes=[pltpu.SemaphoreType.DMA((4,))],
+            compiler_params=pltpu.CompilerParams(vmem_limit_bytes=GRANT),
+            cost_estimate=estimate(0, 4 * planes * rows * columns),
+            name="pack",
+        )(pltpu.with_memory_space_constraint(x, pltpu.HBM))
+    )
 
 
 def mix_kernel(coef_ref, *refs):
@@ -325,11 +355,11 @@
     for i, (start, size) in enumerate(chunks):
         shape = (2, size, 1, quarter, columns)
         at = jnp.uint32(start)
-        pieces = [None] * 4
-        for lanes in (LANES, (0,)) if i == 0 else ((*LANES, 0),):
-            for d in lanes:
-                pieces[d] = lax.dynamic_slice(quarters, (zero, at, peers[d], zero, zero), shape)[:, :, 0]
-            quarters = after(quarters, [pieces[d] for d in lanes])
+        if i == 0:
+            pieces = pack(velocity, stride, size)
+        else:
+            pieces = [lax.dynamic_slice(quarters, (zero, at, peer, zero, zero), shape)[:, :, 0] for peer in peers]
+        quarters = after(quarters, pieces)
         received.append(pieces[:1] + [exchanged(pieces[d], "gz", d * stride) for d in range(1, 4)])
 
     z_steps, y_steps = list(reversed(range(z_bits - 2))), list(reversed(range(y_bits)))

time: 203 us -> 196 us (0.966)
  local copies, waits for them, and re-layouts: 6.08 us -> 1.57 us
    squeeze x4 -> x2, local copies, waits for them, and re-layouts: 4.69 us -> 0.18 us  [shards(): lax.dynamic_slice(quarters, (zero, at, peer, zero, zero), shape)[:, :, 0]]
  transfers between devices with their start and end apart: 36 -> 36, of which waited for: 18 -> 18; matrix products, arithmetic and copies ran while one was open for 7% -> 5% of each run, Pallas kernels for 7% -> 7%
where the time goes in v3:
time: 196 us
  waiting for transfers between devices  119 us (61%)
  starting transfers between devices  44.5 us (23%)
  Pallas kernels  21.7 us (11%)
  other arithmetic  8.73 us (4%)
    ppermute x36, waiting for transfers between devices, exchanged(): return lax.ppermute(block, axis, [(i, i ^ mask) for i in range(count)])  119 us
    ppermute x36, starting transfers between devices, exchanged(): return lax.ppermute(block, axis, [(i, i ^ mask) for i in range(count)])  44.5 us
    convert_element_type x1, other arithmetic, dft_table(): return (high.astype(BF16), (values - high).astype(BF16))  8.71 us
    pallas_call x9, Pallas kernels, butterfly(): pl.pallas_call(functools.partial(butterfly_kernel, kinds, apart), in_spec...  7.59 us
    pallas_call x3, Pallas kernels, finish(): pl.pallas_call(functools.partial(finish_kernel, start, lanes, base is not...  7.49 us
  transfers between devices with their start and end apart: 36, of which 18 were waited for; matrix products, arithmetic and copies ran while one was open for 5% of the time, Pallas kernels for 7%

profile of v3, /device:TPU:0, one launch (start us, length us, event | category | flops | bytes accessed | tf_op | source)
XLA Modules:
  0.0 196.2 jit_solution(4313350744389288393)
XLA Ops:
  1.4 3.1 %collective-permute-start.6 = (f32[2,2,64,256]{3,2,1,0:T(8,128)S(1)}, f32[2,2,64,256]{3,2,1,0:T(8,128)S(1)}, u32[]{:S(2)}, u32[]{:S(2)}) collective-permute-start(f32[2,2,64,256]{3,2,1,0:T(8,128)S(1)} %get-tuple-element.114), channel_id=1, source_target_pairs={{0,8},{4,12},{8,0},{12,4},{16,24},{20,28},{24,16},{28,20},{1,9},{5... | collective-permute-start | bytes 786440 | tf_op jit(solution)/shard_map/ppermute | solution.py:25
  4.5 2.6 %collective-permute-start.7 = (f32[2,2,64,256]{3,2,1,0:T(8,128)S(1)}, f32[2,2,64,256]{3,2,1,0:T(8,128)S(1)}, u32[]{:S(2)}, u32[]{:S(2)}) collective-permute-start(f32[2,2,64,256]{3,2,1,0:T(8,128)S(1)} %get-tuple-element.115), channel_id=1, source_target_pairs={{0,16},{4,20},{8,24},{12,28},{16,0},{20,4},{24,8},{28,12},{1,17},{... | collective-permute-start | bytes 786440 | tf_op jit(solution)/shard_map/ppermute | solution.py:25
  7.8 7.9 %collective-permute-done.6.refs_1_ = f32[2,2,64,256]{3,2,1,0:T(8,128)S(1)} collective-permute-done((f32[2,2,64,256]{3,2,1,0:T(8,128)S(1)}, f32[2,2,64,256]{3,2,1,0:T(8,128)S(1)}, u32[]{:S(2)}, u32[]{:S(2)}) %collective-permute-start.6) | collective-permute-done | bytes 262176 | tf_op jit(solution)/shard_map/ppermute | solution.py:25
  15.7 10.1 %collective-permute-done.7.refs_2_ = f32[2,2,64,256]{3,2,1,0:T(8,128)S(1)} collective-permute-done((f32[2,2,64,256]{3,2,1,0:T(8,128)S(1)}, f32[2,2,64,256]{3,2,1,0:T(8,128)S(1)}, u32[]{:S(2)}, u32[]{:S(2)}) %collective-permute-start.7) | collective-permute-done | bytes 262176 | tf_op jit(solution)/shard_map/ppermute | solution.py:25
  27.0 1.6 collective-permute-start.9
  28.6 1.5 collective-permute-start.10
  30.8 7.6 %collective-permute-done.9.refs_3_ = f32[4,2,2,32,256]{4,3,2,1,0:T(8,128)S(1)} collective-permute-done((f32[4,2,2,32,256]{4,3,2,1,0:T(8,128)S(1)}, f32[4,2,2,32,256]{4,3,2,1,0:T(8,128)S(1)}, u32[]{:S(2)}, u32[]{:S(2)}) %collective-permute-start.9) | collective-permute-done | bytes 524320 | tf_op jit(solution)/shard_map/ppermute | solution.py:25
  40.6 1.6 collective-permute-start.13
  42.7 2.5 %collective-permute-start.5 = (f32[2,2,64,256]{3,2,1,0:T(8,128)S(1)}, f32[2,2,64,256]{3,2,1,0:T(8,128)S(1)}, u32[]{:S(2)}, u32[]{:S(2)}) collective-permute-start(f32[2,2,64,256]{3,2,1,0:T(8,128)S(1)} %get-tuple-element.213), channel_id=1, source_target_pairs={{0,24},{4,28},{8,16},{12,20},{16,8},{20,12},{24,0},{28,4},{1,25},{... | collective-permute-start | bytes 786440 | tf_op jit(solution)/shard_map/ppermute | solution.py:25
  45.2 4.9 %collective-permute-start.4 = (f32[2,2,64,256]{3,2,1,0:T(8,128)S(1)}, f32[2,2,64,256]{3,2,1,0:T(8,128)S(1)}, u32[]{:S(2)}, u32[]{:S(2)}) collective-permute-start(f32[2,2,64,256]{3,2,1,0:T(8,128)S(1)} %get-tuple-element.214), channel_id=1, source_target_pairs={{0,16},{4,20},{8,24},{12,28},{16,0},{20,4},{24,8},{28,12},{1,17},{... | collective-permute-start | bytes 786440 | tf_op jit(solution)/shard_map/ppermute | solution.py:25
  50.3 1.7 collective-permute-done.5.refs_3_
  52.0 15.5 %collective-permute-done.4.refs_2_ = f32[2,2,64,256]{3,2,1,0:T(8,128)S(1)} collective-permute-done((f32[2,2,64,256]{3,2,1,0:T(8,128)S(1)}, f32[2,2,64,256]{3,2,1,0:T(8,128)S(1)}, u32[]{:S(2)}, u32[]{:S(2)}) %collective-permute-start.4) | collective-permute-done | bytes 262176 | tf_op jit(solution)/shard_map/ppermute | solution.py:25
  73.0 11.0 %collective-permute-done.11.refs_3_ = f32[4,2,2,32,256]{4,3,2,1,0:T(8,128)S(1)} collective-permute-done((f32[4,2,2,32,256]{4,3,2,1,0:T(8,128)S(1)}, f32[4,2,2,32,256]{4,3,2,1,0:T(8,128)S(1)}, u32[]{:S(2)}, u32[]{:S(2)}) %collective-permute-start.11) | collective-permute-done | bytes 524320 | tf_op jit(solution)/shard_map/ppermute | solution.py:25
  87.2 2.5 %collective-permute-start.2 = (f32[2,2,64,256]{3,2,1,0:T(8,128)S(1)}, f32[2,2,64,256]{3,2,1,0:T(8,128)S(1)}, u32[]{:S(2)}, u32[]{:S(2)}) collective-permute-start(f32[2,2,64,256]{3,2,1,0:T(8,128)S(1)} %get-tuple-element.209), channel_id=1, source_target_pairs={{0,24},{4,28},{8,16},{12,20},{16,8},{20,12},{24,0},{28,4},{1,25},{... | collective-permute-start | bytes 786440 | tf_op jit(solution)/shard_map/ppermute | solution.py:25
  89.7 1.9 collective-permute-start
  91.7 6.7 %collective-permute-done.2.refs_3_ = f32[2,2,64,256]{3,2,1,0:T(8,128)S(1)} collective-permute-done((f32[2,2,64,256]{3,2,1,0:T(8,128)S(1)}, f32[2,2,64,256]{3,2,1,0:T(8,128)S(1)}, u32[]{:S(2)}, u32[]{:S(2)}) %collective-permute-start.2) | collective-permute-done | bytes 262176 | tf_op jit(solution)/shard_map/ppermute | solution.py:25
  98.3 11.5 %collective-permute-done.1.refs_2_ = f32[2,2,64,256]{3,2,1,0:T(8,128)S(1)} collective-permute-done((f32[2,2,64,256]{3,2,1,0:T(8,128)S(1)}, f32[2,2,64,256]{3,2,1,0:T(8,128)S(1)}, u32[]{:S(2)}, u32[]{:S(2)}) %collective-permute-start.1) | collective-permute-done | bytes 262176 | tf_op jit(solution)/shard_map/ppermute | solution.py:25
  115.5 1.9 collective-permute-start.26
  117.4 2.4 %collective-permute-start.27 = (f32[2,2,64,256]{3,2,1,0:T(8,128)}, f32[2,2,64,256]{3,2,1,0:T(8,128)S(1)}, u32[]{:S(2)}, u32[]{:S(2)}) collective-permute-start(f32[2,2,64,256]{3,2,1,0:T(8,128)} %copy-done), channel_id=1, source_target_pairs={{0,24},{4,28},{8,16},{12,20},{16,8},{20,12},{24,0},{28,4},{1,25},{... | collective-permute-start | bytes 786440 | tf_op jit(solution)/shard_map/ppermute | solution.py:25
  121.3 5.0 %collective-permute-done.17.refs_3_ = f32[4,2,2,32,256]{4,3,2,1,0:T(8,128)S(1)} collective-permute-done((f32[4,2,2,32,256]{4,3,2,1,0:T(8,128)S(1)}, f32[4,2,2,32,256]{4,3,2,1,0:T(8,128)S(1)}, u32[]{:S(2)}, u32[]{:S(2)}) %collective-permute-start.17) | collective-permute-done | bytes 524320 | tf_op jit(solution)/shard_map/ppermute | solution.py:25
  128.3 1.6 collective-permute-start.23
  130.4 8.7 %fusion.1 = (bf16[512,512]{1,0:T(8,128)(2,1)S(1)}, bf16[512,512]{1,0:T(8,128)(2,1)S(1)}, bf16[512,512]{1,0:T(8,128)(2,1)S(1)}, bf16[512,512]{1,0:T(8,128)(2,1)S(1)}) fusion(s32[512]{0:T(512)S(1)} %get-tuple-element.224, s32[512]{0:T(512)S(1)} %get-tuple-element.223, s32[512]{0:T(512)S(1)} %get-tuple-element.227, s32[512]{0:T(512)S(1)} %get-tuple-element.226, ...), kind=kLoop, calls=%fused_computation.11 | loop fusion | flops 11534336 | bytes 2109440 | tf_op jit(solution)/shard_map/convert_element_type | solution.py:46
  139.2 2.8 %finish.3.refs_8_ = f32[2,6,256,256]{3,2,1,0:T(8,128)} custom-call(bf16[512,512]{1,0:T(8,128)(2,1)S(1)} %get-tuple-element.221.refs_0_, bf16[512,512]{1,0:T(8,128)(2,1)S(1)} %get-tuple-element.222.refs_1_, bf16[512,512]{1,0:T(8,128)(2,1)S(1)} %get-tuple-element.218.refs_2_, bf16[512,512]{1,0:T(8,128)(2,1)S(1)} %get-tuple-element.217.refs_3_, ...), custom_call_target="tpu_custom_call" | custom-call | flops 1610612736 | bytes 2097152 | tf_op jit(solution)/shard_map/finish/pallas_call | solution.py:261
  143.7 2.3 %collective-permute-start.33 = (f32[2,2,64,256]{3,2,1,0:T(8,128)S(1)}, f32[2,2,64,256]{3,2,1,0:T(8,128)S(1)}, u32[]{:S(2)}, u32[]{:S(2)}) collective-permute-start(f32[2,2,64,256]{3,2,1,0:T(8,128)S(1)} %get-tuple-element.174), channel_id=1, source_target_pairs={{0,8},{4,12},{8,0},{12,4},{16,24},{20,28},{24,16},{28,20},{1,9},{5... | collective-permute-start | bytes 786440 | tf_op jit(solution)/shard_map/ppermute | solution.py:25
  146.0 2.4 %collective-permute-start.35 = (f32[2,2,64,256]{3,2,1,0:T(8,128)S(1)}, f32[2,2,64,256]{3,2,1,0:T(8,128)S(1)}, u32[]{:S(2)}, u32[]{:S(2)}) collective-permute-start(f32[2,2,64,256]{3,2,1,0:T(8,128)S(1)} %get-tuple-element.176), channel_id=1, source_target_pairs={{0,24},{4,28},{8,16},{12,20},{16,8},{20,12},{24,0},{28,4},{1,25},{... | collective-permute-start | bytes 786440 | tf_op jit(solution)/shard_map/ppermute | solution.py:25
  151.7 5.9 %collective-permute-done.33.refs_5_ = f32[2,2,64,256]{3,2,1,0:T(8,128)S(1)} collective-permute-done((f32[2,2,64,256]{3,2,1,0:T(8,128)S(1)}, f32[2,2,64,256]{3,2,1,0:T(8,128)S(1)}, u32[]{:S(2)}, u32[]{:S(2)}) %collective-permute-start.33) | collective-permute-done | bytes 262176 | tf_op jit(solution)/shard_map/ppermute | solution.py:25
  157.6 9.7 %collective-permute-done.34.refs_6_ = f32[2,2,64,256]{3,2,1,0:T(8,128)S(1)} collective-permute-done((f32[2,2,64,256]{3,2,1,0:T(8,128)S(1)}, f32[2,2,64,256]{3,2,1,0:T(8,128)S(1)}, u32[]{:S(2)}, u32[]{:S(2)}) %collective-permute-start.34) | collective-permute-done | bytes 262176 | tf_op jit(solution)/shard_map/ppermute | solution.py:25
  167.4 2.8 %finish.4.refs_6_ = f32[2,6,256,256]{3,2,1,0:T(8,128)} custom-call(bf16[512,512]{1,0:T(8,128)(2,1)S(1)} %get-tuple-element.221.refs_0_, bf16[512,512]{1,0:T(8,128)(2,1)S(1)} %get-tuple-element.222.refs_1_, bf16[512,512]{1,0:T(8,128)(2,1)S(1)} %get-tuple-element.218.refs_2_, ...), custom_call_target="tpu_custom_call", output_to_operand_aliasing={{}: (8, {})} | custom-call | flops 1610612736 | bytes 2097152 | tf_op jit(solution)/shard_map/finish/pallas_call | solution.py:261
  170.2 7.0 %collective-permute-done.32.refs_6_ = f32[2,2,64,256]{3,2,1,0:T(8,128)S(1)} collective-permute-done((f32[2,2,64,256]{3,2,1,0:T(8,128)S(1)}, f32[2,2,64,256]{3,2,1,0:T(8,128)S(1)}, u32[]{:S(2)}, u32[]{:S(2)}) %collective-permute-start.32) | collective-permute-done | bytes 262176 | tf_op jit(solution)/shard_map/ppermute | solution.py:25
  177.2 1.7 begin.1.refs_5_
  178.9 15.4 %collective-permute-done.30.refs_4_ = f32[2,2,64,256]{3,2,1,0:T(8,128)S(1)} collective-permute-done((f32[2,2,64,256]{3,2,1,0:T(8,128)S(1)}, f32[2,2,64,256]{3,2,1,0:T(8,128)S(1)}, u32[]{:S(2)}, u32[]{:S(2)}) %collective-permute-start.30) | collective-permute-done | bytes 262176 | tf_op jit(solution)/shard_map/ppermute | solution.py:25
  194.3 1.9 finish.5
  (73 shorter events, 30.1 us)
Async XLA Ops:
  1.4 14.3 %collective-permute-start.6 = (f32[2,2,64,256]{3,2,1,0:T(8,128)S(1)}, f32[2,2,64,256]{3,2,1,0:T(8,128)S(1)}, u32[]{:S(2)}, u32[]{:S(2)}) collective-permute-start(f32[2,2,64,256]{3,2,1,0:T(8,128)S(1)} %get-tuple-element.114), channel_id=1, source_target_pairs={{0,8},{4,12},{8,0},{12,4},{16,24},{20,28},{24,16},{28,20},{1,9},{5... | collective-permute-start | bytes 786440 | tf_op jit(solution)/shard_map/ppermute | solution.py:25
  4.5 21.3 %collective-permute-start.7 = (f32[2,2,64,256]{3,2,1,0:T(8,128)S(1)}, f32[2,2,64,256]{3,2,1,0:T(8,128)S(1)}, u32[]{:S(2)}, u32[]{:S(2)}) collective-permute-start(f32[2,2,64,256]{3,2,1,0:T(8,128)S(1)} %get-tuple-element.115), channel_id=1, source_target_pairs={{0,16},{4,20},{8,24},{12,28},{16,0},{20,4},{24,8},{28,12},{1,17},{... | collective-permute-start | bytes 786440 | tf_op jit(solution)/shard_map/ppermute | solution.py:25
  7.1 18.7 %collective-permute-start.8 = (f32[2,2,64,256]{3,2,1,0:T(8,128)S(1)}, f32[2,2,64,256]{3,2,1,0:T(8,128)S(1)}, u32[]{:S(2)}, u32[]{:S(2)}) collective-permute-start(f32[2,2,64,256]{3,2,1,0:T(8,128)S(1)} %get-tuple-element.116), channel_id=1, source_target_pairs={{0,24},{4,28},{8,16},{12,20},{16,8},{20,12},{24,0},{28,4},{1,25},{... | collective-permute-start | bytes 786440 | tf_op jit(solution)/shard_map/ppermute | solution.py:25
  27.0 11.3 %collective-permute-start.9 = (f32[4,2,2,32,256]{4,3,2,1,0:T(8,128)S(1)}, f32[4,2,2,32,256]{4,3,2,1,0:T(8,128)S(1)}, u32[]{:S(2)}, u32[]{:S(2)}) collective-permute-start(f32[4,2,2,32,256]{4,3,2,1,0:T(8,128)S(1)} %get-tuple-element.125.refs_2_), channel_id=1, source_target_pairs={{0,4},{4,0},{8,12},{12,8},{16,20},{20,16},{24,28},{28,24},{1,5},{5... | collective-permute-start | bytes 1572872 | tf_op jit(solution)/shard_map/ppermute | solution.py:25
  28.6 11.2 %collective-permute-start.10 = (f32[4,2,2,32,256]{4,3,2,1,0:T(8,128)S(1)}, f32[4,2,2,32,256]{4,3,2,1,0:T(8,128)S(1)}, u32[]{:S(2)}, u32[]{:S(2)}) collective-permute-start(f32[4,2,2,32,256]{4,3,2,1,0:T(8,128)S(1)} %get-tuple-element.127.refs_4_), channel_id=1, source_target_pairs={{0,2},{1,3},{2,0},{3,1},{4,6},{5,7},{6,4},{7,5},{8,10},{9,11},{10,... | collective-permute-start | bytes 1572872 | tf_op jit(solution)/shard_map/ppermute | solution.py:25
  40.6 28.1 %collective-permute-start.13 = (f32[4,2,2,32,256]{4,3,2,1,0:T(8,128)S(1)}, f32[4,2,2,32,256]{4,3,2,1,0:T(8,128)S(1)}, u32[]{:S(2)}, u32[]{:S(2)}) collective-permute-start(f32[4,2,2,32,256]{4,3,2,1,0:T(8,128)S(1)} %get-tuple-element.137.refs_2_), channel_id=1, source_target_pairs={{0,2},{1,3},{2,0},{3,1},{4,6},{5,7},{6,4},{7,5},{8,10},{9,11},{10,... | collective-permute-start | bytes 1572872 | tf_op jit(solution)/shard_map/ppermute | solution.py:25
  42.2 26.5 %collective-permute-start.14 = (f32[4,2,2,32,256]{4,3,2,1,0:T(8,128)S(1)}, f32[4,2,2,32,256]{4,3,2,1,0:T(8,128)S(1)}, u32[]{:S(2)}, u32[]{:S(2)}) collective-permute-start(f32[4,2,2,32,256]{4,3,2,1,0:T(8,128)S(1)} %get-tuple-element.139.refs_4_), channel_id=1, source_target_pairs={{0,4},{4,0},{8,12},{12,8},{16,20},{20,16},{24,28},{28,24},{1,5},{5... | collective-permute-start | bytes 1572872 | tf_op jit(solution)/shard_map/ppermute | solution.py:25
  42.7 9.3 %collective-permute-start.5 = (f32[2,2,64,256]{3,2,1,0:T(8,128)S(1)}, f32[2,2,64,256]{3,2,1,0:T(8,128)S(1)}, u32[]{:S(2)}, u32[]{:S(2)}) collective-permute-start(f32[2,2,64,256]{3,2,1,0:T(8,128)S(1)} %get-tuple-element.213), channel_id=1, source_target_pairs={{0,24},{4,28},{8,16},{12,20},{16,8},{20,12},{24,0},{28,4},{1,25},{... | collective-permute-start | bytes 786440 | tf_op jit(solution)/shard_map/ppermute | solution.py:25
  45.2 22.2 %collective-permute-start.4 = (f32[2,2,64,256]{3,2,1,0:T(8,128)S(1)}, f32[2,2,64,256]{3,2,1,0:T(8,128)S(1)}, u32[]{:S(2)}, u32[]{:S(2)}) collective-permute-start(f32[2,2,64,256]{3,2,1,0:T(8,128)S(1)} %get-tuple-element.214), channel_id=1, source_target_pairs={{0,16},{4,20},{8,24},{12,28},{16,0},{20,4},{24,8},{28,12},{1,17},{... | collective-permute-start | bytes 786440 | tf_op jit(solution)/shard_map/ppermute | solution.py:25
  50.2 17.3 %collective-permute-start.3 = (f32[2,2,64,256]{3,2,1,0:T(8,128)S(1)}, f32[2,2,64,256]{3,2,1,0:T(8,128)S(1)}, u32[]{:S(2)}, u32[]{:S(2)}) collective-permute-start(f32[2,2,64,256]{3,2,1,0:T(8,128)S(1)} %get-tuple-element.215), channel_id=1, source_target_pairs={{0,8},{4,12},{8,0},{12,4},{16,24},{20,28},{24,16},{28,20},{1,9},{5... | collective-permute-start | bytes 786440 | tf_op jit(solution)/shard_map/ppermute | solution.py:25
  70.1 13.9 %collective-permute-start.11 = (f32[4,2,2,32,256]{4,3,2,1,0:T(8,128)S(1)}, f32[4,2,2,32,256]{4,3,2,1,0:T(8,128)S(1)}, u32[]{:S(2)}, u32[]{:S(2)}) collective-permute-start(f32[4,2,2,32,256]{4,3,2,1,0:T(8,128)S(1)} %get-tuple-element.151.refs_2_), channel_id=1, source_target_pairs={{0,4},{4,0},{8,12},{12,8},{16,20},{20,16},{24,28},{28,24},{1,5},{5... | collective-permute-start | bytes 1572872 | tf_op jit(solution)/shard_map/ppermute | solution.py:25
  71.5 13.6 %collective-permute-start.12 = (f32[4,2,2,32,256]{4,3,2,1,0:T(8,128)S(1)}, f32[4,2,2,32,256]{4,3,2,1,0:T(8,128)S(1)}, u32[]{:S(2)}, u32[]{:S(2)}) collective-permute-start(f32[4,2,2,32,256]{4,3,2,1,0:T(8,128)S(1)} %get-tuple-element.153.refs_4_), channel_id=1, source_target_pairs={{0,2},{1,3},{2,0},{3,1},{4,6},{5,7},{6,4},{7,5},{8,10},{9,11},{10,... | collective-permute-start | bytes 1572872 | tf_op jit(solution)/shard_map/ppermute | solution.py:25
  85.9 25.0 %collective-permute-start.19 = (f32[4,2,2,32,256]{4,3,2,1,0:T(8,128)S(1)}, f32[4,2,2,32,256]{4,3,2,1,0:T(8,128)S(1)}, u32[]{:S(2)}, u32[]{:S(2)}) collective-permute-start(f32[4,2,2,32,256]{4,3,2,1,0:T(8,128)S(1)} %get-tuple-element.163.refs_2_), channel_id=1, source_target_pairs={{0,2},{1,3},{2,0},{3,1},{4,6},{5,7},{6,4},{7,5},{8,10},{9,11},{10,... | collective-permute-start | bytes 1572872 | tf_op jit(solution)/shard_map/ppermute | solution.py:25
  86.5 24.5 %collective-permute-start.20 = (f32[4,2,2,32,256]{4,3,2,1,0:T(8,128)S(1)}, f32[4,2,2,32,256]{4,3,2,1,0:T(8,128)S(1)}, u32[]{:S(2)}, u32[]{:S(2)}) collective-permute-start(f32[4,2,2,32,256]{4,3,2,1,0:T(8,128)S(1)} %get-tuple-element.165.refs_4_), channel_id=1, source_target_pairs={{0,4},{4,0},{8,12},{12,8},{16,20},{20,16},{24,28},{28,24},{1,5},{5... | collective-permute-start | bytes 1572872 | tf_op jit(solution)/shard_map/ppermute | solution.py:25
  87.2 11.1 %collective-permute-start.2 = (f32[2,2,64,256]{3,2,1,0:T(8,128)S(1)}, f32[2,2,64,256]{3,2,1,0:T(8,128)S(1)}, u32[]{:S(2)}, u32[]{:S(2)}) collective-permute-start(f32[2,2,64,256]{3,2,1,0:T(8,128)S(1)} %get-tuple-element.209), channel_id=1, source_target_pairs={{0,24},{4,28},{8,16},{12,20},{16,8},{20,12},{24,0},{28,4},{1,25},{... | collective-permute-start | bytes 786440 | tf_op jit(solution)/shard_map/ppermute | solution.py:25
  89.7 20.1 %collective-permute-start.1 = (f32[2,2,64,256]{3,2,1,0:T(8,128)S(1)}, f32[2,2,64,256]{3,2,1,0:T(8,128)S(1)}, u32[]{:S(2)}, u32[]{:S(2)}) collective-permute-start(f32[2,2,64,256]{3,2,1,0:T(8,128)S(1)} %get-tuple-element.210), channel_id=1, source_target_pairs={{0,16},{4,20},{8,24},{12,28},{16,0},{20,4},{24,8},{28,12},{1,17},{... | collective-permute-start | bytes 786440 | tf_op jit(solution)/shard_map/ppermute | solution.py:25
  89.7 20.1 %collective-permute-start = (f32[2,2,64,256]{3,2,1,0:T(8,128)S(1)}, f32[2,2,64,256]{3,2,1,0:T(8,128)S(1)}, u32[]{:S(2)}, u32[]{:S(2)}) collective-permute-start(f32[2,2,64,256]{3,2,1,0:T(8,128)S(1)} %get-tuple-element.211), channel_id=1, source_target_pairs={{0,8},{4,12},{8,0},{12,4},{16,24},{20,28},{24,16},{28,20},{1,9},{5... | collective-permute-start | bytes 786440 | tf_op jit(solution)/shard_map/ppermute | solution.py:25
  111.9 5.5 %collective-permute-start.22 = (f32[4,2,2,32,256]{4,3,2,1,0:T(8,128)S(1)}, f32[4,2,2,32,256]{4,3,2,1,0:T(8,128)}, u32[]{:S(2)}, u32[]{:S(2)}) collective-permute-start(f32[4,2,2,32,256]{4,3,2,1,0:T(8,128)S(1)} %get-tuple-element.171.refs_4_), channel_id=1, source_target_pairs={{0,1},{1,0},{2,3},{3,2},{4,5},{5,4},{6,7},{7,6},{8,9},{9,8},{10,11... | collective-permute-start | bytes 1572872 | tf_op jit(solution)/shard_map/ppermute | solution.py:25
  112.4 13.9 %collective-permute-start.17 = (f32[4,2,2,32,256]{4,3,2,1,0:T(8,128)S(1)}, f32[4,2,2,32,256]{4,3,2,1,0:T(8,128)S(1)}, u32[]{:S(2)}, u32[]{:S(2)}) collective-permute-start(f32[4,2,2,32,256]{4,3,2,1,0:T(8,128)S(1)} %get-tuple-element.177.refs_2_), channel_id=1, source_target_pairs={{0,4},{4,0},{8,12},{12,8},{16,20},{20,16},{24,28},{28,24},{1,5},{5... | collective-permute-start | bytes 1572872 | tf_op jit(solution)/shard_map/ppermute | solution.py:25
  113.9 13.6 %collective-permute-start.18 = (f32[4,2,2,32,256]{4,3,2,1,0:T(8,128)S(1)}, f32[4,2,2,32,256]{4,3,2,1,0:T(8,128)S(1)}, u32[]{:S(2)}, u32[]{:S(2)}) collective-permute-start(f32[4,2,2,32,256]{4,3,2,1,0:T(8,128)S(1)} %get-tuple-element.179.refs_4_), channel_id=1, source_target_pairs={{0,2},{1,3},{2,0},{3,1},{4,6},{5,7},{6,4},{7,5},{8,10},{9,11},{10,... | collective-permute-start | bytes 1572872 | tf_op jit(solution)/shard_map/ppermute | solution.py:25
  115.4 23.7 %collective-permute-start.25 = (f32[2,2,64,256]{3,2,1,0:T(8,128)}, f32[2,2,64,256]{3,2,1,0:T(8,128)S(1)}, u32[]{:S(2)}, u32[]{:S(2)}) collective-permute-start(f32[2,2,64,256]{3,2,1,0:T(8,128)} %copy-done.2), channel_id=1, source_target_pairs={{0,8},{4,12},{8,0},{12,4},{16,24},{20,28},{24,16},{28,20},{1,9},{5... | collective-permute-start | bytes 786440 | tf_op jit(solution)/shard_map/ppermute | solution.py:25
  115.5 23.7 %collective-permute-start.26 = (f32[2,2,64,256]{3,2,1,0:T(8,128)}, f32[2,2,64,256]{3,2,1,0:T(8,128)S(1)}, u32[]{:S(2)}, u32[]{:S(2)}) collective-permute-start(f32[2,2,64,256]{3,2,1,0:T(8,128)} %copy-done.1), channel_id=1, source_target_pairs={{0,16},{4,20},{8,24},{12,28},{16,0},{20,4},{24,8},{28,12},{1,17},{... | collective-permute-start | bytes 786440 | tf_op jit(solution)/shard_map/ppermute | solution.py:25
  117.4 21.7 %collective-permute-start.27 = (f32[2,2,64,256]{3,2,1,0:T(8,128)}, f32[2,2,64,256]{3,2,1,0:T(8,128)S(1)}, u32[]{:S(2)}, u32[]{:S(2)}) collective-permute-start(f32[2,2,64,256]{3,2,1,0:T(8,128)} %copy-done), channel_id=1, source_target_pairs={{0,24},{4,28},{8,16},{12,20},{16,8},{20,12},{24,0},{28,4},{1,25},{... | collective-permute-start | bytes 786440 | tf_op jit(solution)/shard_map/ppermute | solution.py:25
  128.3 13.7 %collective-permute-start.23 = (f32[4,2,2,32,256]{4,3,2,1,0:T(8,128)S(1)}, f32[4,2,2,32,256]{4,3,2,1,0:T(8,128)S(1)}, u32[]{:S(2)}, u32[]{:S(2)}) collective-permute-start(f32[4,2,2,32,256]{4,3,2,1,0:T(8,128)S(1)} %get-tuple-element.187.refs_2_), channel_id=1, source_target_pairs={{0,2},{1,3},{2,0},{3,1},{4,6},{5,7},{6,4},{7,5},{8,10},{9,11},{10,... | collective-permute-start | bytes 1572872 | tf_op jit(solution)/shard_map/ppermute | solution.py:25
  129.8 12.5 %collective-permute-start.24 = (f32[4,2,2,32,256]{4,3,2,1,0:T(8,128)S(1)}, f32[4,2,2,32,256]{4,3,2,1,0:T(8,128)S(1)}, u32[]{:S(2)}, u32[]{:S(2)}) collective-permute-start(f32[4,2,2,32,256]{4,3,2,1,0:T(8,128)S(1)} %get-tuple-element.189.refs_4_), channel_id=1, source_target_pairs={{0,4},{4,0},{8,12},{12,8},{16,20},{20,16},{24,28},{28,24},{1,5},{5... | collective-permute-start | bytes 1572872 | tf_op jit(solution)/shard_map/ppermute | solution.py:25
  143.1 5.3 %collective-permute-start.28 = (f32[4,2,2,32,256]{4,3,2,1,0:T(8,128)S(1)}, f32[4,2,2,32,256]{4,3,2,1,0:T(8,128)S(1)}, u32[]{:S(2)}, u32[]{:S(2)}) collective-permute-start(f32[4,2,2,32,256]{4,3,2,1,0:T(8,128)S(1)} %get-tuple-element.193.refs_2_), channel_id=1, source_target_pairs={{0,1},{1,0},{2,3},{3,2},{4,5},{5,4},{6,7},{7,6},{8,9},{9,8},{10,11... | collective-permute-start | bytes 1572872 | tf_op jit(solution)/shard_map/ppermute | solution.py:25
  143.7 13.9 %collective-permute-start.33 = (f32[2,2,64,256]{3,2,1,0:T(8,128)S(1)}, f32[2,2,64,256]{3,2,1,0:T(8,128)S(1)}, u32[]{:S(2)}, u32[]{:S(2)}) collective-permute-start(f32[2,2,64,256]{3,2,1,0:T(8,128)S(1)} %get-tuple-element.174), channel_id=1, source_target_pairs={{0,8},{4,12},{8,0},{12,4},{16,24},{20,28},{24,16},{28,20},{1,9},{5... | collective-permute-start | bytes 786440 | tf_op jit(solution)/shard_map/ppermute | solution.py:25
  146.0 21.4 %collective-permute-start.34 = (f32[2,2,64,256]{3,2,1,0:T(8,128)S(1)}, f32[2,2,64,256]{3,2,1,0:T(8,128)S(1)}, u32[]{:S(2)}, u32[]{:S(2)}) collective-permute-start(f32[2,2,64,256]{3,2,1,0:T(8,128)S(1)} %get-tuple-element.175), channel_id=1, source_target_pairs={{0,16},{4,20},{8,24},{12,28},{16,0},{20,4},{24,8},{28,12},{1,17},{... | collective-permute-start | bytes 786440 | tf_op jit(solution)/shard_map/ppermute | solution.py:25
  146.0 21.4 %collective-permute-start.35 = (f32[2,2,64,256]{3,2,1,0:T(8,128)S(1)}, f32[2,2,64,256]{3,2,1,0:T(8,128)S(1)}, u32[]{:S(2)}, u32[]{:S(2)}) collective-permute-start(f32[2,2,64,256]{3,2,1,0:T(8,128)S(1)} %get-tuple-element.176), channel_id=1, source_target_pairs={{0,24},{4,28},{8,16},{12,20},{16,8},{20,12},{24,0},{28,4},{1,25},{... | collective-permute-start | bytes 786440 | tf_op jit(solution)/shard_map/ppermute | solution.py:25
  149.1 21.0 %collective-permute-start.31 = (f32[2,2,64,256]{3,2,1,0:T(8,128)S(1)}, f32[2,2,64,256]{3,2,1,0:T(8,128)S(1)}, u32[]{:S(2)}, u32[]{:S(2)}) collective-permute-start(f32[2,2,64,256]{3,2,1,0:T(8,128)S(1)} %get-tuple-element.199), channel_id=1, source_target_pairs={{0,8},{4,12},{8,0},{12,4},{16,24},{20,28},{24,16},{28,20},{1,9},{5... | collective-permute-start | bytes 786440 | tf_op jit(solution)/shard_map/ppermute | solution.py:25
  150.3 26.9 %collective-permute-start.32 = (f32[2,2,64,256]{3,2,1,0:T(8,128)S(1)}, f32[2,2,64,256]{3,2,1,0:T(8,128)S(1)}, u32[]{:S(2)}, u32[]{:S(2)}) collective-permute-start(f32[2,2,64,256]{3,2,1,0:T(8,128)S(1)} %get-tuple-element.200), channel_id=1, source_target_pairs={{0,24},{4,28},{8,16},{12,20},{16,8},{20,12},{24,0},{28,4},{1,25},{... | collective-permute-start | bytes 786440 | tf_op jit(solution)/shard_map/ppermute | solution.py:25
  157.6 36.7 %collective-permute-start.30 = (f32[2,2,64,256]{3,2,1,0:T(8,128)S(1)}, f32[2,2,64,256]{3,2,1,0:T(8,128)S(1)}, u32[]{:S(2)}, u32[]{:S(2)}) collective-permute-start(f32[2,2,64,256]{3,2,1,0:T(8,128)S(1)} %get-tuple-element.197), channel_id=1, source_target_pairs={{0,16},{4,20},{8,24},{12,28},{16,0},{20,4},{24,8},{28,12},{1,17},{... | collective-permute-start | bytes 786440 | tf_op jit(solution)/shard_map/ppermute | solution.py:25
  (8 other events, 173.1 us)

commit v4 on v2

--- a/solution.py
+++ b/solution.py
@@ -11,7 +11,7 @@
 
 
 GRANT = 16 * 2**20
-LANES = (3, 2, 1)
+LANES = (2, 3, 1)
 
 F32 = jnp.float32
 BF16 = jnp.bfloat16
@@ -171,22 +171,22 @@
     count = high.shape[0]
     both = jnp.dot(jnp.concatenate([high, low], axis=0), right[0][...], preferred_element_type=F32)
     mixed = both[:count] + (both[count:] + jnp.dot(high, right[1][...], preferred_element_type=F32))
-    width = 2 * quarter
-    sides = [jnp.concatenate([ref[:, d * width : (d + 1) * width] for d in lanes], axis=1) for ref in left]
+    width, local = 2 * quarter, 4 * quarter
     for plane in range(planes):
         rows = []
         for i in range(len(lanes)):
             at = (plane * len(lanes) + i) * quarter
             rows += [mixed[at : at + quarter, :columns], mixed[at : at + quarter, columns:]]
-        yield dot3(sides, halves(jnp.concatenate(rows, axis=0)))
+        rows = halves(jnp.concatenate(rows, axis=0))
+        for part in range(2):
+            at = slice(part * local, (part + 1) * local)
+            sides = [jnp.concatenate([ref[at, d * width : (d + 1) * width] for d in lanes], axis=1) for ref in left]
+            yield plane, part, dot3(sides, rows)
 
 
 def begin_kernel(lanes, *refs):
-    base_ref = refs[-1]
-    local = base_ref.shape[2]
-    for plane, values in enumerate(transformed(lanes, refs[:4], refs[4:-1])):
-        base_ref[plane, 0] = values[:local]
-        base_ref[plane, 1] = values[local:]
+    for plane, part, values in transformed(lanes, refs[:4], refs[4:-1]):
+        refs[-1][plane, part] = values
 
 
 def begin(pieces, lanes, tables):
@@ -206,13 +206,10 @@
 def finish_kernel(start, lanes, has_base, *refs):
     out_ref, done, sems = refs[-3:]
     count = len(lanes)
-    local = done.shape[2]
     copies = []
-    for plane, values in enumerate(transformed(lanes, refs[:4], refs[4 : 4 + count])):
-        for part in range(2):
-            half = values[part * local : (part + 1) * local]
-            done[plane, part] = half + refs[4 + count][plane, part] if has_base else half
-        copies.append(pltpu.make_async_copy(done.at[plane], out_ref.at[:, start + plane], sems.at[plane]))
+    for plane, part, values in transformed(lanes, refs[:4], refs[4 : 4 + count]):
+        done[plane, part] = values + refs[4 + count][plane, part] if has_base else values
+        copies.append(pltpu.make_async_copy(done.at[plane, part], out_ref.at[part, start + plane], sems.at[plane, part]))
         copies[-1].start()
     for copy in copies:
         copy.wait()
@@ -235,7 +232,7 @@
         out_shape=jax.ShapeDtypeStruct((2, total, rows, columns), F32),
         scratch_shapes=[
             pltpu.VMEM((planes, 2, rows, columns), F32),
-            pltpu.SemaphoreType.DMA((planes,)),
+            pltpu.SemaphoreType.DMA((planes, 2)),
         ],
         input_output_aliases=aliases,
         compiler_params=pltpu.CompilerParams(vmem_limit_bytes=GRANT),
@@ -326,7 +323,7 @@
         shape = (2, size, 1, quarter, columns)
         at = jnp.uint32(start)
         pieces = [None] * 4
-        for lanes in (LANES, (0,)) if i == 0 else ((*LANES, 0),):
+        for lanes in ((LANES[0],), (*LANES[1:], 0)) if i == 0 else ((*LANES, 0),):
             for d in lanes:
                 pieces[d] = lax.dynamic_slice(quarters, (zero, at, peers[d], zero, zero), shape)[:, :, 0]
             quarters = after(quarters, [pieces[d] for d in lanes])
@@ -364,7 +361,7 @@
         elif kind == "end":
             lanes, base = (0, 1, 2, 3), None
             if i == len(chunks) - 1:
-                early, lanes = (0, 1, 3), (2,)
+                early, lanes = (0, LANES[2], LANES[0]), LANES[1:2]
                 pieces = after([back[i][d] for d in early], done)
                 base = begin(pieces, early, tables)
                 done = base

time: 203 us -> 201 us (level)
  the two profiles are of different devices: /device:TPU:0 before, /device:TPU:19 now
where the time goes in v4:
time: 201 us; the launch traced here: 198 us
  waiting for transfers between devices  125 us (62%)
  starting transfers between devices  37.2 us (19%)
  Pallas kernels  19.9 us (10%)
  other arithmetic  8.73 us (4%)
  local copies, waits for them, and re-layouts  6.08 us (3%)
    ppermute x36, waiting for transfers between devices, exchanged(): return lax.ppermute(block, axis, [(i, i ^ mask) for i in range(count)])  125 us
    ppermute x36, starting transfers between devices, exchanged(): return lax.ppermute(block, axis, [(i, i ^ mask) for i in range(count)])  37.2 us
    convert_element_type x1, other arithmetic, dft_table(): return (high.astype(BF16), (values - high).astype(BF16))  8.71 us
    pallas_call x9, Pallas kernels, butterfly(): pl.pallas_call(functools.partial(butterfly_kernel, kinds, apart), in_spec...  7.59 us
    pallas_call x3, Pallas kernels, finish(): pl.pallas_call(functools.partial(finish_kernel, start, lanes, base is not...  7.13 us
    squeeze x4, local copies, waits for them, and re-layouts, shards(): lax.dynamic_slice(quarters, (zero, at, peers[d], zero, zero), shape)  4.69 us
  transfers between devices with their start and end apart: 36, of which 20 were waited for; matrix products, arithmetic and copies ran while one was open for 7% of the time, Pallas kernels for 7%

profile of v4, /device:TPU:19, one launch (start us, length us, event | category | flops | bytes accessed | tf_op | source)
XLA Modules:
  0.0 197.7 jit_solution(6635658385698976453)
XLA Ops:
  5.6 6.2 %collective-permute-done.7.refs_2_ = f32[2,2,64,256]{3,2,1,0:T(8,128)S(1)} collective-permute-done((f32[2,2,64,256]{3,2,1,0:T(8,128)S(1)}, f32[2,2,64,256]{3,2,1,0:T(8,128)S(1)}, u32[]{:S(2)}, u32[]{:S(2)}) %collective-permute-start.7) | collective-permute-done | bytes 262176 | tf_op jit(solution)/shard_map/ppermute | solution.py:25
  11.8 2.1 %collective-permute-done.6.refs_1_ = f32[2,2,64,256]{3,2,1,0:T(8,128)S(1)} collective-permute-done((f32[2,2,64,256]{3,2,1,0:T(8,128)S(1)}, f32[2,2,64,256]{3,2,1,0:T(8,128)S(1)}, u32[]{:S(2)}, u32[]{:S(2)}) %collective-permute-start.6) | collective-permute-done | bytes 262176 | tf_op jit(solution)/shard_map/ppermute | solution.py:25
  13.8 13.2 %collective-permute-done.8.refs_3_ = f32[2,2,64,256]{3,2,1,0:T(8,128)S(1)} collective-permute-done((f32[2,2,64,256]{3,2,1,0:T(8,128)S(1)}, f32[2,2,64,256]{3,2,1,0:T(8,128)S(1)}, u32[]{:S(2)}, u32[]{:S(2)}) %collective-permute-start.8) | collective-permute-done | bytes 262176 | tf_op jit(solution)/shard_map/ppermute | solution.py:25
  30.5 10.8 %collective-permute-done.9.refs_3_ = f32[4,2,2,32,256]{4,3,2,1,0:T(8,128)S(1)} collective-permute-done((f32[4,2,2,32,256]{4,3,2,1,0:T(8,128)S(1)}, f32[4,2,2,32,256]{4,3,2,1,0:T(8,128)S(1)}, u32[]{:S(2)}, u32[]{:S(2)}) %collective-permute-start.9) | collective-permute-done | bytes 524320 | tf_op jit(solution)/shard_map/ppermute | solution.py:25
  45.1 3.5 %collective-permute-start.4 = (f32[2,2,64,256]{3,2,1,0:T(8,128)S(1)}, f32[2,2,64,256]{3,2,1,0:T(8,128)S(1)}, u32[]{:S(2)}, u32[]{:S(2)}) collective-permute-start(f32[2,2,64,256]{3,2,1,0:T(8,128)S(1)} %get-tuple-element.210), channel_id=1, source_target_pairs={{0,16},{4,20},{8,24},{12,28},{16,0},{20,4},{24,8},{28,12},{1,17},{... | collective-permute-start | bytes 786440 | tf_op jit(solution)/shard_map/ppermute | solution.py:25
  48.5 2.2 %collective-permute-done.3.refs_1_ = f32[2,2,64,256]{3,2,1,0:T(8,128)S(1)} collective-permute-done((f32[2,2,64,256]{3,2,1,0:T(8,128)S(1)}, f32[2,2,64,256]{3,2,1,0:T(8,128)S(1)}, u32[]{:S(2)}, u32[]{:S(2)}) %collective-permute-start.3) | collective-permute-done | bytes 262176 | tf_op jit(solution)/shard_map/ppermute | solution.py:25
  50.7 1.7 collective-permute-done.5.refs_3_
  52.4 13.5 %collective-permute-done.4.refs_2_ = f32[2,2,64,256]{3,2,1,0:T(8,128)S(1)} collective-permute-done((f32[2,2,64,256]{3,2,1,0:T(8,128)S(1)}, f32[2,2,64,256]{3,2,1,0:T(8,128)S(1)}, u32[]{:S(2)}, u32[]{:S(2)}) %collective-permute-start.4) | collective-permute-done | bytes 262176 | tf_op jit(solution)/shard_map/ppermute | solution.py:25
  67.9 2.6 %collective-permute-start.15 = (f32[4,2,2,32,256]{4,3,2,1,0:T(8,128)S(1)}, f32[4,2,2,32,256]{4,3,2,1,0:T(8,128)S(1)}, u32[]{:S(2)}, u32[]{:S(2)}) collective-permute-start(f32[4,2,2,32,256]{4,3,2,1,0:T(8,128)S(1)} %get-tuple-element.137.refs_2_), channel_id=1, source_target_pairs={{0,1},{1,0},{2,3},{3,2},{4,5},{5,4},{6,7},{7,6},{8,9},{9,8},{10,11... | collective-permute-start | bytes 1572872 | tf_op jit(solution)/shard_map/ppermute | solution.py:25
  73.8 9.9 %collective-permute-done.11.refs_3_ = f32[4,2,2,32,256]{4,3,2,1,0:T(8,128)S(1)} collective-permute-done((f32[4,2,2,32,256]{4,3,2,1,0:T(8,128)S(1)}, f32[4,2,2,32,256]{4,3,2,1,0:T(8,128)S(1)}, u32[]{:S(2)}, u32[]{:S(2)}) %collective-permute-start.11) | collective-permute-done | bytes 524320 | tf_op jit(solution)/shard_map/ppermute | solution.py:25
  88.2 1.5 collective-permute-start.2
  89.7 4.0 %collective-permute-start.1 = (f32[2,2,64,256]{3,2,1,0:T(8,128)S(1)}, f32[2,2,64,256]{3,2,1,0:T(8,128)S(1)}, u32[]{:S(2)}, u32[]{:S(2)}) collective-permute-start(f32[2,2,64,256]{3,2,1,0:T(8,128)S(1)} %get-tuple-element.204), channel_id=1, source_target_pairs={{0,16},{4,20},{8,24},{12,28},{16,0},{20,4},{24,8},{28,12},{1,17},{... | collective-permute-start | bytes 786440 | tf_op jit(solution)/shard_map/ppermute | solution.py:25
  93.7 8.2 %collective-permute-done.2.refs_3_ = f32[2,2,64,256]{3,2,1,0:T(8,128)S(1)} collective-permute-done((f32[2,2,64,256]{3,2,1,0:T(8,128)S(1)}, f32[2,2,64,256]{3,2,1,0:T(8,128)S(1)}, u32[]{:S(2)}, u32[]{:S(2)}) %collective-permute-start.2) | collective-permute-done | bytes 262176 | tf_op jit(solution)/shard_map/ppermute | solution.py:25
  101.9 8.2 %collective-permute-done.1.refs_2_ = f32[2,2,64,256]{3,2,1,0:T(8,128)S(1)} collective-permute-done((f32[2,2,64,256]{3,2,1,0:T(8,128)S(1)}, f32[2,2,64,256]{3,2,1,0:T(8,128)S(1)}, u32[]{:S(2)}, u32[]{:S(2)}) %collective-permute-start.1) | collective-permute-done | bytes 262176 | tf_op jit(solution)/shard_map/ppermute | solution.py:25
  112.1 3.0 %collective-permute-start.21 = (f32[4,2,2,32,256]{4,3,2,1,0:T(8,128)S(1)}, f32[4,2,2,32,256]{4,3,2,1,0:T(8,128)}, u32[]{:S(2)}, u32[]{:S(2)}) collective-permute-start(f32[4,2,2,32,256]{4,3,2,1,0:T(8,128)S(1)} %get-tuple-element.163.refs_2_), channel_id=1, source_target_pairs={{0,1},{1,0},{2,3},{3,2},{4,5},{5,4},{6,7},{7,6},{8,9},{9,8},{10,11... | collective-permute-start | bytes 1572872 | tf_op jit(solution)/shard_map/ppermute | solution.py:25
  116.7 2.0 %collective-permute-start.25 = (f32[2,2,64,256]{3,2,1,0:T(8,128)}, f32[2,2,64,256]{3,2,1,0:T(8,128)S(1)}, u32[]{:S(2)}, u32[]{:S(2)}) collective-permute-start(f32[2,2,64,256]{3,2,1,0:T(8,128)} %copy-done.2), channel_id=1, source_target_pairs={{0,8},{4,12},{8,0},{12,4},{16,24},{20,28},{24,16},{28,20},{1,9},{5... | collective-permute-start | bytes 786440 | tf_op jit(solution)/shard_map/ppermute | solution.py:25
  120.2 1.4 butterfly.14
  121.6 6.6 %collective-permute-done.17.refs_3_ = f32[4,2,2,32,256]{4,3,2,1,0:T(8,128)S(1)} collective-permute-done((f32[4,2,2,32,256]{4,3,2,1,0:T(8,128)S(1)}, f32[4,2,2,32,256]{4,3,2,1,0:T(8,128)S(1)}, u32[]{:S(2)}, u32[]{:S(2)}) %collective-permute-start.17) | collective-permute-done | bytes 524320 | tf_op jit(solution)/shard_map/ppermute | solution.py:25
  130.6 8.7 %fusion.1 = (bf16[512,512]{1,0:T(8,128)(2,1)S(1)}, bf16[512,512]{1,0:T(8,128)(2,1)S(1)}, bf16[512,512]{1,0:T(8,128)(2,1)S(1)}, bf16[512,512]{1,0:T(8,128)(2,1)S(1)}) fusion(s32[512]{0:T(512)S(1)} %get-tuple-element.221, s32[512]{0:T(512)S(1)} %get-tuple-element.220, s32[512]{0:T(512)S(1)} %get-tuple-element.224, s32[512]{0:T(512)S(1)} %get-tuple-element.223, ...), kind=kLoop, calls=%fused_computation.11 | loop fusion | flops 11534336 | bytes 2109440 | tf_op jit(solution)/shard_map/convert_element_type | solution.py:46
  139.3 3.4 %collective-permute-done.27.refs_7_ = f32[2,2,64,256]{3,2,1,0:T(8,128)S(1)} collective-permute-done((f32[2,2,64,256]{3,2,1,0:T(8,128)}, f32[2,2,64,256]{3,2,1,0:T(8,128)S(1)}, u32[]{:S(2)}, u32[]{:S(2)}) %collective-permute-start.27) | collective-permute-done | bytes 262176 | tf_op jit(solution)/shard_map/ppermute | solution.py:25
  142.7 2.7 %finish.3.refs_8_ = f32[2,6,256,256]{3,2,1,0:T(8,128)} custom-call(bf16[512,512]{1,0:T(8,128)(2,1)S(1)} %get-tuple-element.218.refs_0_, bf16[512,512]{1,0:T(8,128)(2,1)S(1)} %get-tuple-element.219.refs_1_, bf16[512,512]{1,0:T(8,128)(2,1)S(1)} %get-tuple-element.215.refs_2_, bf16[512,512]{1,0:T(8,128)(2,1)S(1)} %get-tuple-element.214.refs_3_, ...), custom_call_target="tpu_custom_call" | custom-call | flops 1610612736 | bytes 2097152 | tf_op jit(solution)/shard_map/finish/pallas_call | solution.py:228
  146.2 1.9 collective-permute-start.28
  148.2 2.5 %collective-permute-start.34 = (f32[2,2,64,256]{3,2,1,0:T(8,128)S(1)}, f32[2,2,64,256]{3,2,1,0:T(8,128)S(1)}, u32[]{:S(2)}, u32[]{:S(2)}) collective-permute-start(f32[2,2,64,256]{3,2,1,0:T(8,128)S(1)} %get-tuple-element.169), channel_id=1, source_target_pairs={{0,16},{4,20},{8,24},{12,28},{16,0},{20,4},{24,8},{28,12},{1,17},{... | collective-permute-start | bytes 786440 | tf_op jit(solution)/shard_map/ppermute | solution.py:25
  152.6 1.5 collective-permute-start.32
  154.1 4.6 %collective-permute-done.33.refs_5_ = f32[2,2,64,256]{3,2,1,0:T(8,128)S(1)} collective-permute-done((f32[2,2,64,256]{3,2,1,0:T(8,128)S(1)}, f32[2,2,64,256]{3,2,1,0:T(8,128)S(1)}, u32[]{:S(2)}, u32[]{:S(2)}) %collective-permute-start.33) | collective-permute-done | bytes 262176 | tf_op jit(solution)/shard_map/ppermute | solution.py:25
  159.3 2.9 %collective-permute-done.34.refs_6_ = f32[2,2,64,256]{3,2,1,0:T(8,128)S(1)} collective-permute-done((f32[2,2,64,256]{3,2,1,0:T(8,128)S(1)}, f32[2,2,64,256]{3,2,1,0:T(8,128)S(1)}, u32[]{:S(2)}, u32[]{:S(2)}) %collective-permute-start.34) | collective-permute-done | bytes 262176 | tf_op jit(solution)/shard_map/ppermute | solution.py:25
  162.3 11.2 %collective-permute-done.35.refs_7_ = f32[2,2,64,256]{3,2,1,0:T(8,128)S(1)} collective-permute-done((f32[2,2,64,256]{3,2,1,0:T(8,128)S(1)}, f32[2,2,64,256]{3,2,1,0:T(8,128)S(1)}, u32[]{:S(2)}, u32[]{:S(2)}) %collective-permute-start.35) | collective-permute-done | bytes 262176 | tf_op jit(solution)/shard_map/ppermute | solution.py:25
  173.5 2.7 %finish.4.refs_6_ = f32[2,6,256,256]{3,2,1,0:T(8,128)} custom-call(bf16[512,512]{1,0:T(8,128)(2,1)S(1)} %get-tuple-element.218.refs_0_, bf16[512,512]{1,0:T(8,128)(2,1)S(1)} %get-tuple-element.219.refs_1_, bf16[512,512]{1,0:T(8,128)(2,1)S(1)} %get-tuple-element.215.refs_2_, ...), custom_call_target="tpu_custom_call", output_to_operand_aliasing={{}: (8, {})} | custom-call | flops 1610612736 | bytes 2097152 | tf_op jit(solution)/shard_map/finish/pallas_call | solution.py:228
  176.2 13.2 %collective-permute-done.32.refs_6_ = f32[2,2,64,256]{3,2,1,0:T(8,128)S(1)} collective-permute-done((f32[2,2,64,256]{3,2,1,0:T(8,128)S(1)}, f32[2,2,64,256]{3,2,1,0:T(8,128)S(1)}, u32[]{:S(2)}, u32[]{:S(2)}) %collective-permute-start.32) | collective-permute-done | bytes 262176 | tf_op jit(solution)/shard_map/ppermute | solution.py:25
  189.4 1.7 begin.1.refs_5_
  191.1 4.9 %collective-permute-done.30.refs_4_ = f32[2,2,64,256]{3,2,1,0:T(8,128)S(1)} collective-permute-done((f32[2,2,64,256]{3,2,1,0:T(8,128)S(1)}, f32[2,2,64,256]{3,2,1,0:T(8,128)S(1)}, u32[]{:S(2)}, u32[]{:S(2)}) %collective-permute-start.30) | collective-permute-done | bytes 262176 | tf_op jit(solution)/shard_map/ppermute | solution.py:25
  196.0 1.8 finish.5
  (72 shorter events, 33.3 us)
Async XLA Ops:
  1.0 10.8 %collective-permute-start.7 = (f32[2,2,64,256]{3,2,1,0:T(8,128)S(1)}, f32[2,2,64,256]{3,2,1,0:T(8,128)S(1)}, u32[]{:S(2)}, u32[]{:S(2)}) collective-permute-start(f32[2,2,64,256]{3,2,1,0:T(8,128)S(1)} %dynamic-slice_bitcast_fusion.11), channel_id=1, source_target_pairs={{0,16},{4,20},{8,24},{12,28},{16,0},{20,4},{24,8},{28,12},{1,17},{... | collective-permute-start | bytes 786440 | tf_op jit(solution)/shard_map/ppermute | solution.py:25
  2.3 11.6 %collective-permute-start.6 = (f32[2,2,64,256]{3,2,1,0:T(8,128)S(1)}, f32[2,2,64,256]{3,2,1,0:T(8,128)S(1)}, u32[]{:S(2)}, u32[]{:S(2)}) collective-permute-start(f32[2,2,64,256]{3,2,1,0:T(8,128)S(1)} %get-tuple-element.212), channel_id=1, source_target_pairs={{0,8},{4,12},{8,0},{12,4},{16,24},{20,28},{24,16},{28,20},{1,9},{5... | collective-permute-start | bytes 786440 | tf_op jit(solution)/shard_map/ppermute | solution.py:25
  3.6 23.4 %collective-permute-start.8 = (f32[2,2,64,256]{3,2,1,0:T(8,128)S(1)}, f32[2,2,64,256]{3,2,1,0:T(8,128)S(1)}, u32[]{:S(2)}, u32[]{:S(2)}) collective-permute-start(f32[2,2,64,256]{3,2,1,0:T(8,128)S(1)} %get-tuple-element.213), channel_id=1, source_target_pairs={{0,24},{4,28},{8,16},{12,20},{16,8},{20,12},{24,0},{28,4},{1,25},{... | collective-permute-start | bytes 786440 | tf_op jit(solution)/shard_map/ppermute | solution.py:25
  28.2 13.1 %collective-permute-start.9 = (f32[4,2,2,32,256]{4,3,2,1,0:T(8,128)S(1)}, f32[4,2,2,32,256]{4,3,2,1,0:T(8,128)S(1)}, u32[]{:S(2)}, u32[]{:S(2)}) collective-permute-start(f32[4,2,2,32,256]{4,3,2,1,0:T(8,128)S(1)} %get-tuple-element.119.refs_2_), channel_id=1, source_target_pairs={{0,4},{4,0},{8,12},{12,8},{16,20},{20,16},{24,28},{28,24},{1,5},{5... | collective-permute-start | bytes 1572872 | tf_op jit(solution)/shard_map/ppermute | solution.py:25
  29.5 12.7 %collective-permute-start.10 = (f32[4,2,2,32,256]{4,3,2,1,0:T(8,128)S(1)}, f32[4,2,2,32,256]{4,3,2,1,0:T(8,128)S(1)}, u32[]{:S(2)}, u32[]{:S(2)}) collective-permute-start(f32[4,2,2,32,256]{4,3,2,1,0:T(8,128)S(1)} %get-tuple-element.121.refs_4_), channel_id=1, source_target_pairs={{0,2},{1,3},{2,0},{3,1},{4,6},{5,7},{6,4},{7,5},{8,10},{9,11},{10,... | collective-permute-start | bytes 1572872 | tf_op jit(solution)/shard_map/ppermute | solution.py:25
  43.0 24.0 %collective-permute-start.13 = (f32[4,2,2,32,256]{4,3,2,1,0:T(8,128)S(1)}, f32[4,2,2,32,256]{4,3,2,1,0:T(8,128)S(1)}, u32[]{:S(2)}, u32[]{:S(2)}) collective-permute-start(f32[4,2,2,32,256]{4,3,2,1,0:T(8,128)S(1)} %get-tuple-element.131.refs_2_), channel_id=1, source_target_pairs={{0,2},{1,3},{2,0},{3,1},{4,6},{5,7},{6,4},{7,5},{8,10},{9,11},{10,... | collective-permute-start | bytes 1572872 | tf_op jit(solution)/shard_map/ppermute | solution.py:25
  43.4 23.7 %collective-permute-start.14 = (f32[4,2,2,32,256]{4,3,2,1,0:T(8,128)S(1)}, f32[4,2,2,32,256]{4,3,2,1,0:T(8,128)S(1)}, u32[]{:S(2)}, u32[]{:S(2)}) collective-permute-start(f32[4,2,2,32,256]{4,3,2,1,0:T(8,128)S(1)} %get-tuple-element.133.refs_4_), channel_id=1, source_target_pairs={{0,4},{4,0},{8,12},{12,8},{16,20},{20,16},{24,28},{28,24},{1,5},{5... | collective-permute-start | bytes 1572872 | tf_op jit(solution)/shard_map/ppermute | solution.py:25
  44.9 5.8 %collective-permute-start.3 = (f32[2,2,64,256]{3,2,1,0:T(8,128)S(1)}, f32[2,2,64,256]{3,2,1,0:T(8,128)S(1)}, u32[]{:S(2)}, u32[]{:S(2)}) collective-permute-start(f32[2,2,64,256]{3,2,1,0:T(8,128)S(1)} %get-tuple-element.208), channel_id=1, source_target_pairs={{0,8},{4,12},{8,0},{12,4},{16,24},{20,28},{24,16},{28,20},{1,9},{5... | collective-permute-start | bytes 786440 | tf_op jit(solution)/shard_map/ppermute | solution.py:25
  45.0 7.4 %collective-permute-start.5 = (f32[2,2,64,256]{3,2,1,0:T(8,128)S(1)}, f32[2,2,64,256]{3,2,1,0:T(8,128)S(1)}, u32[]{:S(2)}, u32[]{:S(2)}) collective-permute-start(f32[2,2,64,256]{3,2,1,0:T(8,128)S(1)} %get-tuple-element.209), channel_id=1, source_target_pairs={{0,24},{4,28},{8,16},{12,20},{16,8},{20,12},{24,0},{28,4},{1,25},{... | collective-permute-start | bytes 786440 | tf_op jit(solution)/shard_map/ppermute | solution.py:25
  45.1 20.8 %collective-permute-start.4 = (f32[2,2,64,256]{3,2,1,0:T(8,128)S(1)}, f32[2,2,64,256]{3,2,1,0:T(8,128)S(1)}, u32[]{:S(2)}, u32[]{:S(2)}) collective-permute-start(f32[2,2,64,256]{3,2,1,0:T(8,128)S(1)} %get-tuple-element.210), channel_id=1, source_target_pairs={{0,16},{4,20},{8,24},{12,28},{16,0},{20,4},{24,8},{28,12},{1,17},{... | collective-permute-start | bytes 786440 | tf_op jit(solution)/shard_map/ppermute | solution.py:25
  67.9 5.1 %collective-permute-start.15 = (f32[4,2,2,32,256]{4,3,2,1,0:T(8,128)S(1)}, f32[4,2,2,32,256]{4,3,2,1,0:T(8,128)S(1)}, u32[]{:S(2)}, u32[]{:S(2)}) collective-permute-start(f32[4,2,2,32,256]{4,3,2,1,0:T(8,128)S(1)} %get-tuple-element.137.refs_2_), channel_id=1, source_target_pairs={{0,1},{1,0},{2,3},{3,2},{4,5},{5,4},{6,7},{7,6},{8,9},{9,8},{10,11... | collective-permute-start | bytes 1572872 | tf_op jit(solution)/shard_map/ppermute | solution.py:25
  70.6 13.1 %collective-permute-start.11 = (f32[4,2,2,32,256]{4,3,2,1,0:T(8,128)S(1)}, f32[4,2,2,32,256]{4,3,2,1,0:T(8,128)S(1)}, u32[]{:S(2)}, u32[]{:S(2)}) collective-permute-start(f32[4,2,2,32,256]{4,3,2,1,0:T(8,128)S(1)} %get-tuple-element.145.refs_2_), channel_id=1, source_target_pairs={{0,4},{4,0},{8,12},{12,8},{16,20},{20,16},{24,28},{28,24},{1,5},{5... | collective-permute-start | bytes 1572872 | tf_op jit(solution)/shard_map/ppermute | solution.py:25
  71.8 12.8 %collective-permute-start.12 = (f32[4,2,2,32,256]{4,3,2,1,0:T(8,128)S(1)}, f32[4,2,2,32,256]{4,3,2,1,0:T(8,128)S(1)}, u32[]{:S(2)}, u32[]{:S(2)}) collective-permute-start(f32[4,2,2,32,256]{4,3,2,1,0:T(8,128)S(1)} %get-tuple-element.147.refs_4_), channel_id=1, source_target_pairs={{0,2},{1,3},{2,0},{3,1},{4,6},{5,7},{6,4},{7,5},{8,10},{9,11},{10,... | collective-permute-start | bytes 1572872 | tf_op jit(solution)/shard_map/ppermute | solution.py:25
  85.3 26.0 %collective-permute-start.19 = (f32[4,2,2,32,256]{4,3,2,1,0:T(8,128)S(1)}, f32[4,2,2,32,256]{4,3,2,1,0:T(8,128)S(1)}, u32[]{:S(2)}, u32[]{:S(2)}) collective-permute-start(f32[4,2,2,32,256]{4,3,2,1,0:T(8,128)S(1)} %get-tuple-element.157.refs_2_), channel_id=1, source_target_pairs={{0,2},{1,3},{2,0},{3,1},{4,6},{5,7},{6,4},{7,5},{8,10},{9,11},{10,... | collective-permute-start | bytes 1572872 | tf_op jit(solution)/shard_map/ppermute | solution.py:25
  86.6 24.7 %collective-permute-start.20 = (f32[4,2,2,32,256]{4,3,2,1,0:T(8,128)S(1)}, f32[4,2,2,32,256]{4,3,2,1,0:T(8,128)S(1)}, u32[]{:S(2)}, u32[]{:S(2)}) collective-permute-start(f32[4,2,2,32,256]{4,3,2,1,0:T(8,128)S(1)} %get-tuple-element.159.refs_4_), channel_id=1, source_target_pairs={{0,4},{4,0},{8,12},{12,8},{16,20},{20,16},{24,28},{28,24},{1,5},{5... | collective-permute-start | bytes 1572872 | tf_op jit(solution)/shard_map/ppermute | solution.py:25
  88.2 13.7 %collective-permute-start.2 = (f32[2,2,64,256]{3,2,1,0:T(8,128)S(1)}, f32[2,2,64,256]{3,2,1,0:T(8,128)S(1)}, u32[]{:S(2)}, u32[]{:S(2)}) collective-permute-start(f32[2,2,64,256]{3,2,1,0:T(8,128)S(1)} %get-tuple-element.203), channel_id=1, source_target_pairs={{0,24},{4,28},{8,16},{12,20},{16,8},{20,12},{24,0},{28,4},{1,25},{... | collective-permute-start | bytes 786440 | tf_op jit(solution)/shard_map/ppermute | solution.py:25
  89.7 20.4 %collective-permute-start.1 = (f32[2,2,64,256]{3,2,1,0:T(8,128)S(1)}, f32[2,2,64,256]{3,2,1,0:T(8,128)S(1)}, u32[]{:S(2)}, u32[]{:S(2)}) collective-permute-start(f32[2,2,64,256]{3,2,1,0:T(8,128)S(1)} %get-tuple-element.204), channel_id=1, source_target_pairs={{0,16},{4,20},{8,24},{12,28},{16,0},{20,4},{24,8},{28,12},{1,17},{... | collective-permute-start | bytes 786440 | tf_op jit(solution)/shard_map/ppermute | solution.py:25
  93.7 16.4 %collective-permute-start = (f32[2,2,64,256]{3,2,1,0:T(8,128)S(1)}, f32[2,2,64,256]{3,2,1,0:T(8,128)S(1)}, u32[]{:S(2)}, u32[]{:S(2)}) collective-permute-start(f32[2,2,64,256]{3,2,1,0:T(8,128)S(1)} %get-tuple-element.205), channel_id=1, source_target_pairs={{0,8},{4,12},{8,0},{12,4},{16,24},{20,28},{24,16},{28,20},{1,9},{5... | collective-permute-start | bytes 786440 | tf_op jit(solution)/shard_map/ppermute | solution.py:25
  112.1 6.6 %collective-permute-start.21 = (f32[4,2,2,32,256]{4,3,2,1,0:T(8,128)S(1)}, f32[4,2,2,32,256]{4,3,2,1,0:T(8,128)}, u32[]{:S(2)}, u32[]{:S(2)}) collective-permute-start(f32[4,2,2,32,256]{4,3,2,1,0:T(8,128)S(1)} %get-tuple-element.163.refs_2_), channel_id=1, source_target_pairs={{0,1},{1,0},{2,3},{3,2},{4,5},{5,4},{6,7},{7,6},{8,9},{9,8},{10,11... | collective-permute-start | bytes 1572872 | tf_op jit(solution)/shard_map/ppermute | solution.py:25
  115.2 13.1 %collective-permute-start.17 = (f32[4,2,2,32,256]{4,3,2,1,0:T(8,128)S(1)}, f32[4,2,2,32,256]{4,3,2,1,0:T(8,128)S(1)}, u32[]{:S(2)}, u32[]{:S(2)}) collective-permute-start(f32[4,2,2,32,256]{4,3,2,1,0:T(8,128)S(1)} %get-tuple-element.171.refs_2_), channel_id=1, source_target_pairs={{0,4},{4,0},{8,12},{12,8},{16,20},{20,16},{24,28},{28,24},{1,5},{5... | collective-permute-start | bytes 1572872 | tf_op jit(solution)/shard_map/ppermute | solution.py:25
  116.4 12.8 %collective-permute-start.18 = (f32[4,2,2,32,256]{4,3,2,1,0:T(8,128)S(1)}, f32[4,2,2,32,256]{4,3,2,1,0:T(8,128)S(1)}, u32[]{:S(2)}, u32[]{:S(2)}) collective-permute-start(f32[4,2,2,32,256]{4,3,2,1,0:T(8,128)S(1)} %get-tuple-element.173.refs_4_), channel_id=1, source_target_pairs={{0,2},{1,3},{2,0},{3,1},{4,6},{5,7},{6,4},{7,5},{8,10},{9,11},{10,... | collective-permute-start | bytes 1572872 | tf_op jit(solution)/shard_map/ppermute | solution.py:25
  116.7 22.6 %collective-permute-start.25 = (f32[2,2,64,256]{3,2,1,0:T(8,128)}, f32[2,2,64,256]{3,2,1,0:T(8,128)S(1)}, u32[]{:S(2)}, u32[]{:S(2)}) collective-permute-start(f32[2,2,64,256]{3,2,1,0:T(8,128)} %copy-done.2), channel_id=1, source_target_pairs={{0,8},{4,12},{8,0},{12,4},{16,24},{20,28},{24,16},{28,20},{1,9},{5... | collective-permute-start | bytes 786440 | tf_op jit(solution)/shard_map/ppermute | solution.py:25
  118.7 20.6 %collective-permute-start.26 = (f32[2,2,64,256]{3,2,1,0:T(8,128)}, f32[2,2,64,256]{3,2,1,0:T(8,128)S(1)}, u32[]{:S(2)}, u32[]{:S(2)}) collective-permute-start(f32[2,2,64,256]{3,2,1,0:T(8,128)} %copy-done.1), channel_id=1, source_target_pairs={{0,16},{4,20},{8,24},{12,28},{16,0},{20,4},{24,8},{28,12},{1,17},{... | collective-permute-start | bytes 786440 | tf_op jit(solution)/shard_map/ppermute | solution.py:25
  120.0 22.8 %collective-permute-start.27 = (f32[2,2,64,256]{3,2,1,0:T(8,128)}, f32[2,2,64,256]{3,2,1,0:T(8,128)S(1)}, u32[]{:S(2)}, u32[]{:S(2)}) collective-permute-start(f32[2,2,64,256]{3,2,1,0:T(8,128)} %copy-done), channel_id=1, source_target_pairs={{0,24},{4,28},{8,16},{12,20},{16,8},{20,12},{24,0},{28,4},{1,25},{... | collective-permute-start | bytes 786440 | tf_op jit(solution)/shard_map/ppermute | solution.py:25
  130.0 15.4 %collective-permute-start.23 = (f32[4,2,2,32,256]{4,3,2,1,0:T(8,128)S(1)}, f32[4,2,2,32,256]{4,3,2,1,0:T(8,128)S(1)}, u32[]{:S(2)}, u32[]{:S(2)}) collective-permute-start(f32[4,2,2,32,256]{4,3,2,1,0:T(8,128)S(1)} %get-tuple-element.181.refs_2_), channel_id=1, source_target_pairs={{0,2},{1,3},{2,0},{3,1},{4,6},{5,7},{6,4},{7,5},{8,10},{9,11},{10,... | collective-permute-start | bytes 1572872 | tf_op jit(solution)/shard_map/ppermute | solution.py:25
  130.3 15.1 %collective-permute-start.24 = (f32[4,2,2,32,256]{4,3,2,1,0:T(8,128)S(1)}, f32[4,2,2,32,256]{4,3,2,1,0:T(8,128)S(1)}, u32[]{:S(2)}, u32[]{:S(2)}) collective-permute-start(f32[4,2,2,32,256]{4,3,2,1,0:T(8,128)S(1)} %get-tuple-element.183.refs_4_), channel_id=1, source_target_pairs={{0,4},{4,0},{8,12},{12,8},{16,20},{20,16},{24,28},{28,24},{1,5},{5... | collective-permute-start | bytes 1572872 | tf_op jit(solution)/shard_map/ppermute | solution.py:25
  148.2 10.5 %collective-permute-start.33 = (f32[2,2,64,256]{3,2,1,0:T(8,128)S(1)}, f32[2,2,64,256]{3,2,1,0:T(8,128)S(1)}, u32[]{:S(2)}, u32[]{:S(2)}) collective-permute-start(f32[2,2,64,256]{3,2,1,0:T(8,128)S(1)} %get-tuple-element.168), channel_id=1, source_target_pairs={{0,8},{4,12},{8,0},{12,4},{16,24},{20,28},{24,16},{28,20},{1,9},{5... | collective-permute-start | bytes 786440 | tf_op jit(solution)/shard_map/ppermute | solution.py:25
  148.2 14.1 %collective-permute-start.34 = (f32[2,2,64,256]{3,2,1,0:T(8,128)S(1)}, f32[2,2,64,256]{3,2,1,0:T(8,128)S(1)}, u32[]{:S(2)}, u32[]{:S(2)}) collective-permute-start(f32[2,2,64,256]{3,2,1,0:T(8,128)S(1)} %get-tuple-element.169), channel_id=1, source_target_pairs={{0,16},{4,20},{8,24},{12,28},{16,0},{20,4},{24,8},{28,12},{1,17},{... | collective-permute-start | bytes 786440 | tf_op jit(solution)/shard_map/ppermute | solution.py:25
  150.6 22.9 %collective-permute-start.35 = (f32[2,2,64,256]{3,2,1,0:T(8,128)S(1)}, f32[2,2,64,256]{3,2,1,0:T(8,128)S(1)}, u32[]{:S(2)}, u32[]{:S(2)}) collective-permute-start(f32[2,2,64,256]{3,2,1,0:T(8,128)S(1)} %get-tuple-element.170), channel_id=1, source_target_pairs={{0,24},{4,28},{8,16},{12,20},{16,8},{20,12},{24,0},{28,4},{1,25},{... | collective-permute-start | bytes 786440 | tf_op jit(solution)/shard_map/ppermute | solution.py:25
  151.6 24.6 %collective-permute-start.31 = (f32[2,2,64,256]{3,2,1,0:T(8,128)S(1)}, f32[2,2,64,256]{3,2,1,0:T(8,128)S(1)}, u32[]{:S(2)}, u32[]{:S(2)}) collective-permute-start(f32[2,2,64,256]{3,2,1,0:T(8,128)S(1)} %get-tuple-element.193), channel_id=1, source_target_pairs={{0,8},{4,12},{8,0},{12,4},{16,24},{20,28},{24,16},{28,20},{1,9},{5... | collective-permute-start | bytes 786440 | tf_op jit(solution)/shard_map/ppermute | solution.py:25
  152.6 36.8 %collective-permute-start.32 = (f32[2,2,64,256]{3,2,1,0:T(8,128)S(1)}, f32[2,2,64,256]{3,2,1,0:T(8,128)S(1)}, u32[]{:S(2)}, u32[]{:S(2)}) collective-permute-start(f32[2,2,64,256]{3,2,1,0:T(8,128)S(1)} %get-tuple-element.194), channel_id=1, source_target_pairs={{0,16},{4,20},{8,24},{12,28},{16,0},{20,4},{24,8},{28,12},{1,17},{... | collective-permute-start | bytes 786440 | tf_op jit(solution)/shard_map/ppermute | solution.py:25
  158.7 37.3 %collective-permute-start.30 = (f32[2,2,64,256]{3,2,1,0:T(8,128)S(1)}, f32[2,2,64,256]{3,2,1,0:T(8,128)S(1)}, u32[]{:S(2)}, u32[]{:S(2)}) collective-permute-start(f32[2,2,64,256]{3,2,1,0:T(8,128)S(1)} %get-tuple-element.191), channel_id=1, source_target_pairs={{0,24},{4,28},{8,16},{12,20},{16,8},{20,12},{24,0},{28,4},{1,25},{... | collective-permute-start | bytes 786440 | tf_op jit(solution)/shard_map/ppermute | solution.py:25
  (7 other events, 129.6 us)
